TPU v7x, 128 devices: a whole 4x4x4 slice. The times are simulated.
128 devices in a mesh: frame: 8 (over y_lo, z), patch: 16 (over y_hi, x, core).
Axes of the slice: x: 4, y: 4 (y_hi: 2, y_lo: 2; y = y_hi * 2 + y_lo), z: 4, core: 2. Of those that a mesh axis runs over, the one named last changes fastest.
Arguments:
- query_rows: bfloat16 [32, 1024, 1408], P('frame', 'patch'), may hold values from -6 to 6, as said below
- key_rows: bfloat16 [32, 1024, 1408], P('frame', 'patch'), may hold values from -6 to 6, as said below
- value_rows: bfloat16 [32, 1024, 1408], P('frame', 'patch'), may hold values from -6 to 6
- grad_out: bfloat16 [32, 1024, 1408], P('frame', 'patch'), may hold values from -6 to 6
- out_weight: bfloat16 [1408, 1408], replicated, may hold values from -0.15625 to 0.15625
Outputs:
- grad_query: bfloat16 [32, 1024, 1408], P('frame', 'patch')
- grad_key: bfloat16 [32, 1024, 1408], P('frame', 'patch')
- grad_value: bfloat16 [32, 1024, 1408], P('frame', 'patch')
- grad_weight: float32 [1408, 1408], P(('frame', 'patch'))
Inputs may be any that keep to these rules, and one draw needn't show every extreme that they name: `query_rows`: entries of order one. `key_rows`: entries of order one.
All inputs are finite; a program needn't handle non-finite values.
Results may differ from a plain program's by a relative error of at most 0.017.
Values may be sent and summed in bfloat16 or wider, within the bound.
No kernel may reach another device: no remote copies, remote signals or barrier semaphores. Data moves between devices by JAX's collectives and lax.ppermute only.
A program may use at most 128 MiB of HBM per device.

v0:
```python
import jax
import jax.numpy as jnp
from jax import lax
from jax.sharding import PartitionSpec as P

HEAD_DIM = 88


def for_sending(array):

    def short(part):
        return part.astype(jnp.bfloat16) if part.dtype == jnp.float32 else part

    return jax.tree.map(short, array)


def split_up(array, dim, size):
    lengths = array.shape
    pieces = array.reshape(*lengths[:dim], size, lengths[dim] // size, *lengths[dim + 1 :])
    return jnp.moveaxis(pieces, dim, 0)


def sum_at_owner(array, axis, dim):
    pieces = split_up(array, dim, lax.axis_size(axis))
    arrived = lax.all_to_all(pieces, axis, split_axis=0, concat_axis=0, tiled=True)
    return arrived.astype(jnp.float32).sum(axis=0)


def frame_grads(pieces):
    query_part, key_part, value_part, upstream = pieces
    patches = query_part.shape[0]
    local_heads = query_part.shape[1] // HEAD_DIM
    softmax_scale = HEAD_DIM ** (-0.5)
    query_heads = query_part.reshape(patches, local_heads, HEAD_DIM)
    key_heads = key_part.reshape(patches, local_heads, HEAD_DIM)
    value_heads = value_part.reshape(patches, local_heads, HEAD_DIM)
    upstream_heads = upstream.reshape(patches, local_heads, HEAD_DIM)
    scores = (
        jnp.einsum("qhd,khd->hqk", query_heads, key_heads, preferred_element_type=jnp.float32)
        * softmax_scale
    )
    row_max = jnp.max(scores, axis=-1, keepdims=True)
    raised = jnp.exp(scores - row_max)
    weights = raised / jnp.sum(raised, axis=-1, keepdims=True)
    weights_low = weights.astype(jnp.bfloat16)
    attended = jnp.einsum(
        "hqk,khd->qhd", weights_low, value_heads, preferred_element_type=jnp.float32
    ).astype(jnp.bfloat16)
    grad_weights = jnp.einsum(
        "qhd,khd->hqk", upstream_heads, value_heads, preferred_element_type=jnp.float32
    )
    row_dot = jnp.sum(upstream_heads.astype(jnp.float32) * attended.astype(jnp.float32), axis=-1)
    grad_scores = (weights * (grad_weights - jnp.transpose(row_dot)[:, :, None])).astype(
        jnp.bfloat16
    )
    grad_query = (
        jnp.einsum("hqk,khd->qhd", grad_scores, key_heads, preferred_element_type=jnp.float32)
        * softmax_scale
    ).astype(jnp.bfloat16)
    grad_key = (
        jnp.einsum("hqk,qhd->khd", grad_scores, query_heads, preferred_element_type=jnp.float32)
        * softmax_scale
    ).astype(jnp.bfloat16)
    grad_value = jnp.einsum(
        "hqk,qhd->khd", weights_low, upstream_heads, preferred_element_type=jnp.float32
    ).astype(jnp.bfloat16)
    return (
        grad_query.reshape(patches, -1),
        grad_key.reshape(patches, -1),
        grad_value.reshape(patches, -1),
        attended.reshape(patches, -1),
    )


def head_results(pieces):
    results = lax.map(frame_grads, pieces)
    return jax.tree.map(
        lambda part, own: part.astype(own.dtype),
        lax.all_to_all(for_sending(results), "patch", split_axis=1, concat_axis=2, tiled=True),
        results,
    )


def shards(query_rows, key_rows, value_rows, grad_out, out_weight):
    frames_here, patches_here, features = grad_out.shape
    flat_grad = grad_out.reshape(frames_here * patches_here, features)
    grad_attn = jnp.dot(flat_grad, out_weight, preferred_element_type=jnp.float32).astype(
        jnp.bfloat16
    )
    grad_attn = grad_attn.reshape(frames_here, patches_here, features)
    grad_query, grad_key, grad_value, attended = head_results(
        (
            lax.all_to_all(query_rows, "patch", split_axis=2, concat_axis=1, tiled=True),
            lax.all_to_all(key_rows, "patch", split_axis=2, concat_axis=1, tiled=True),
            lax.all_to_all(value_rows, "patch", split_axis=2, concat_axis=1, tiled=True),
            lax.all_to_all(grad_attn, "patch", split_axis=2, concat_axis=1, tiled=True),
        )
    )
    flat_attn = attended.reshape(frames_here * patches_here, features)
    frame_rows = lax.psum_scatter(
        lax.dot_general(
            flat_grad, flat_attn, (((0,), (0,)), ((), ())), preferred_element_type=jnp.float32
        ).astype(jnp.bfloat16),
        "frame",
        scatter_dimension=0,
        tiled=True,
    )
    grad_weight = sum_at_owner(frame_rows, "patch", 0)
    return (grad_query, grad_key, grad_value, grad_weight)


def solution(mesh):
    placed = (
        P("frame", "patch", None),
        P("frame", "patch", None),
        P("frame", "patch", None),
        P("frame", "patch", None),
        P(),
    )
    return jax.shard_map(
        shards,
        mesh=mesh,
        in_specs=placed,
        out_specs=(
            P("frame", "patch", None),
            P("frame", "patch", None),
            P("frame", "patch", None),
            P(("frame", "patch"), None),
        ),
        check_vma=False,
    )
```

profile of v0, /device:TPU:1, one launch (start us, length us, event | category | flops | bytes accessed | tf_op | source)
XLA Modules:
  0.0 285.5 jit_solution(2404625837832974164)
XLA Ops:
  7.2 1.1 copy-done
  8.3 3.5 %convolution_convert_fusion.3 = bf16[256,1408]{1,0:T(8,128)(2,1)S(1)} fusion(bf16[256,1408]{1,0:T(8,128)(2,1)S(1)} %bitcast.148, bf16[1408,1408]{1,0:T(8,128)(2,1)} %param.11), kind=kOutput, calls=%fused_computation.47 | convolution fusion | flops 1015382016 | bytes 5406720 | tf_op jit(solution)/shard_map/dot_general | solution.py:87
  11.8 1.6 copy.48
  13.4 1.6 reshape.131
  15.0 8.4 %all-to-all-start.2 = ((bf16[16,2,11264]{2,1,0:T(2,128)(2,1)}), bf16[16,2,11264]{2,1,0:T(2,128)(2,1)S(1)}, u32[]{:S(2)}, u32[]{:S(2)}) async-start(bf16[16,2,11264]{2,1,0:T(2,128)(2,1)} %reshape.131), calls=%async_computation.2 | async-start | bytes 1441792 | tf_op jit(solution)/shard_map/all_to_all | solution.py:96
  23.5 2.8 copy.46
  26.3 1.6 reshape.129
  28.0 9.0 %all-to-all-done.2 = bf16[16,2,11264]{2,1,0:T(2,128)(2,1)S(1)} async-done(((bf16[16,2,11264]{2,1,0:T(2,128)(2,1)}), bf16[16,2,11264]{2,1,0:T(2,128)(2,1)S(1)}, u32[]{:S(2)}, u32[]{:S(2)}) %all-to-all-start.2) | async-done | bytes 720928 | tf_op jit(solution)/shard_map/all_to_all | solution.py:96
  36.9 5.1 %all-to-all-start.1 = ((bf16[16,2,11264]{2,1,0:T(2,128)(2,1)}), bf16[16,2,11264]{2,1,0:T(2,128)(2,1)}, u32[]{:S(2)}, u32[]{:S(2)}) async-start(bf16[16,2,11264]{2,1,0:T(2,128)(2,1)} %reshape.129), calls=%async_computation.1 | async-start | bytes 1441792 | tf_op jit(solution)/shard_map/all_to_all | solution.py:93
  42.0 2.8 copy.44
  44.9 1.6 reshape.127
  46.5 9.2 %all-to-all-done.1 = bf16[16,2,11264]{2,1,0:T(2,128)(2,1)} async-done(((bf16[16,2,11264]{2,1,0:T(2,128)(2,1)}), bf16[16,2,11264]{2,1,0:T(2,128)(2,1)}, u32[]{:S(2)}, u32[]{:S(2)}) %all-to-all-start.1) | async-done | bytes 720928 | tf_op jit(solution)/shard_map/all_to_all | solution.py:93
  55.7 5.0 %all-to-all-start = ((bf16[16,2,11264]{2,1,0:T(2,128)(2,1)}), bf16[16,2,11264]{2,1,0:T(2,128)(2,1)}, u32[]{:S(2)}, u32[]{:S(2)}) async-start(bf16[16,2,11264]{2,1,0:T(2,128)(2,1)} %reshape.127), calls=%async_computation | async-start | bytes 1441792 | tf_op jit(solution)/shard_map/all_to_all | solution.py:94
  60.8 2.8 copy.51
  63.6 1.6 reshape.133
  65.3 9.2 %all-to-all-done = bf16[16,2,11264]{2,1,0:T(2,128)(2,1)} async-done(((bf16[16,2,11264]{2,1,0:T(2,128)(2,1)}), bf16[16,2,11264]{2,1,0:T(2,128)(2,1)}, u32[]{:S(2)}, u32[]{:S(2)}) %all-to-all-start) | async-done | bytes 720928 | tf_op jit(solution)/shard_map/all_to_all | solution.py:94
  74.5 5.0 %all-to-all-start.3 = ((bf16[16,2,11264]{2,1,0:T(2,128)(2,1)}), bf16[16,2,11264]{2,1,0:T(2,128)(2,1)}, u32[]{:S(2)}, u32[]{:S(2)}) async-start(bf16[16,2,11264]{2,1,0:T(2,128)(2,1)} %reshape.133), calls=%async_computation.3 | async-start | bytes 1441792 | tf_op jit(solution)/shard_map/all_to_all | solution.py:95
  80.7 2.0 copy.69
  82.7 1.2 copy.53
  83.9 2.0 reshape.130
  85.9 2.0 copy.47
  88.0 2.9 %reshape.128 = bf16[1408,4,64]{2,1,0:T(4,128)(2,1)} reshape(bf16[16,2,11264]{2,1,0:T(2,128)(2,1)} %all-to-all-done) | data formatting | bytes 1441792
  90.9 2.7 copy.45
  93.7 2.9 %reshape.134 = bf16[1408,4,64]{2,1,0:T(4,128)(2,1)} reshape(bf16[16,2,11264]{2,1,0:T(2,128)(2,1)} %all-to-all-done.3) | data formatting | bytes 1441792
  96.5 3.4 %copy.52 = bf16[4,16,64,88]{3,2,1,0:T(8,128)(2,1)} copy(bf16[4,16,64,88]{2,0,3,1:T(4,128)(2,1)} %bitcast.156) | data formatting | bytes 1441792 | tf_op jit(solution)/shard_map/all_to_all | solution.py:95
  99.9 34.6 %while.16 = (s32[]{:T(128)}, bf16[4,1024,88]{1,2,0:T(8,128)(2,1)}, bf16[4,1024,88]{1,2,0:T(8,128)(2,1)}, bf16[4,1024,88]{1,2,0:T(8,128)(2,1)}, bf16[4,1024,88]{1...) while((s32[]{:T(128)}, bf16[4,1024,88]{1,2,0:T(8,128)(2,1)}, ...), condition=%wide.region_4.5_spmd, body=%wide.region_0.4_spmd.sunk | while | flops 1128117248 | bytes 33392780 | solution.py:76
  101.4 1.0 fusion.67
  103.1 1.7 fusion.70
  104.8 1.2 multiply_convert_fusion.2
  105.9 1.5 fusion.69
  107.4 1.2 fusion.68
  111.8 1.7 fusion.70
  113.4 1.2 multiply_convert_fusion.2
  114.6 1.5 fusion.69
  116.1 1.2 fusion.68
  120.4 1.7 fusion.70
  122.1 1.2 multiply_convert_fusion.2
  123.3 1.5 fusion.69
  124.7 1.2 fusion.68
  129.1 1.7 fusion.70
  130.7 1.2 multiply_convert_fusion.2
  131.9 1.5 fusion.69
  133.4 1.2 fusion.68
  134.6 1.6 copy.63
  136.2 23.7 %all_to_all.146 = bf16[4,1024,88]{2,0,1:T(4,128)(2,1)S(1)} all-to-all(bf16[4,1024,88]{2,0,1:T(4,128)(2,1)S(1)} %copy.63), channel_id=1, replica_groups=mesh['frame'=8,'patch'=16] {'patch'}, dimensions={1} | all-to-all | bytes 1441792 | tf_op jit(solution)/shard_map/all_to_all | solution.py:79
  160.7 1.4 reshape.122
  162.1 3.2 %fusion.38 = bf16[1408,1408]{0,1:T(8,128)(2,1)} fusion(bf16[256,1408]{1,0:T(8,128)(2,1)S(1)} %reshape.122, bf16[256,1408]{1,0:T(8,128)(2,1)S(1)} %bitcast.149), kind=kOutput, calls=%fused_computation.46 | convolution fusion | flops 1017004032 | bytes 5406720 | tf_op jit(solution)/shard_map/dot_general | solution.py:101
  165.3 6.3 %copy.70 = bf16[1408,1408]{1,0:T(8,128)(2,1)} copy(bf16[1408,1408]{0,1:T(8,128)(2,1)} %fusion.38) | data formatting | bytes 7929856
  171.7 1.4 copy.54
  173.1 4.9 %all-to-all-start.4 = ((bf16[4,1024,88]{2,0,1:T(4,128)(2,1)}), bf16[4,1024,88]{2,0,1:T(4,128)(2,1)S(1)}, u32[]{:S(2)}, u32[]{:S(2)}) async-start(bf16[4,1024,88]{2,0,1:T(4,128)(2,1)} %copy.54), calls=%async_computation.4 | async-start | bytes 2097152 | tf_op jit(solution)/shard_map/all_to_all | solution.py:79
  178.0 1.4 copy.57
  179.4 17.2 %all-to-all-done.4 = bf16[4,1024,88]{2,0,1:T(4,128)(2,1)S(1)} async-done(((bf16[4,1024,88]{2,0,1:T(4,128)(2,1)}), bf16[4,1024,88]{2,0,1:T(4,128)(2,1)S(1)}, u32[]{:S(2)}, u32[]{:S(2)}) %all-to-all-start.4) | async-done | bytes 720928 | tf_op jit(solution)/shard_map/all_to_all | solution.py:79
  196.6 4.4 %all-to-all-start.5 = ((bf16[4,1024,88]{2,0,1:T(4,128)(2,1)}), bf16[4,1024,88]{2,0,1:T(4,128)(2,1)S(1)}, u32[]{:S(2)}, u32[]{:S(2)}) async-start(bf16[4,1024,88]{2,0,1:T(4,128)(2,1)} %copy.57), calls=%async_computation.5 | async-start | bytes 2097152 | tf_op jit(solution)/shard_map/all_to_all | solution.py:79
  201.0 1.4 copy.60
  202.4 17.3 %all-to-all-done.5 = bf16[4,1024,88]{2,0,1:T(4,128)(2,1)S(1)} async-done(((bf16[4,1024,88]{2,0,1:T(4,128)(2,1)}), bf16[4,1024,88]{2,0,1:T(4,128)(2,1)S(1)}, u32[]{:S(2)}, u32[]{:S(2)}) %all-to-all-start.5) | async-done | bytes 720928 | tf_op jit(solution)/shard_map/all_to_all | solution.py:79
  219.8 4.3 %all-to-all-start.6 = ((bf16[4,1024,88]{2,0,1:T(4,128)(2,1)}), bf16[4,1024,88]{2,0,1:T(4,128)(2,1)}, u32[]{:S(2)}, u32[]{:S(2)}) async-start(bf16[4,1024,88]{2,0,1:T(4,128)(2,1)} %copy.60), calls=%async_computation.6 | async-start | bytes 2097152 | tf_op jit(solution)/shard_map/all_to_all | solution.py:79
  224.1 31.4 %reduce-scatter.4.cloned.1.call-done = bf16[176,1408]{1,0:T(8,128)(2,1)} async-done(((bf16[1408,1408]{1,0:T(8,128)(2,1)}), bf16[176,1408]{1,0:T(8,128)(2,1)}) %reduce-scatter.4.cloned.1.call-update) | async-done | bytes 495632 | tf_op jit(solution)/shard_map/reduce_scatter | solution.py:100
  255.5 2.1 reshape.123
  257.6 6.9 %all-to-all-start.8 = ((bf16[16,11,1408]{2,1,0:T(8,128)(2,1)}), bf16[16,11,1408]{2,1,0:T(8,128)(2,1)S(1)}, u32[]{:S(2)}, u32[]{:S(2)}) async-start(bf16[16,11,1408]{2,1,0:T(8,128)(2,1)} %reshape.123), calls=%async_computation.8 | async-start | bytes 1441792 | tf_op jit(solution)/shard_map/all_to_all | solution.py:25
  265.3 2.2 all_to_all.124
  268.4 2.2 all_to_all.128
  270.6 1.4 copy.61
  272.7 2.2 all_to_all.132
  274.9 3.1 %all-to-all-done.8 = bf16[16,11,1408]{2,1,0:T(8,128)(2,1)S(1)} async-done(((bf16[16,11,1408]{2,1,0:T(8,128)(2,1)}), bf16[16,11,1408]{2,1,0:T(8,128)(2,1)S(1)}, u32[]{:S(2)}, u32[]{:S(2)}) %all-to-all-start.8) | async-done | bytes 495648 | tf_op jit(solution)/shard_map/all_to_all | solution.py:25
  (49 shorter events, 16.6 us)
Async XLA Ops:
  7.2 1.1 copy-start
  15.0 21.9 %all-to-all-start.2 = ((bf16[16,2,11264]{2,1,0:T(2,128)(2,1)}), bf16[16,2,11264]{2,1,0:T(2,128)(2,1)S(1)}, u32[]{:S(2)}, u32[]{:S(2)}) async-start(bf16[16,2,11264]{2,1,0:T(2,128)(2,1)} %reshape.131), calls=%async_computation.2 | async-start | bytes 1441792 | tf_op jit(solution)/shard_map/all_to_all | solution.py:96
  36.9 18.8 %all-to-all-start.1 = ((bf16[16,2,11264]{2,1,0:T(2,128)(2,1)}), bf16[16,2,11264]{2,1,0:T(2,128)(2,1)}, u32[]{:S(2)}, u32[]{:S(2)}) async-start(bf16[16,2,11264]{2,1,0:T(2,128)(2,1)} %reshape.129), calls=%async_computation.1 | async-start | bytes 1441792 | tf_op jit(solution)/shard_map/all_to_all | solution.py:93
  55.7 18.7 %all-to-all-start = ((bf16[16,2,11264]{2,1,0:T(2,128)(2,1)}), bf16[16,2,11264]{2,1,0:T(2,128)(2,1)}, u32[]{:S(2)}, u32[]{:S(2)}) async-start(bf16[16,2,11264]{2,1,0:T(2,128)(2,1)} %reshape.127), calls=%async_computation | async-start | bytes 1441792 | tf_op jit(solution)/shard_map/all_to_all | solution.py:94
  74.5 19.2 %all-to-all-start.3 = ((bf16[16,2,11264]{2,1,0:T(2,128)(2,1)}), bf16[16,2,11264]{2,1,0:T(2,128)(2,1)}, u32[]{:S(2)}, u32[]{:S(2)}) async-start(bf16[16,2,11264]{2,1,0:T(2,128)(2,1)} %reshape.133), calls=%async_computation.3 | async-start | bytes 1441792 | tf_op jit(solution)/shard_map/all_to_all | solution.py:95
  79.5 176.0 %reduce-scatter.4.cloned.1.call-start = ((), (), s32[]{:S(2)}) async-start(), calls=%async_computation.10 | async-start | bytes 4460544 | tf_op jit(solution)/shard_map/reduce_scatter | solution.py:100
  88.0 12.0 %copy-start.2 = (bf16[4,1024,88]{1,2,0:T(8,128)(2,1)S(1)}, bf16[4,1024,88]{1,2,0:T(8,128)(2,1)}, u32[]{:S(2)}) copy-start(bf16[4,1024,88]{1,2,0:T(8,128)(2,1)} %copy.53) | copy-start | bytes 2162692
  99.9 1.5 copy-start.1
  108.6 1.5 copy-start.1
  117.3 1.5 copy-start.1
  125.9 1.5 copy-start.1
  165.3 6.4 %copy-start.5 = (bf16[4,1024,88]{1,2,0:T(8,128)(2,1)S(1)}, bf16[4,1024,88]{1,2,0:T(8,128)(2,1)}, u32[]{:S(2)}) copy-start(bf16[4,1024,88]{1,2,0:T(8,128)(2,1)} %get-tuple-element.54) | copy-start | bytes 2162692
  171.6 6.4 %copy-start.4 = (bf16[4,1024,88]{1,2,0:T(8,128)(2,1)S(1)}, bf16[4,1024,88]{1,2,0:T(8,128)(2,1)}, u32[]{:S(2)}) copy-start(bf16[4,1024,88]{1,2,0:T(8,128)(2,1)} %get-tuple-element.55) | copy-start | bytes 2162692
  171.6 29.4 %copy-start.3 = (bf16[4,1024,88]{1,2,0:T(8,128)(2,1)S(1)}, bf16[4,1024,88]{1,2,0:T(8,128)(2,1)}, u32[]{:S(2)}) copy-start(bf16[4,1024,88]{1,2,0:T(8,128)(2,1)} %get-tuple-element.56) | copy-start | bytes 2162692
  173.1 23.5 %all-to-all-start.4 = ((bf16[4,1024,88]{2,0,1:T(4,128)(2,1)}), bf16[4,1024,88]{2,0,1:T(4,128)(2,1)S(1)}, u32[]{:S(2)}, u32[]{:S(2)}) async-start(bf16[4,1024,88]{2,0,1:T(4,128)(2,1)} %copy.54), calls=%async_computation.4 | async-start | bytes 2097152 | tf_op jit(solution)/shard_map/all_to_all | solution.py:79
  196.6 23.1 %all-to-all-start.5 = ((bf16[4,1024,88]{2,0,1:T(4,128)(2,1)}), bf16[4,1024,88]{2,0,1:T(4,128)(2,1)S(1)}, u32[]{:S(2)}, u32[]{:S(2)}) async-start(bf16[4,1024,88]{2,0,1:T(4,128)(2,1)} %copy.57), calls=%async_computation.5 | async-start | bytes 2097152 | tf_op jit(solution)/shard_map/all_to_all | solution.py:79
  219.8 37.9 %all-to-all-start.6 = ((bf16[4,1024,88]{2,0,1:T(4,128)(2,1)}), bf16[4,1024,88]{2,0,1:T(4,128)(2,1)}, u32[]{:S(2)}, u32[]{:S(2)}) async-start(bf16[4,1024,88]{2,0,1:T(4,128)(2,1)} %copy.60), calls=%async_computation.6 | async-start | bytes 2097152 | tf_op jit(solution)/shard_map/all_to_all | solution.py:79
  257.6 20.3 %all-to-all-start.8 = ((bf16[16,11,1408]{2,1,0:T(8,128)(2,1)}), bf16[16,11,1408]{2,1,0:T(8,128)(2,1)S(1)}, u32[]{:S(2)}, u32[]{:S(2)}) async-start(bf16[16,11,1408]{2,1,0:T(8,128)(2,1)} %reshape.123), calls=%async_computation.8 | async-start | bytes 1441792 | tf_op jit(solution)/shard_map/all_to_all | solution.py:25
Sparse Core Ops, SparseCore 0:
  171.8 83.7 reduce-scatter.3
where the time goes:
time: 287 us; the launch traced here: 286 us
  waiting for transfers between devices  96.4 us (34%)
  local copies, waits for them, and re-layouts  67.6 us (24%)
  starting transfers between devices  44.3 us (15%)
  matrix products  35.5 us (12%)
  blocking collectives  23.7 us (8%)
  between operations  14.3 us (5%)
  other arithmetic  3.7 us (1%)
    all_to_all x3, waiting for transfers between devices, head_results(): lax.all_to_all(for_sending(results), 'patch', split_axis=1, concat_axis=2...  34.5 us
    reduce_scatter x1, waiting for transfers between devices, shards(): lax.psum_scatter(lax.dot_general(flat_grad, flat_attn, (((0,), (0,)), (()...  31.4 us
    unnamed x22, local copies, waits for them, and re-layouts  31.2 us
    all_to_all x1, blocking collectives, head_results(): lax.all_to_all(for_sending(results), 'patch', split_axis=1, concat_axis=2...  23.7 us
    all_to_all x3, starting transfers between devices, head_results(): lax.all_to_all(for_sending(results), 'patch', split_axis=1, concat_axis=2...  13.6 us
    all_to_all x11, local copies, waits for them, and re-layouts, head_results(): lax.all_to_all(for_sending(results), 'patch', split_axis=1, concat_axis=2...  11.2 us
    all_to_all x1, waiting for transfers between devices, shards(): lax.all_to_all(query_rows, 'patch', split_axis=2, concat_axis=1, tiled=True)  9.22 us
    all_to_all x1, waiting for transfers between devices, shards(): lax.all_to_all(key_rows, 'patch', split_axis=2, concat_axis=1, tiled=True)  9.2 us
  transfers between devices with their start and end apart: 9, of which 7 were waited for; matrix products, arithmetic and copies ran while one was open for 13% of the time, Pallas kernels for 0%

commit v1 on v0

v1 whole, which is shorter than its diff:
```python
import functools

import jax
import jax.numpy as jnp
from jax import lax
from jax.experimental import pallas as pl
from jax.experimental.pallas import tpu as pltpu
from jax.sharding import Mesh, PartitionSpec as P

HEAD_DIM = 88
HEADS = 16
HALF = 64
BLOCK = 256
SOFTMAX_SCALE = HEAD_DIM ** (-0.5)
EXP2_SCALE = SOFTMAX_SCALE * 1.4426950408889634
F32, BF16 = jnp.float32, jnp.bfloat16


def head_of(slot):
    return 8 * (slot % 2) + slot // 2


def low_lanes(shape):
    return lax.broadcasted_iota(jnp.int32, shape, 1) < HALF


def turned(tile):
    return pltpu.roll(tile, HALF, 1)


def frame_pair(ref, n):
    first, second = [], []
    for s in range(8):
        a, b = ref[s, n].astype(F32), ref[s + 8, n].astype(F32)
        low = low_lanes(a.shape)
        first.append(jnp.where(low, a, turned(b)).astype(BF16))
        second.append(jnp.where(low, turned(a), b).astype(BF16))
    return jnp.concatenate(first, 1), jnp.concatenate(second, 1)


def put_back(ref, n, first, second):
    for s in range(8):
        a, b = first[:, 128 * s : 128 * (s + 1)], second[:, 128 * s : 128 * (s + 1)]
        low = low_lanes(a.shape)
        ref[s, n] = jnp.where(low, a, turned(b)).astype(BF16)
        ref[s + 8, n] = jnp.where(low, turned(a), b).astype(BF16)


def pack_kernel(q_ref, k_ref, v_ref, g_ref, w_hbm, out_ref, w_ref, sem):
    fetch = pltpu.make_async_copy(w_hbm, w_ref, sem)
    fetch.start()

    def place(n, rows):
        turned_rows = rows.T
        for slot in range(HEADS):
            at = HEAD_DIM * head_of(slot)
            out_ref[slot, n] = turned_rows[at : at + HEAD_DIM].astype(BF16)

    features = q_ref.shape[-1]
    for n, ref in enumerate((q_ref, k_ref, v_ref)):
        place(n, ref[...].reshape(-1, features))
    fetch.wait()
    place(
        3,
        jnp.dot(g_ref[...].reshape(-1, features), w_ref[...], preferred_element_type=F32).astype(BF16),
    )


def pack(query, key, value, upstream, weight):
    tokens = query.shape[0] * query.shape[1]
    return pl.pallas_call(
        pack_kernel,
        in_specs=[pl.BlockSpec(memory_space=pltpu.VMEM)] * 4 + [pl.BlockSpec(memory_space=pl.ANY)],
        out_specs=pl.BlockSpec(memory_space=pltpu.VMEM),
        out_shape=jax.ShapeDtypeStruct((HEADS, 4, HEAD_DIM, tokens), BF16),
        scratch_shapes=[pltpu.VMEM(weight.shape, BF16), pltpu.SemaphoreType.DMA],
        cost_estimate=pl.CostEstimate(flops=2 * tokens * weight.size, bytes_accessed=10_000_000, transcendentals=0),
        name="pack_by_head",
    )(query, key, value, upstream, weight)


def forward_kernel(x_ref, att_ref, e_ref, inv_ref, o_ref):
    qs, ks, vs = (frame_pair(x_ref, n) for n in range(3))
    for f in range(2):
        q_t, k, v_t = qs[f], ks[f].T, vs[f]
        for b in range(1024 // BLOCK):
            cols = slice(b * BLOCK, (b + 1) * BLOCK)
            scores = jnp.dot(k, q_t[:, cols], preferred_element_type=F32)
            row_max = jnp.max(scores, axis=0, keepdims=True)
            raised = jnp.exp2(scores * EXP2_SCALE - row_max * EXP2_SCALE)
            inverse = 1.0 / jnp.sum(raised, axis=0, keepdims=True)
            raised = raised.astype(BF16)
            e_ref[f, :, cols] = raised
            o_ref[f, :, cols] = jnp.dot(v_t, raised, preferred_element_type=F32) * inverse
            inv_ref[f, :, cols] = jnp.broadcast_to(inverse, (8, BLOCK))
    put_back(att_ref, 0, o_ref[0], o_ref[1])


PAIR = pl.BlockSpec((HEADS, 4, HEAD_DIM, 128), lambda i: (0, 0, 0, i))
ONE = pl.BlockSpec((HEADS, 1, HEAD_DIM, 128), lambda i: (0, 0, 0, i))
RAISED = pl.BlockSpec((2, 1024, 1024), lambda i: (i, 0, 0))
INVERSE = pl.BlockSpec((2, 8, 1024), lambda i: (i, 0, 0))


def forward(x):
    return pl.pallas_call(
        forward_kernel,
        grid=(2,),
        in_specs=[PAIR],
        out_specs=[ONE, RAISED, INVERSE],
        out_shape=[
            jax.ShapeDtypeStruct((HEADS, 1, HEAD_DIM, 256), BF16),
            jax.ShapeDtypeStruct((4, 1024, 1024), BF16),
            jax.ShapeDtypeStruct((4, 8, 1024), F32),
        ],
        scratch_shapes=[pltpu.VMEM((2, HEAD_DIM, 1024), F32)],
        cost_estimate=pl.CostEstimate(flops=4 * 4 * 1024 * 1024 * 256, bytes_accessed=12_000_000, transcendentals=1 << 22),
        name="spatial_forward",
    )(x)


def backward_kernel(x_ref, att_ref, e_ref, inv_ref, out_ref, dq_ref, dk_ref, dv_ref):
    qs, ks, vs, gs = (frame_pair(x_ref, n) for n in range(4))
    os = frame_pair(att_ref, 0)
    for f in range(2):
        q_t, k_t, v = qs[f], ks[f], vs[f].T
        scaled = gs[f].astype(F32) * inv_ref[f, 0:1, :]
        row_dot = jnp.sum(scaled * os[f].astype(F32), axis=0, keepdims=True)
        g_t = scaled.astype(BF16)
        for b in range(1024 // BLOCK):
            cols = slice(b * BLOCK, (b + 1) * BLOCK)
            raised = e_ref[f, :, cols]
            grad_probs = jnp.dot(v, g_t[:, cols], preferred_element_type=F32)
            grad_scores = (raised.astype(F32) * (grad_probs - row_dot[:, cols])).astype(BF16)
            dq_ref[f, :, cols] = jnp.dot(k_t, grad_scores, preferred_element_type=F32) * SOFTMAX_SCALE
            dk = lax.dot_general(q_t[:, cols], grad_scores, (((1,), (1,)), ((), ())), preferred_element_type=F32)
            dv = lax.dot_general(g_t[:, cols], raised, (((1,), (1,)), ((), ())), preferred_element_type=F32)
            if b == 0:
                dk_ref[f], dv_ref[f] = dk, dv
            else:
                dk_ref[f] += dk
                dv_ref[f] += dv
    put_back(out_ref, 0, dq_ref[0], dq_ref[1])
    put_back(out_ref, 1, dk_ref[0] * SOFTMAX_SCALE, dk_ref[1] * SOFTMAX_SCALE)
    put_back(out_ref, 2, dv_ref[0], dv_ref[1])


def backward(x, attended, raised, inverse):
    return pl.pallas_call(
        backward_kernel,
        grid=(2,),
        in_specs=[PAIR, ONE, RAISED, INVERSE],
        out_specs=pl.BlockSpec((HEADS, 3, HEAD_DIM, 128), lambda i: (0, 0, 0, i)),
        out_shape=jax.ShapeDtypeStruct((HEADS, 3, HEAD_DIM, 256), BF16),
        scratch_shapes=[pltpu.VMEM((2, HEAD_DIM, 1024), F32)] * 3,
        cost_estimate=pl.CostEstimate(flops=8 * 4 * 1024 * 1024 * 256, bytes_accessed=14_000_000, transcendentals=0),
        name="spatial_backward",
    )(x, attended, raised, inverse)


def weight_kernel(place_ref, mine_ref, other_ref, att_ref, o0, o1, o2, o3, g_ref, a_ref):
    core, z = place_ref[0], place_ref[1]
    features = mine_ref.shape[-1]
    g_ref[:, :256] = mine_ref[...].reshape(-1, features).T
    g_ref[:, 256:] = other_ref[...].reshape(-1, features).T
    for i in range(8):
        rows = slice(HEAD_DIM * i, HEAD_DIM * (i + 1))
        a_ref[rows, :256] = att_ref[i, core]
        a_ref[rows, 256:] = att_ref[i, 1 - core]
    att = a_ref[...]
    for r, out in enumerate((o0, o1, o2, o3)):
        for half in range(2):
            block = half * 4 + lax.rem(z + r, 4)
            rows = pl.ds(pl.multiple_of(block * 176, 16), 176)
            out[half] = lax.dot_general(
                g_ref[rows, :], att, (((1,), (1,)), ((), ())), preferred_element_type=F32
            ).astype(out.dtype)


def weight_terms(place, mine, other, att):
    features = mine.shape[-1]
    return pl.pallas_call(
        weight_kernel,
        in_specs=[pl.BlockSpec(memory_space=pltpu.SMEM)] + [pl.BlockSpec(memory_space=pltpu.VMEM)] * 3,
        out_specs=[pl.BlockSpec(memory_space=pltpu.VMEM)] * 4,
        out_shape=[jax.ShapeDtypeStruct((2, 176, 704), BF16)] * 4,
        scratch_shapes=[pltpu.VMEM((features, 512), BF16), pltpu.VMEM((704, 512), BF16)],
        cost_estimate=pl.CostEstimate(flops=2 * 512 * 1408 * 704, bytes_accessed=5_000_000, transcendentals=0),
        name="weight_terms",
    )(place, mine, other, att)


def rows_kernel(a, b, c, d, out):
    total = a[...].astype(F32) + b[...].astype(F32) + c[...].astype(F32) + d[...].astype(F32)
    total = total.reshape(352, 704)
    for p in range(32):
        out[p] = total[11 * p : 11 * (p + 1)].astype(BF16)


def row_sums(parts):
    return pl.pallas_call(
        rows_kernel,
        in_specs=[pl.BlockSpec(memory_space=pltpu.VMEM)] * 4,
        out_specs=pl.BlockSpec(memory_space=pltpu.VMEM),
        out_shape=jax.ShapeDtypeStruct((32, 11, 704), BF16),
        cost_estimate=pl.CostEstimate(flops=1_000_000, bytes_accessed=3_000_000, transcendentals=0),
        name="row_sums",
    )(*parts)


def unpack_kernel(x_ref, q_ref, k_ref, v_ref, t_ref):
    for n, ref in enumerate((q_ref, k_ref, v_ref)):
        for slot in range(HEADS):
            at = HEAD_DIM * head_of(slot)
            t_ref[at : at + HEAD_DIM] = x_ref[slot, n]
        ref[...] = t_ref[...].T.reshape(ref.shape)


def unpack(x, shape):
    return pl.pallas_call(
        unpack_kernel,
        in_specs=[pl.BlockSpec(memory_space=pltpu.VMEM)],
        out_specs=[pl.BlockSpec(memory_space=pltpu.VMEM)] * 3,
        out_shape=[jax.ShapeDtypeStruct(shape, BF16)] * 3,
        scratch_shapes=[pltpu.VMEM((shape[-1], shape[0] * shape[1]), BF16)],
        cost_estimate=pl.CostEstimate(flops=0, bytes_accessed=5_000_000, transcendentals=0),
        name="unpack_by_token",
    )(x)


FRAME, PATCH = ("y_lo", "z"), ("y_hi", "x", "core")
PLANE = ("y_lo", "y_hi", "x", "core")


def exchange(array, axes):
    return lax.all_to_all(array, axes, split_axis=0, concat_axis=0, tiled=True)


def along_z(array, step):
    return lax.ppermute(array, "z", [(i, (i + step) % 4) for i in range(4)])


def shards(query_rows, key_rows, value_rows, grad_out, out_weight):
    place = jnp.stack([lax.axis_index("core"), lax.axis_index("z")]).astype(jnp.int32)
    other_grad = lax.ppermute(grad_out, "core", [(0, 1), (1, 0)])
    x = exchange(pack(query_rows, key_rows, value_rows, grad_out, out_weight), PATCH)
    attended, raised, inverse = forward(x)
    att = exchange(attended.reshape(8, 2, HEAD_DIM, 256), ("y_hi", "x"))
    grads = backward(x, attended, raised, inverse)
    own, *sent = weight_terms(place, grad_out, other_grad, att)
    parts = [own] + [along_z(part, step + 1) for step, part in enumerate(sent)]
    outs = unpack(exchange(grads, PATCH), query_rows.shape)
    rows = exchange(row_sums(parts), PLANE)
    total = rows.reshape(16, 2, 11, 704).astype(F32).sum(0)
    grad_weight = jnp.concatenate([total[0], total[1]], axis=1)
    return (*outs, grad_weight)


def solution(mesh):
    chips = Mesh(mesh.devices.reshape(2, 4, 2, 4, 2), FRAME + PATCH)
    rows = P(FRAME, PATCH, None)
    return jax.shard_map(
        shards,
        mesh=chips,
        in_specs=(rows, rows, rows, rows, P()),
        out_specs=(rows, rows, rows, P(FRAME + PATCH, None)),
        check_vma=False,
    )
```

time: 287 us -> 189 us (0.66)
  local copies, waits for them, and re-layouts: 67.6 us -> 4.86 us
  Pallas kernels: 0 us -> 47.1 us
  matrix products: 35.5 us -> 0 us
  blocking collectives: 23.7 us -> 0 us
  between operations: 14.3 us -> 0.68 us
  starting transfers between devices: 44.3 us -> 31.5 us
  waiting for transfers between devices: 96.4 us -> 103 us
    pallas_call x0 -> x6, Pallas kernels: none -> 47.1 us  [the longest x1 15.5 us: forward(): pl.pallas_call(forward_kernel, grid=(2,), in_specs=[PAIR], out_specs=[ONE...]
    dot_general x26 -> x0, matrix products: 35.5 us -> none  [the longest x4 6.64 us: frame_grads(): jnp.einsum('hqk,qhd->khd', weights_low, upstream_heads, preferred_element...]
    reduce_scatter x1 -> x0, waiting for transfers between devices: 31.4 us -> none  [shards(): lax.psum_scatter(lax.dot_general(flat_grad, flat_attn, (((0,), (0,)), (()...]
    unnamed x22 -> x12, local copies, waits for them, and re-layouts: 31.2 us -> 4.85 us
    all_to_all x1 -> x0, blocking collectives: 23.7 us -> none  [head_results(): lax.all_to_all(for_sending(results), 'patch', split_axis=1, concat_axis=2...]
    ppermute x0 -> x4, waiting for transfers between devices: none -> 22.6 us  [the longest x3 22.6 us: along_z(): return lax.ppermute(array, 'z', [(i, (i + step) % 4) for i in range(4)])]
    all_to_all x15 -> x0, local copies, waits for them, and re-layouts: 21.4 us -> none  [the longest x11 11.2 us: head_results(): lax.all_to_all(for_sending(results), 'patch', split_axis=1, concat_axis=2...]
    all_to_all x8 -> x4, starting transfers between devices: 44.1 us -> 25.7 us  [exchange(): return lax.all_to_all(array, axes, split_axis=0, concat_axis=0, tiled=True)]
  transfers between devices with their start and end apart: 9 -> 8, of which waited for: 7 -> 6; matrix products, arithmetic and copies ran while one was open for 13% -> 1% of each run, Pallas kernels for 0% -> 16%
where the time goes in v1:
time: 189 us; the launch traced here: 188 us
  waiting for transfers between devices  103 us (54%)
  Pallas kernels  47.1 us (25%)
  starting transfers between devices  31.5 us (17%)
  local copies, waits for them, and re-layouts  4.86 us (3%)
    all_to_all x4, waiting for transfers between devices, exchange(): return lax.all_to_all(array, axes, split_axis=0, concat_axis=0, tiled=True)  80 us
    all_to_all x4, starting transfers between devices, exchange(): return lax.all_to_all(array, axes, split_axis=0, concat_axis=0, tiled=True)  25.7 us
    ppermute x3, waiting for transfers between devices, along_z(): return lax.ppermute(array, 'z', [(i, (i + step) % 4) for i in range(4)])  22.6 us
    pallas_call x1, Pallas kernels, forward(): pl.pallas_call(forward_kernel, grid=(2,), in_specs=[PAIR], out_specs=[ONE...  15.5 us
    pallas_call x1, Pallas kernels, backward(): pl.pallas_call(backward_kernel, grid=(2,), in_specs=[PAIR, ONE, RAISED, I...  14 us
    pallas_call x1, Pallas kernels, pack(): pl.pallas_call(pack_kernel, in_specs=[pl.BlockSpec(memory_space=pltpu.VME...  6.92 us
    ppermute x3, starting transfers between devices, along_z(): return lax.ppermute(array, 'z', [(i, (i + step) % 4) for i in range(4)])  5.67 us
    unnamed x12, local copies, waits for them, and re-layouts  4.85 us
  transfers between devices with their start and end apart: 8, of which 6 were waited for; matrix products, arithmetic and copies ran while one was open for 1% of the time, Pallas kernels for 16%

profile of v1, /device:TPU:1, one launch (start us, length us, event | category | flops | bytes accessed | tf_op | source)
XLA Modules:
  0.0 188.4 jit_solution(5850906009830434757)
XLA Ops:
  0.6 6.9 %pack_by_head.1 = bf16[16,4,88,256]{3,2,1,0:T(8,128)(2,1)} custom-call(bf16[4,64,1408]{2,1,0:T(8,128)(2,1)} %q_ref.1, bf16[4,64,1408]{2,1,0:T(8,128)(2,1)} %k_ref.1, bf16[4,64,1408]{2,1,0:T(8,128)(2,1)} %v_ref.1, bf16[4,64,1408]{2,1,0:T(8,128)(2,1)} %mine_ref.1, bf16[1408,1408]{1,0:T(8,128)(2,1)} %w_hbm.1), custom_call_target="tpu_custom_call" | custom-call | flops 1015021568 | bytes 10000000 | tf_op jit(solution)/shard_map/pack_by_head/pallas_call | solution.py:71
  7.6 8.4 %all-to-all-start = ((bf16[16,4,88,256]{3,2,1,0:T(8,128)(2,1)}), bf16[16,4,88,256]{3,2,1,0:T(8,128)(2,1)S(1)}, u32[]{:S(2)}, u32[]{:S(2)}) async-start(bf16[16,4,88,256]{3,2,1,0:T(8,128)(2,1)} %pack_by_head.1), calls=%async_computation | async-start | bytes 5767168 | tf_op jit(solution)/shard_map/all_to_all | solution.py:236
  16.0 0.2 collective-permute-start
  16.2 38.0 %all-to-all-done.x_ref = bf16[16,4,88,256]{3,2,1,0:T(8,128)(2,1)S(1)} async-done(((bf16[16,4,88,256]{3,2,1,0:T(8,128)(2,1)}), bf16[16,4,88,256]{3,2,1,0:T(8,128)(2,1)S(1)}, u32[]{:S(2)}, u32[]{:S(2)}) %all-to-all-start) | async-done | bytes 2883616 | tf_op jit(solution)/shard_map/all_to_all | solution.py:236
  54.2 0.0 copy-start.1
  54.2 1.7 copy-done.1
  55.8 15.5 %spatial_forward.1 = (bf16[16,1,88,256]{3,2,1,0:T(8,128)(2,1)}, bf16[4,1024,1024]{2,1,0:T(8,128)(2,1)}, f32[4,8,1024]{2,1,0:T(8,128)}) custom-call(bf16[16,4,88,256]{3,2,1,0:T(8,128)(2,1)} %copy-done.1), custom_call_target="tpu_custom_call" | custom-call | flops 4294967296 | bytes 12000000 | tf_op jit(solution)/shard_map/spatial_forward/pallas_call | solution.py:106
  71.3 5.2 %all-to-all-start.2 = ((bf16[8,2,88,256]{3,2,1,0:T(8,128)(2,1)}), bf16[8,2,88,256]{3,2,1,0:T(8,128)(2,1)S(1)}, u32[]{:S(2)}, u32[]{:S(2)}) async-start(bf16[8,2,88,256]{3,2,1,0:T(8,128)(2,1)} %bitcast.10), calls=%async_computation.2 | async-start | bytes 1441792 | tf_op jit(solution)/shard_map/all_to_all | solution.py:236
  76.6 0.7 pad_add_fusion.place_ref
  77.3 0.0 collective-permute-done.other_ref
  77.3 13.2 %all-to-all-done.2.att_ref = bf16[8,2,88,256]{3,2,1,0:T(8,128)(2,1)S(1)} async-done(((bf16[8,2,88,256]{3,2,1,0:T(8,128)(2,1)}), bf16[8,2,88,256]{3,2,1,0:T(8,128)(2,1)S(1)}, u32[]{:S(2)}, u32[]{:S(2)}) %all-to-all-start.2) | async-done | bytes 720928 | tf_op jit(solution)/shard_map/all_to_all | solution.py:236
  90.5 0.0 copy-start.2
  90.5 0.9 copy-done.2
  91.3 4.6 %weight_terms.1 = (bf16[2,176,704]{2,1,0:T(8,128)(2,1)}, bf16[2,176,704]{2,1,0:T(8,128)(2,1)}, bf16[2,176,704]{2,1,0:T(8,128)(2,1)}, bf16[2,176,704]{2,1,0:T(8,128)(2,1)}) custom-call(s32[2]{0:T(128)} %pad_add_fusion.place_ref, bf16[4,64,1408]{2,1,0:T(8,128)(2,1)} %mine_ref.1, bf16[4,64,1408]{2,1,0:T(8,128)(2,1)} %collective-permute-done.other_ref, ...), custom_call_target="tpu_custom_call" | custom-call | flops 1015021568 | bytes 5000000 | tf_op jit(solution)/shard_map/weight_terms/pallas_call | solution.py:182
  95.9 1.6 collective-permute-start.1
  97.6 3.3 %collective-permute-start.2 = (bf16[2,176,704]{2,1,0:T(8,128)(2,1)}, bf16[2,176,704]{2,1,0:T(8,128)(2,1)S(1)}, u32[]{:S(2)}, u32[]{:S(2)}) collective-permute-start(bf16[2,176,704]{2,1,0:T(8,128)(2,1)} %get-tuple-element.22), channel_id=1, source_target_pairs={{0,32},{16,48},{32,0},{48,16},{1,33},{17,49},{33,1},{49,17},{2,34}... | collective-permute-start | bytes 1486856 | tf_op jit(solution)/shard_map/ppermute | solution.py:240
  100.9 0.7 collective-permute-start.3
  101.6 10.2 %collective-permute-done.1.b = bf16[2,176,704]{2,1,0:T(8,128)(2,1)S(1)} collective-permute-done((bf16[2,176,704]{2,1,0:T(8,128)(2,1)}, bf16[2,176,704]{2,1,0:T(8,128)(2,1)S(1)}, u32[]{:S(2)}, u32[]{:S(2)}) %collective-permute-start.1) | collective-permute-done | bytes 495648 | tf_op jit(solution)/shard_map/ppermute | solution.py:240
  111.7 0.0 copy-start.3
  111.8 12.5 %collective-permute-done.2.c = bf16[2,176,704]{2,1,0:T(8,128)(2,1)S(1)} collective-permute-done((bf16[2,176,704]{2,1,0:T(8,128)(2,1)}, bf16[2,176,704]{2,1,0:T(8,128)(2,1)S(1)}, u32[]{:S(2)}, u32[]{:S(2)}) %collective-permute-start.2) | collective-permute-done | bytes 495648 | tf_op jit(solution)/shard_map/ppermute | solution.py:240
  124.2 0.0 copy-start.4
  124.2 0.0 collective-permute-done.3.d
  124.2 0.0 copy-start.5
  124.2 0.0 copy-done.3
  124.2 0.8 copy-done.4
  125.0 0.2 copy-done.5
  125.2 2.8 %row_sums.1 = bf16[32,11,704]{2,1,0:T(8,128)(2,1)} custom-call(bf16[2,176,704]{2,1,0:T(8,128)(2,1)} %get-tuple-element.20.a, bf16[2,176,704]{2,1,0:T(8,128)(2,1)} %copy-done.3, bf16[2,176,704]{2,1,0:T(8,128)(2,1)} %copy-done.4, bf16[2,176,704]{2,1,0:T(8,128)(2,1)} %copy-done.5), custom_call_target="tpu_custom_call" | custom-call | flops 1000000 | bytes 3000000 | tf_op jit(solution)/shard_map/row_sums/pallas_call | solution.py:201
  128.1 5.2 %all-to-all-start.3 = ((bf16[32,11,704]{2,1,0:T(8,128)(2,1)}), bf16[32,11,704]{2,1,0:T(8,128)(2,1)S(1)}, u32[]{:S(2)}, u32[]{:S(2)}) async-start(bf16[32,11,704]{2,1,0:T(8,128)(2,1)} %row_sums.1), calls=%async_computation.3 | async-start | bytes 1572864 | tf_op jit(solution)/shard_map/all_to_all | solution.py:236
  133.3 14.0 %spatial_backward.1 = bf16[16,3,88,256]{3,2,1,0:T(8,128)(2,1)} custom-call(bf16[16,4,88,256]{3,2,1,0:T(8,128)(2,1)} %copy-done.1, bf16[16,1,88,256]{3,2,1,0:T(8,128)(2,1)} %get-tuple-element.14.att_ref, bf16[4,1024,1024]{2,1,0:T(8,128)(2,1)} %get-tuple-element.15.e_ref, f32[4,8,1024]{2,1,0:T(8,128)} %get-tuple-element.16.inv_ref), custom_call_target="tpu_custom_call" | custom-call | flops 8589934592 | bytes 14000000 | tf_op jit(solution)/shard_map/spatial_backward/pallas_call | solution.py:149
  147.3 0.5 all-to-all-done.3
  147.8 6.8 %all-to-all-start.1 = ((bf16[16,3,88,256]{3,2,1,0:T(8,128)(2,1)}), bf16[16,3,88,256]{3,2,1,0:T(8,128)(2,1)S(1)}, u32[]{:S(2)}, u32[]{:S(2)}) async-start(bf16[16,3,88,256]{3,2,1,0:T(8,128)(2,1)} %spatial_backward.1), calls=%async_computation.1 | async-start | bytes 4325376 | tf_op jit(solution)/shard_map/all_to_all | solution.py:236
  154.6 0.1 convert_reduce_fusion
  154.8 0.7 pad_maximum_fusion
  155.5 28.3 %all-to-all-done.1.x_ref = bf16[16,3,88,256]{3,2,1,0:T(8,128)(2,1)S(1)} async-done(((bf16[16,3,88,256]{3,2,1,0:T(8,128)(2,1)}), bf16[16,3,88,256]{3,2,1,0:T(8,128)(2,1)S(1)}, u32[]{:S(2)}, u32[]{:S(2)}) %all-to-all-start.1) | async-done | bytes 2162720 | tf_op jit(solution)/shard_map/all_to_all | solution.py:236
  183.8 0.0 copy-start
  183.8 1.3 copy-done
  185.2 3.2 %unpack_by_token.1 = (bf16[4,64,1408]{2,1,0:T(8,128)(2,1)}, bf16[4,64,1408]{2,1,0:T(8,128)(2,1)}, bf16[4,64,1408]{2,1,0:T(8,128)(2,1)}) custom-call(bf16[16,3,88,256]{3,2,1,0:T(8,128)(2,1)} %copy-done), custom_call_target="tpu_custom_call" | custom-call | bytes 5000000 | tf_op jit(solution)/shard_map/unpack_by_token/pallas_call | solution.py:220
  (1 shorter events, 0.0 us)
Async XLA Ops:
  7.6 46.6 %all-to-all-start = ((bf16[16,4,88,256]{3,2,1,0:T(8,128)(2,1)}), bf16[16,4,88,256]{3,2,1,0:T(8,128)(2,1)S(1)}, u32[]{:S(2)}, u32[]{:S(2)}) async-start(bf16[16,4,88,256]{3,2,1,0:T(8,128)(2,1)} %pack_by_head.1), calls=%async_computation | async-start | bytes 5767168 | tf_op jit(solution)/shard_map/all_to_all | solution.py:236
  16.0 61.3 %collective-permute-start = (bf16[4,64,1408]{2,1,0:T(8,128)(2,1)}, bf16[4,64,1408]{2,1,0:T(8,128)(2,1)}, u32[]{:S(2)}, u32[]{:S(2)}) collective-permute-start(bf16[4,64,1408]{2,1,0:T(8,128)(2,1)} %mine_ref.1), channel_id=1, source_target_pairs={{0,1},{1,0},{2,3},{3,2},{4,5},{5,4},{6,7},{7,6},{8,9},{9,8},{10,11... | collective-permute-start | bytes 2162696 | tf_op jit(solution)/shard_map/ppermute | solution.py:245
  54.2 1.7 copy-start.1
  71.3 19.1 %all-to-all-start.2 = ((bf16[8,2,88,256]{3,2,1,0:T(8,128)(2,1)}), bf16[8,2,88,256]{3,2,1,0:T(8,128)(2,1)S(1)}, u32[]{:S(2)}, u32[]{:S(2)}) async-start(bf16[8,2,88,256]{3,2,1,0:T(8,128)(2,1)} %bitcast.10), calls=%async_computation.2 | async-start | bytes 1441792 | tf_op jit(solution)/shard_map/all_to_all | solution.py:236
  90.5 0.9 copy-start.2
  95.9 15.8 %collective-permute-start.1 = (bf16[2,176,704]{2,1,0:T(8,128)(2,1)}, bf16[2,176,704]{2,1,0:T(8,128)(2,1)S(1)}, u32[]{:S(2)}, u32[]{:S(2)}) collective-permute-start(bf16[2,176,704]{2,1,0:T(8,128)(2,1)} %get-tuple-element.21), channel_id=1, source_target_pairs={{0,16},{16,32},{32,48},{48,0},{1,17},{17,33},{33,49},{49,1},{2,18}... | collective-permute-start | bytes 1486856 | tf_op jit(solution)/shard_map/ppermute | solution.py:240
  97.6 26.7 %collective-permute-start.2 = (bf16[2,176,704]{2,1,0:T(8,128)(2,1)}, bf16[2,176,704]{2,1,0:T(8,128)(2,1)S(1)}, u32[]{:S(2)}, u32[]{:S(2)}) collective-permute-start(bf16[2,176,704]{2,1,0:T(8,128)(2,1)} %get-tuple-element.22), channel_id=1, source_target_pairs={{0,32},{16,48},{32,0},{48,16},{1,33},{17,49},{33,1},{49,17},{2,34}... | collective-permute-start | bytes 1486856 | tf_op jit(solution)/shard_map/ppermute | solution.py:240
  100.9 23.4 %collective-permute-start.3 = (bf16[2,176,704]{2,1,0:T(8,128)(2,1)}, bf16[2,176,704]{2,1,0:T(8,128)(2,1)S(1)}, u32[]{:S(2)}, u32[]{:S(2)}) collective-permute-start(bf16[2,176,704]{2,1,0:T(8,128)(2,1)} %get-tuple-element.23), channel_id=1, source_target_pairs={{0,48},{16,0},{32,16},{48,32},{1,49},{17,1},{33,17},{49,33},{2,50}... | collective-permute-start | bytes 1486856 | tf_op jit(solution)/shard_map/ppermute | solution.py:240
  111.7 12.5 %copy-start.3 = (bf16[2,176,704]{2,1,0:T(8,128)(2,1)}, bf16[2,176,704]{2,1,0:T(8,128)(2,1)S(1)}, u32[]{:S(2)}) copy-start(bf16[2,176,704]{2,1,0:T(8,128)(2,1)S(1)} %collective-permute-done.1.b) | copy-start | bytes 1486852
  124.2 0.8 copy-start.4
  124.2 1.0 copy-start.5
  128.1 19.8 %all-to-all-start.3 = ((bf16[32,11,704]{2,1,0:T(8,128)(2,1)}), bf16[32,11,704]{2,1,0:T(8,128)(2,1)S(1)}, u32[]{:S(2)}, u32[]{:S(2)}) async-start(bf16[32,11,704]{2,1,0:T(8,128)(2,1)} %row_sums.1), calls=%async_computation.3 | async-start | bytes 1572864 | tf_op jit(solution)/shard_map/all_to_all | solution.py:236
  147.8 36.0 %all-to-all-start.1 = ((bf16[16,3,88,256]{3,2,1,0:T(8,128)(2,1)}), bf16[16,3,88,256]{3,2,1,0:T(8,128)(2,1)S(1)}, u32[]{:S(2)}, u32[]{:S(2)}) async-start(bf16[16,3,88,256]{3,2,1,0:T(8,128)(2,1)} %spatial_backward.1), calls=%async_computation.1 | async-start | bytes 4325376 | tf_op jit(solution)/shard_map/all_to_all | solution.py:236
  183.8 1.3 copy-start

commit v2 on v1

--- a/solution.py
+++ b/solution.py
@@ -1,11 +1,10 @@
-import functools
-
 import jax
 import jax.numpy as jnp
 from jax import lax
 from jax.experimental import pallas as pl
 from jax.experimental.pallas import tpu as pltpu
 from jax.sharding import Mesh, PartitionSpec as P
+
 
 HEAD_DIM = 88
 HEADS = 16
@@ -249,8 +248,10 @@
     grads = backward(x, attended, raised, inverse)
     own, *sent = weight_terms(place, grad_out, other_grad, att)
     parts = [own] + [along_z(part, step + 1) for step, part in enumerate(sent)]
-    outs = unpack(exchange(grads, PATCH), query_rows.shape)
-    rows = exchange(row_sums(parts), PLANE)
+    home = exchange(grads, PATCH)
+    rows = row_sums(parts)
+    rows = exchange(rows, PLANE)
+    outs = unpack(home, query_rows.shape)
     total = rows.reshape(16, 2, 11, 704).astype(F32).sum(0)
     grad_weight = jnp.concatenate([total[0], total[1]], axis=1)
     return (*outs, grad_weight)

time: 189 us -> 189 us (level)
  no operation moved by 1% of the time
where the time goes in v2:
time: 189 us; the launch traced here: 188 us
  waiting for transfers between devices  103 us (54%)
  Pallas kernels  47.1 us (25%)
  starting transfers between devices  31.5 us (17%)
  local copies, waits for them, and re-layouts  4.86 us (3%)
    all_to_all x4, waiting for transfers between devices, exchange(): return lax.all_to_all(array, axes, split_axis=0, concat_axis=0, tiled=True)  80 us
    all_to_all x4, starting transfers between devices, exchange(): return lax.all_to_all(array, axes, split_axis=0, concat_axis=0, tiled=True)  25.7 us
    ppermute x3, waiting for transfers between devices, along_z(): return lax.ppermute(array, 'z', [(i, (i + step) % 4) for i in range(4)])  22.6 us
    pallas_call x1, Pallas kernels, forward(): pl.pallas_call(forward_kernel, grid=(2,), in_specs=[PAIR], out_specs=[ONE...  15.5 us
    pallas_call x1, Pallas kernels, backward(): pl.pallas_call(backward_kernel, grid=(2,), in_specs=[PAIR, ONE, RAISED, I...  14 us
    pallas_call x1, Pallas kernels, pack(): pl.pallas_call(pack_kernel, in_specs=[pl.BlockSpec(memory_space=pltpu.VME...  6.92 us
    ppermute x3, starting transfers between devices, along_z(): return lax.ppermute(array, 'z', [(i, (i + step) % 4) for i in range(4)])  5.67 us
    unnamed x12, local copies, waits for them, and re-layouts  4.85 us
  transfers between devices with their start and end apart: 8, of which 6 were waited for; matrix products, arithmetic and copies ran while one was open for 1% of the time, Pallas kernels for 16%

profile of v2, /device:TPU:1, one launch (start us, length us, event | category | flops | bytes accessed | tf_op | source)
XLA Modules:
  0.0 188.4 jit_solution(5850906009830434757)
XLA Ops:
  0.6 6.9 %pack_by_head.1 = bf16[16,4,88,256]{3,2,1,0:T(8,128)(2,1)} custom-call(bf16[4,64,1408]{2,1,0:T(8,128)(2,1)} %q_ref.1, bf16[4,64,1408]{2,1,0:T(8,128)(2,1)} %k_ref.1, bf16[4,64,1408]{2,1,0:T(8,128)(2,1)} %v_ref.1, bf16[4,64,1408]{2,1,0:T(8,128)(2,1)} %mine_ref.1, bf16[1408,1408]{1,0:T(8,128)(2,1)} %w_hbm.1), custom_call_target="tpu_custom_call" | custom-call | flops 1015021568 | bytes 10000000 | tf_op jit(solution)/shard_map/pack_by_head/pallas_call | solution.py:70
  7.6 8.4 %all-to-all-start = ((bf16[16,4,88,256]{3,2,1,0:T(8,128)(2,1)}), bf16[16,4,88,256]{3,2,1,0:T(8,128)(2,1)S(1)}, u32[]{:S(2)}, u32[]{:S(2)}) async-start(bf16[16,4,88,256]{3,2,1,0:T(8,128)(2,1)} %pack_by_head.1), calls=%async_computation | async-start | bytes 5767168 | tf_op jit(solution)/shard_map/all_to_all | solution.py:235
  16.0 0.2 collective-permute-start
  16.2 38.0 %all-to-all-done.x_ref = bf16[16,4,88,256]{3,2,1,0:T(8,128)(2,1)S(1)} async-done(((bf16[16,4,88,256]{3,2,1,0:T(8,128)(2,1)}), bf16[16,4,88,256]{3,2,1,0:T(8,128)(2,1)S(1)}, u32[]{:S(2)}, u32[]{:S(2)}) %all-to-all-start) | async-done | bytes 2883616 | tf_op jit(solution)/shard_map/all_to_all | solution.py:235
  54.2 0.0 copy-start.1
  54.2 1.7 copy-done.1
  55.8 15.5 %spatial_forward.1 = (bf16[16,1,88,256]{3,2,1,0:T(8,128)(2,1)}, bf16[4,1024,1024]{2,1,0:T(8,128)(2,1)}, f32[4,8,1024]{2,1,0:T(8,128)}) custom-call(bf16[16,4,88,256]{3,2,1,0:T(8,128)(2,1)} %copy-done.1), custom_call_target="tpu_custom_call" | custom-call | flops 4294967296 | bytes 12000000 | tf_op jit(solution)/shard_map/spatial_forward/pallas_call | solution.py:105
  71.3 5.2 %all-to-all-start.2 = ((bf16[8,2,88,256]{3,2,1,0:T(8,128)(2,1)}), bf16[8,2,88,256]{3,2,1,0:T(8,128)(2,1)S(1)}, u32[]{:S(2)}, u32[]{:S(2)}) async-start(bf16[8,2,88,256]{3,2,1,0:T(8,128)(2,1)} %bitcast.10), calls=%async_computation.2 | async-start | bytes 1441792 | tf_op jit(solution)/shard_map/all_to_all | solution.py:235
  76.6 0.7 pad_add_fusion.place_ref
  77.3 0.0 collective-permute-done.other_ref
  77.3 13.2 %all-to-all-done.2.att_ref = bf16[8,2,88,256]{3,2,1,0:T(8,128)(2,1)S(1)} async-done(((bf16[8,2,88,256]{3,2,1,0:T(8,128)(2,1)}), bf16[8,2,88,256]{3,2,1,0:T(8,128)(2,1)S(1)}, u32[]{:S(2)}, u32[]{:S(2)}) %all-to-all-start.2) | async-done | bytes 720928 | tf_op jit(solution)/shard_map/all_to_all | solution.py:235
  90.5 0.0 copy-start.2
  90.5 0.9 copy-done.2
  91.3 4.6 %weight_terms.1 = (bf16[2,176,704]{2,1,0:T(8,128)(2,1)}, bf16[2,176,704]{2,1,0:T(8,128)(2,1)}, bf16[2,176,704]{2,1,0:T(8,128)(2,1)}, bf16[2,176,704]{2,1,0:T(8,128)(2,1)}) custom-call(s32[2]{0:T(128)} %pad_add_fusion.place_ref, bf16[4,64,1408]{2,1,0:T(8,128)(2,1)} %mine_ref.1, bf16[4,64,1408]{2,1,0:T(8,128)(2,1)} %collective-permute-done.other_ref, ...), custom_call_target="tpu_custom_call" | custom-call | flops 1015021568 | bytes 5000000 | tf_op jit(solution)/shard_map/weight_terms/pallas_call | solution.py:181
  95.9 1.6 collective-permute-start.1
  97.6 3.3 %collective-permute-start.2 = (bf16[2,176,704]{2,1,0:T(8,128)(2,1)}, bf16[2,176,704]{2,1,0:T(8,128)(2,1)S(1)}, u32[]{:S(2)}, u32[]{:S(2)}) collective-permute-start(bf16[2,176,704]{2,1,0:T(8,128)(2,1)} %get-tuple-element.22), channel_id=1, source_target_pairs={{0,32},{16,48},{32,0},{48,16},{1,33},{17,49},{33,1},{49,17},{2,34}... | collective-permute-start | bytes 1486856 | tf_op jit(solution)/shard_map/ppermute | solution.py:239
  100.9 0.7 collective-permute-start.3
  101.6 10.2 %collective-permute-done.1.b = bf16[2,176,704]{2,1,0:T(8,128)(2,1)S(1)} collective-permute-done((bf16[2,176,704]{2,1,0:T(8,128)(2,1)}, bf16[2,176,704]{2,1,0:T(8,128)(2,1)S(1)}, u32[]{:S(2)}, u32[]{:S(2)}) %collective-permute-start.1) | collective-permute-done | bytes 495648 | tf_op jit(solution)/shard_map/ppermute | solution.py:239
  111.7 0.0 copy-start.3
  111.8 12.5 %collective-permute-done.2.c = bf16[2,176,704]{2,1,0:T(8,128)(2,1)S(1)} collective-permute-done((bf16[2,176,704]{2,1,0:T(8,128)(2,1)}, bf16[2,176,704]{2,1,0:T(8,128)(2,1)S(1)}, u32[]{:S(2)}, u32[]{:S(2)}) %collective-permute-start.2) | collective-permute-done | bytes 495648 | tf_op jit(solution)/shard_map/ppermute | solution.py:239
  124.2 0.0 copy-start.4
  124.2 0.0 collective-permute-done.3.d
  124.2 0.0 copy-start.5
  124.2 0.0 copy-done.3
  124.2 0.8 copy-done.4
  125.0 0.2 copy-done.5
  125.2 2.8 %row_sums.1 = bf16[32,11,704]{2,1,0:T(8,128)(2,1)} custom-call(bf16[2,176,704]{2,1,0:T(8,128)(2,1)} %get-tuple-element.20.a, bf16[2,176,704]{2,1,0:T(8,128)(2,1)} %copy-done.3, bf16[2,176,704]{2,1,0:T(8,128)(2,1)} %copy-done.4, bf16[2,176,704]{2,1,0:T(8,128)(2,1)} %copy-done.5), custom_call_target="tpu_custom_call" | custom-call | flops 1000000 | bytes 3000000 | tf_op jit(solution)/shard_map/row_sums/pallas_call | solution.py:200
  128.1 5.2 %all-to-all-start.3 = ((bf16[32,11,704]{2,1,0:T(8,128)(2,1)}), bf16[32,11,704]{2,1,0:T(8,128)(2,1)S(1)}, u32[]{:S(2)}, u32[]{:S(2)}) async-start(bf16[32,11,704]{2,1,0:T(8,128)(2,1)} %row_sums.1), calls=%async_computation.3 | async-start | bytes 1572864 | tf_op jit(solution)/shard_map/all_to_all | solution.py:235
  133.3 14.0 %spatial_backward.1 = bf16[16,3,88,256]{3,2,1,0:T(8,128)(2,1)} custom-call(bf16[16,4,88,256]{3,2,1,0:T(8,128)(2,1)} %copy-done.1, bf16[16,1,88,256]{3,2,1,0:T(8,128)(2,1)} %get-tuple-element.14.att_ref, bf16[4,1024,1024]{2,1,0:T(8,128)(2,1)} %get-tuple-element.15.e_ref, f32[4,8,1024]{2,1,0:T(8,128)} %get-tuple-element.16.inv_ref), custom_call_target="tpu_custom_call" | custom-call | flops 8589934592 | bytes 14000000 | tf_op jit(solution)/shard_map/spatial_backward/pallas_call | solution.py:148
  147.3 0.5 all-to-all-done.3
  147.8 6.8 %all-to-all-start.1 = ((bf16[16,3,88,256]{3,2,1,0:T(8,128)(2,1)}), bf16[16,3,88,256]{3,2,1,0:T(8,128)(2,1)S(1)}, u32[]{:S(2)}, u32[]{:S(2)}) async-start(bf16[16,3,88,256]{3,2,1,0:T(8,128)(2,1)} %spatial_backward.1), calls=%async_computation.1 | async-start | bytes 4325376 | tf_op jit(solution)/shard_map/all_to_all | solution.py:235
  154.6 0.1 convert_reduce_fusion
  154.8 0.7 pad_maximum_fusion
  155.5 28.3 %all-to-all-done.1.x_ref = bf16[16,3,88,256]{3,2,1,0:T(8,128)(2,1)S(1)} async-done(((bf16[16,3,88,256]{3,2,1,0:T(8,128)(2,1)}), bf16[16,3,88,256]{3,2,1,0:T(8,128)(2,1)S(1)}, u32[]{:S(2)}, u32[]{:S(2)}) %all-to-all-start.1) | async-done | bytes 2162720 | tf_op jit(solution)/shard_map/all_to_all | solution.py:235
  183.8 0.0 copy-start
  183.8 1.3 copy-done
  185.2 3.2 %unpack_by_token.1 = (bf16[4,64,1408]{2,1,0:T(8,128)(2,1)}, bf16[4,64,1408]{2,1,0:T(8,128)(2,1)}, bf16[4,64,1408]{2,1,0:T(8,128)(2,1)}) custom-call(bf16[16,3,88,256]{3,2,1,0:T(8,128)(2,1)} %copy-done), custom_call_target="tpu_custom_call" | custom-call | bytes 5000000 | tf_op jit(solution)/shard_map/unpack_by_token/pallas_call | solution.py:219
  (1 shorter events, 0.0 us)
Async XLA Ops:
  7.6 46.6 %all-to-all-start = ((bf16[16,4,88,256]{3,2,1,0:T(8,128)(2,1)}), bf16[16,4,88,256]{3,2,1,0:T(8,128)(2,1)S(1)}, u32[]{:S(2)}, u32[]{:S(2)}) async-start(bf16[16,4,88,256]{3,2,1,0:T(8,128)(2,1)} %pack_by_head.1), calls=%async_computation | async-start | bytes 5767168 | tf_op jit(solution)/shard_map/all_to_all | solution.py:235
  16.0 61.3 %collective-permute-start = (bf16[4,64,1408]{2,1,0:T(8,128)(2,1)}, bf16[4,64,1408]{2,1,0:T(8,128)(2,1)}, u32[]{:S(2)}, u32[]{:S(2)}) collective-permute-start(bf16[4,64,1408]{2,1,0:T(8,128)(2,1)} %mine_ref.1), channel_id=1, source_target_pairs={{0,1},{1,0},{2,3},{3,2},{4,5},{5,4},{6,7},{7,6},{8,9},{9,8},{10,11... | collective-permute-start | bytes 2162696 | tf_op jit(solution)/shard_map/ppermute | solution.py:244
  54.2 1.7 copy-start.1
  71.3 19.1 %all-to-all-start.2 = ((bf16[8,2,88,256]{3,2,1,0:T(8,128)(2,1)}), bf16[8,2,88,256]{3,2,1,0:T(8,128)(2,1)S(1)}, u32[]{:S(2)}, u32[]{:S(2)}) async-start(bf16[8,2,88,256]{3,2,1,0:T(8,128)(2,1)} %bitcast.10), calls=%async_computation.2 | async-start | bytes 1441792 | tf_op jit(solution)/shard_map/all_to_all | solution.py:235
  90.5 0.9 copy-start.2
  95.9 15.8 %collective-permute-start.1 = (bf16[2,176,704]{2,1,0:T(8,128)(2,1)}, bf16[2,176,704]{2,1,0:T(8,128)(2,1)S(1)}, u32[]{:S(2)}, u32[]{:S(2)}) collective-permute-start(bf16[2,176,704]{2,1,0:T(8,128)(2,1)} %get-tuple-element.21), channel_id=1, source_target_pairs={{0,16},{16,32},{32,48},{48,0},{1,17},{17,33},{33,49},{49,1},{2,18}... | collective-permute-start | bytes 1486856 | tf_op jit(solution)/shard_map/ppermute | solution.py:239
  97.6 26.7 %collective-permute-start.2 = (bf16[2,176,704]{2,1,0:T(8,128)(2,1)}, bf16[2,176,704]{2,1,0:T(8,128)(2,1)S(1)}, u32[]{:S(2)}, u32[]{:S(2)}) collective-permute-start(bf16[2,176,704]{2,1,0:T(8,128)(2,1)} %get-tuple-element.22), channel_id=1, source_target_pairs={{0,32},{16,48},{32,0},{48,16},{1,33},{17,49},{33,1},{49,17},{2,34}... | collective-permute-start | bytes 1486856 | tf_op jit(solution)/shard_map/ppermute | solution.py:239
  100.9 23.4 %collective-permute-start.3 = (bf16[2,176,704]{2,1,0:T(8,128)(2,1)}, bf16[2,176,704]{2,1,0:T(8,128)(2,1)S(1)}, u32[]{:S(2)}, u32[]{:S(2)}) collective-permute-start(bf16[2,176,704]{2,1,0:T(8,128)(2,1)} %get-tuple-element.23), channel_id=1, source_target_pairs={{0,48},{16,0},{32,16},{48,32},{1,49},{17,1},{33,17},{49,33},{2,50}... | collective-permute-start | bytes 1486856 | tf_op jit(solution)/shard_map/ppermute | solution.py:239
  111.7 12.5 %copy-start.3 = (bf16[2,176,704]{2,1,0:T(8,128)(2,1)}, bf16[2,176,704]{2,1,0:T(8,128)(2,1)S(1)}, u32[]{:S(2)}) copy-start(bf16[2,176,704]{2,1,0:T(8,128)(2,1)S(1)} %collective-permute-done.1.b) | copy-start | bytes 1486852
  124.2 0.8 copy-start.4
  124.2 1.0 copy-start.5
  128.1 19.8 %all-to-all-start.3 = ((bf16[32,11,704]{2,1,0:T(8,128)(2,1)}), bf16[32,11,704]{2,1,0:T(8,128)(2,1)S(1)}, u32[]{:S(2)}, u32[]{:S(2)}) async-start(bf16[32,11,704]{2,1,0:T(8,128)(2,1)} %row_sums.1), calls=%async_computation.3 | async-start | bytes 1572864 | tf_op jit(solution)/shard_map/all_to_all | solution.py:235
  147.8 36.0 %all-to-all-start.1 = ((bf16[16,3,88,256]{3,2,1,0:T(8,128)(2,1)}), bf16[16,3,88,256]{3,2,1,0:T(8,128)(2,1)S(1)}, u32[]{:S(2)}, u32[]{:S(2)}) async-start(bf16[16,3,88,256]{3,2,1,0:T(8,128)(2,1)} %spatial_backward.1), calls=%async_computation.1 | async-start | bytes 4325376 | tf_op jit(solution)/shard_map/all_to_all | solution.py:235
  183.8 1.3 copy-start

commit v3 on v2

v3 whole, which is shorter than its diff:
```python
import functools

import jax
import jax.numpy as jnp
from jax import lax
from jax.experimental import pallas as pl
from jax.experimental.pallas import tpu as pltpu
from jax.sharding import Mesh, PartitionSpec as P


HEAD_DIM = 88
HEADS = 16
HALF = 64
QUARTER = 22
PADDED = 24
BLOCK = 256
SOFTMAX_SCALE = HEAD_DIM ** (-0.5)
EXP2_SCALE = SOFTMAX_SCALE * 1.4426950408889634
F32, BF16 = jnp.float32, jnp.bfloat16


def head_of(slot):
    return 8 * (slot % 2) + slot // 2


def low_lanes(shape):
    return lax.broadcasted_iota(jnp.int32, shape, 1) < HALF


def turned(tile):
    return pltpu.roll(tile, HALF, 1)


def frame_pair(ref, n):
    first, second = [], []
    for s in range(8):
        a, b = ref[s, n].astype(F32), ref[s + 8, n].astype(F32)
        low = low_lanes(a.shape)
        first.append(jnp.where(low, a, turned(b)).astype(BF16))
        second.append(jnp.where(low, turned(a), b).astype(BF16))
    return jnp.concatenate(first, 1), jnp.concatenate(second, 1)


def put_back(ref, n, first, second):
    for s in range(8):
        a, b = first[:, 128 * s : 128 * (s + 1)], second[:, 128 * s : 128 * (s + 1)]
        low = low_lanes(a.shape)
        ref[s, n] = jnp.where(low, a, turned(b)).astype(BF16)
        ref[s + 8, n] = jnp.where(low, turned(a), b).astype(BF16)


def pack_kernel(q_ref, k_ref, v_ref, g_ref, w_hbm, out_ref, w_ref, sem):
    fetch = pltpu.make_async_copy(w_hbm, w_ref, sem)
    fetch.start()

    def place(n, rows):
        turned_rows = rows.T
        for slot in range(HEADS):
            at = HEAD_DIM * head_of(slot)
            out_ref[slot, n] = turned_rows[at : at + HEAD_DIM].astype(BF16)

    features = q_ref.shape[-1]
    for n, ref in enumerate((q_ref, k_ref, v_ref)):
        place(n, ref[...].reshape(-1, features))
    fetch.wait()
    place(
        3,
        jnp.dot(g_ref[...].reshape(-1, features), w_ref[...], preferred_element_type=F32).astype(BF16),
    )


def pack(query, key, value, upstream, weight):
    tokens = query.shape[0] * query.shape[1]
    return pl.pallas_call(
        pack_kernel,
        in_specs=[pl.BlockSpec(memory_space=pltpu.VMEM)] * 4 + [pl.BlockSpec(memory_space=pl.ANY)],
        out_specs=pl.BlockSpec(memory_space=pltpu.VMEM),
        out_shape=jax.ShapeDtypeStruct((HEADS, 4, HEAD_DIM, tokens), BF16),
        scratch_shapes=[pltpu.VMEM(weight.shape, BF16), pltpu.SemaphoreType.DMA],
        cost_estimate=pl.CostEstimate(flops=2 * tokens * weight.size, bytes_accessed=10_000_000, transcendentals=0),
        compiler_params=pltpu.CompilerParams(vmem_limit_bytes=62 << 20),
        name="pack_by_head",
    )(query, key, value, upstream, weight)


def forward_kernel(x_ref, att_ref, e_ref, row_ref, o_ref):
    qs, ks, vs, gs = (frame_pair(x_ref, n) for n in range(4))
    for f in range(2):
        q_t, k, v_t = qs[f], ks[f].T, vs[f]
        for b in range(1024 // BLOCK):
            cols = slice(b * BLOCK, (b + 1) * BLOCK)
            scores = jnp.dot(k, q_t[:, cols], preferred_element_type=F32)
            row_max = jnp.max(scores, axis=0, keepdims=True)
            raised = jnp.exp2(scores * EXP2_SCALE - row_max * EXP2_SCALE)
            inverse = 1.0 / jnp.sum(raised, axis=0, keepdims=True)
            raised = raised.astype(BF16)
            e_ref[f, :, cols] = raised
            attended = jnp.dot(v_t, raised, preferred_element_type=F32) * inverse
            o_ref[f, :, cols] = attended
            row_dot = jnp.sum(gs[f][:, cols].astype(F32) * attended, axis=0, keepdims=True) * inverse
            row_ref[f, 0:1, cols] = inverse
            row_ref[f, 1:2, cols] = row_dot
    for s in range(8):
        a, b = o_ref[0, :, 128 * s : 128 * (s + 1)], o_ref[1, :, 128 * s : 128 * (s + 1)]
        low = low_lanes(a.shape)
        for slot, tile in ((s, jnp.where(low, a, turned(b))), (s + 8, jnp.where(low, turned(a), b))):
            for quarter in range(4):
                rows = tile[QUARTER * quarter : QUARTER * (quarter + 1)]
                rows = jnp.concatenate([rows, jnp.zeros((PADDED - QUARTER, 128), F32)], axis=0)
                att_ref[quarter, slot // 2, slot % 2] = rows.astype(BF16)


PAIR = pl.BlockSpec((HEADS, 4, HEAD_DIM, 128), lambda i: (0, 0, 0, i))
RAISED = pl.BlockSpec((2, 1024, 1024), lambda i: (i, 0, 0))
PER_ROW = pl.BlockSpec((2, 8, 1024), lambda i: (i, 0, 0))


def forward(x):
    return pl.pallas_call(
        forward_kernel,
        grid=(2,),
        in_specs=[PAIR],
        out_specs=[pl.BlockSpec((4, 8, 2, PADDED, 128), lambda i: (0, 0, 0, 0, i)), RAISED, PER_ROW],
        out_shape=[
            jax.ShapeDtypeStruct((4, 8, 2, PADDED, 256), BF16),
            jax.ShapeDtypeStruct((4, 1024, 1024), BF16),
            jax.ShapeDtypeStruct((4, 8, 1024), F32),
        ],
        scratch_shapes=[pltpu.VMEM((2, HEAD_DIM, 1024), F32)],
        cost_estimate=pl.CostEstimate(flops=4 * 4 * 1024 * 1024 * 256, bytes_accessed=12_000_000, transcendentals=1 << 22),
        compiler_params=pltpu.CompilerParams(vmem_limit_bytes=60 << 20),
        name="spatial_forward",
    )(x)


def backward_kernel(x_ref, e_ref, row_ref, out_ref, dq_ref, dk_ref, dv_ref):
    qs, ks, vs, gs = (frame_pair(x_ref, n) for n in range(4))
    for f in range(2):
        q_t, k_t, v = qs[f], ks[f], vs[f].T
        g_t = (gs[f].astype(F32) * row_ref[f, 0:1, :]).astype(BF16)
        row_dot = row_ref[f, 1:2, :]
        for b in range(1024 // BLOCK):
            cols = slice(b * BLOCK, (b + 1) * BLOCK)
            raised = e_ref[f, :, cols]
            grad_probs = jnp.dot(v, g_t[:, cols], preferred_element_type=F32)
            grad_scores = (raised.astype(F32) * (grad_probs - row_dot[:, cols])).astype(BF16)
            dq_ref[f, :, cols] = jnp.dot(k_t, grad_scores, preferred_element_type=F32) * SOFTMAX_SCALE
            dk = lax.dot_general(q_t[:, cols], grad_scores, (((1,), (1,)), ((), ())), preferred_element_type=F32)
            dv = lax.dot_general(g_t[:, cols], raised, (((1,), (1,)), ((), ())), preferred_element_type=F32)
            if b == 0:
                dk_ref[f], dv_ref[f] = dk, dv
            else:
                dk_ref[f] += dk
                dv_ref[f] += dv
    put_back(out_ref, 0, dq_ref[0], dq_ref[1])
    put_back(out_ref, 1, dk_ref[0] * SOFTMAX_SCALE, dk_ref[1] * SOFTMAX_SCALE)
    put_back(out_ref, 2, dv_ref[0], dv_ref[1])


def backward(x, raised, per_row):
    return pl.pallas_call(
        backward_kernel,
        grid=(2,),
        in_specs=[PAIR, RAISED, PER_ROW],
        out_specs=pl.BlockSpec((HEADS, 3, HEAD_DIM, 128), lambda i: (0, 0, 0, i)),
        out_shape=jax.ShapeDtypeStruct((HEADS, 3, HEAD_DIM, 256), BF16),
        scratch_shapes=[pltpu.VMEM((2, HEAD_DIM, 1024), F32)] * 3,
        cost_estimate=pl.CostEstimate(flops=8 * 4 * 1024 * 1024 * 256, bytes_accessed=14_000_000, transcendentals=0),
        compiler_params=pltpu.CompilerParams(vmem_limit_bytes=60 << 20),
        name="spatial_backward",
    )(x, raised, per_row)


def weight_kernel(place_ref, *refs):
    grads, att_ref, outs, (a_ref, t_ref) = refs[:8], refs[8], refs[9:13], refs[13:]
    core, z, y = place_ref[0], place_ref[1], place_ref[2]
    total = None
    for r in range(4):
        source = lax.rem(z + 4 - r, 4)
        for side in range(2):
            spot = lax.rem(core + side, 2)
            for i in range(8):
                a_ref[QUARTER * i : QUARTER * (i + 1)] = att_ref[source * 8 + i, spot].astype(F32)[:QUARTER]
            grad = grads[4 * side + r][...]
            term = jnp.dot(
                a_ref[...].astype(BF16), grad.reshape(-1, grad.shape[-1]), preferred_element_type=F32
            )
            total = term if total is None else total + term
    t_ref[...] = total.T
    for s, out in enumerate(outs):
        to = lax.rem(y + s, 4)
        for depth in range(4):
            start = lax.rem(to, 2) * 704 + depth * 176 + (to // 2) * 88
            block = t_ref[pl.ds(pl.multiple_of(start, 8), 88), :]
            for x in range(4):
                out[x, depth] = block[QUARTER * x : QUARTER * (x + 1)].astype(out.dtype)


VM, SM = pl.BlockSpec(memory_space=pltpu.VMEM), pl.BlockSpec(memory_space=pltpu.SMEM)


def weight_terms(place, grads, att):
    shape = (4, 4, QUARTER, 8 * QUARTER)
    features = grads[0].shape[-1]
    return pl.pallas_call(
        weight_kernel,
        in_specs=[SM] + [VM] * 9,
        out_specs=[VM] * 4,
        out_shape=[jax.ShapeDtypeStruct(shape, F32)] + [jax.ShapeDtypeStruct(shape, BF16)] * 3,
        scratch_shapes=[pltpu.VMEM((8 * QUARTER, 256), F32), pltpu.VMEM((features, 8 * QUARTER), F32)],
        cost_estimate=pl.CostEstimate(flops=2 * 2048 * 1408 * 176, bytes_accessed=8_000_000, transcendentals=0),
        compiler_params=pltpu.CompilerParams(vmem_limit_bytes=24 << 20),
        name="weight_terms",
    )(place, *grads, att)


def sums_kernel(coordinate, place_ref, *refs):
    parts, outs, total = refs[:4], refs[4:8], refs[8]
    total[...] = sum(part[...].astype(F32) for part in parts[1:]) + parts[0][...]
    for s, out in enumerate(outs):
        out[...] = total[lax.rem(place_ref[coordinate] + s, 4)].astype(out.dtype)


def block_sums(place, parts, coordinate, sent):
    shape = parts[0].shape
    return pl.pallas_call(
        functools.partial(sums_kernel, coordinate),
        in_specs=[SM] + [VM] * 4,
        out_specs=[VM] * 4,
        out_shape=[jax.ShapeDtypeStruct(shape[1:], F32)] + [jax.ShapeDtypeStruct(shape[1:], sent)] * 3,
        scratch_shapes=[pltpu.VMEM(shape, F32)],
        cost_estimate=pl.CostEstimate(flops=1_000_000, bytes_accessed=3_000_000, transcendentals=0),
        compiler_params=pltpu.CompilerParams(vmem_limit_bytes=8 << 20),
        name="block_sums",
    )(place, *parts)


def pick_kernel(place_ref, *refs):
    parts, mine, theirs = refs[:4], refs[4], refs[5]
    core, z = place_ref[0], place_ref[1]
    for r, part in enumerate(parts):
        both = part[...]
        first, second = both[:11], both[11:]
        source = lax.rem(z + 4 - r, 4)
        mine[source] = jnp.where(core == 0, first, second)
        theirs[source] = jnp.where(core == 0, second, first)


def pick(place, parts):
    shape = jax.ShapeDtypeStruct((4, 11, 8 * QUARTER), F32)
    return pl.pallas_call(
        pick_kernel,
        in_specs=[SM] + [VM] * 4,
        out_specs=[VM] * 2,
        out_shape=[shape] * 2,
        cost_estimate=pl.CostEstimate(flops=1_000, bytes_accessed=200_000, transcendentals=0),
        compiler_params=pltpu.CompilerParams(vmem_limit_bytes=4 << 20),
        name="pick_rows",
    )(place, *parts)


def join_kernel(place_ref, mine, theirs, out, scratch):
    core = place_ref[0]
    scratch[core] = mine[...]
    scratch[1 - core] = theirs[...]
    for head in range(HEADS):
        i = head % 8
        for z in range(4):
            at = head * HEAD_DIM + z * QUARTER
            out[:, at : at + QUARTER] = scratch[head // 8, z][:, QUARTER * i : QUARTER * (i + 1)]


def join(place, mine, theirs):
    return pl.pallas_call(
        join_kernel,
        in_specs=[SM, VM, VM],
        out_specs=VM,
        out_shape=jax.ShapeDtypeStruct((11, HEADS * HEAD_DIM), F32),
        scratch_shapes=[pltpu.VMEM((2, 4, 11, 8 * QUARTER), F32)],
        cost_estimate=pl.CostEstimate(flops=1_000, bytes_accessed=200_000, transcendentals=0),
        compiler_params=pltpu.CompilerParams(vmem_limit_bytes=4 << 20),
        name="join_columns",
    )(place, mine, theirs)


def unpack_kernel(x_ref, q_ref, k_ref, v_ref, t_ref):
    for n, ref in enumerate((q_ref, k_ref, v_ref)):
        for slot in range(HEADS):
            at = HEAD_DIM * head_of(slot)
            t_ref[at : at + HEAD_DIM] = x_ref[slot, n]
        ref[...] = t_ref[...].T.reshape(ref.shape)


def unpack(x, shape):
    return pl.pallas_call(
        unpack_kernel,
        in_specs=[pl.BlockSpec(memory_space=pltpu.VMEM)],
        out_specs=[pl.BlockSpec(memory_space=pltpu.VMEM)] * 3,
        out_shape=[jax.ShapeDtypeStruct(shape, BF16)] * 3,
        scratch_shapes=[pltpu.VMEM((shape[-1], shape[0] * shape[1]), BF16)],
        cost_estimate=pl.CostEstimate(flops=0, bytes_accessed=5_000_000, transcendentals=0),
        compiler_params=pltpu.CompilerParams(vmem_limit_bytes=20 << 20),
        name="unpack_by_token",
    )(x)


FRAME, PATCH = ("y_lo", "z"), ("y_hi", "x", "core")


def exchange(array, axes):
    return lax.all_to_all(array, axes, split_axis=0, concat_axis=0, tiled=True)


def along(array, axis, step):
    return lax.ppermute(array, axis, [(i, (i + step) % 4) for i in range(4)])


def along_y(array, step):
    place = lambda y: (y % 2) * 2 + y // 2
    return lax.ppermute(array, ("y_lo", "y_hi"), [(place(y), place((y + step) % 4)) for y in range(4)])


def other_core(array):
    return lax.ppermute(array, "core", [(0, 1), (1, 0)])


def shards(query_rows, key_rows, value_rows, grad_out, out_weight):
    axis = lax.axis_index
    place = jnp.stack([axis("core"), axis("z"), axis("y_hi") * 2 + axis("y_lo"), axis("x")]).astype(jnp.int32)
    x = exchange(pack(query_rows, key_rows, value_rows, grad_out, out_weight), PATCH)
    gathered = [grad_out] + [along(grad_out, "z", r) for r in (1, 2, 3)]
    gathered += [other_core(array) for array in gathered]
    attended, raised, per_row = forward(x)
    att = exchange(attended.reshape(32, 2, PADDED, 256), ("z", "y_hi", "x"))
    grads = backward(x, raised, per_row)
    home = exchange(grads, PATCH)
    own, *sent = weight_terms(place, gathered, att)
    parts = [own] + [along_y(part, s) for s, part in enumerate(sent, 1)]
    own, *sent = block_sums(place, parts, 3, BF16)
    parts = [own] + [along(part, "x", s) for s, part in enumerate(sent, 1)]
    own, *sent = block_sums(place, parts, 1, F32)
    parts = [own] + [along(part, "z", s) for s, part in enumerate(sent, 1)]
    mine, theirs = pick(place, parts)
    theirs = other_core(theirs)
    grad_weight = join(place, mine, theirs)
    outs = unpack(home, query_rows.shape)
    return (*outs, grad_weight)


def solution(mesh):
    chips = Mesh(mesh.devices.reshape(2, 4, 2, 4, 2), FRAME + PATCH)
    rows = P(FRAME, PATCH, None)
    return jax.shard_map(
        shards,
        mesh=chips,
        in_specs=(rows, rows, rows, rows, P()),
        out_specs=(rows, rows, rows, P(FRAME + PATCH, None)),
        check_vma=False,
    )
```

time: 189 us -> 176 us (0.931)
  waiting for transfers between devices: 103 us -> 45.3 us
  blocking collectives: 0 us -> 45.3 us
  starting transfers between devices: 31.5 us -> 38.1 us
  local copies, waits for them, and re-layouts: 4.86 us -> 1.11 us
  Pallas kernels: 47.1 us -> 45.1 us
    all_to_all x4 -> x2, waiting for transfers between devices: 80 us -> 1.1 us  [exchange(): return lax.all_to_all(array, axes, split_axis=0, concat_axis=0, tiled=True)]
    all_to_all x0 -> x1, blocking collectives: none -> 45.3 us  [exchange(): return lax.all_to_all(array, axes, split_axis=0, concat_axis=0, tiled=True)]
    ppermute x4 -> x17, waiting for transfers between devices: 22.6 us -> 44.2 us  [the longest x9 32.4 us: along(): return lax.ppermute(array, axis, [(i, (i + step) % 4) for i in range(4)])]
    ppermute x4 -> x17, starting transfers between devices: 5.85 us -> 25.3 us  [the longest x9 13.2 us: along(): return lax.ppermute(array, axis, [(i, (i + step) % 4) for i in range(4)])]
    all_to_all x4 -> x2, starting transfers between devices: 25.7 us -> 12.8 us  [exchange(): return lax.all_to_all(array, axes, split_axis=0, concat_axis=0, tiled=True)]
    unnamed x12 -> x2, local copies, waits for them, and re-layouts: 4.85 us -> 1.11 us
    pallas_call x4 -> x7, Pallas kernels: 37 us -> 36.6 us  [the longest x1 15.6 us: forward(): pl.pallas_call(forward_kernel, grid=(2,), in_specs=[PAIR], out_specs=[pl....]
  transfers between devices with their start and end apart: 8 -> 19, of which waited for: 6 -> 13; matrix products, arithmetic and copies ran while one was open for 1% -> 0% of each run, Pallas kernels for 16% -> 12%
where the time goes in v3:
time: 176 us
  blocking collectives  45.3 us (26%)
  waiting for transfers between devices  45.3 us (26%)
  Pallas kernels  45.1 us (26%)
  starting transfers between devices  38.1 us (22%)
    all_to_all x1, blocking collectives, exchange(): return lax.all_to_all(array, axes, split_axis=0, concat_axis=0, tiled=True)  45.3 us
    ppermute x9, waiting for transfers between devices, along(): return lax.ppermute(array, axis, [(i, (i + step) % 4) for i in range(4)])  32.4 us
    pallas_call x1, Pallas kernels, forward(): pl.pallas_call(forward_kernel, grid=(2,), in_specs=[PAIR], out_specs=[pl....  15.6 us
    pallas_call x1, Pallas kernels, backward(): pl.pallas_call(backward_kernel, grid=(2,), in_specs=[PAIR, RAISED, PER_RO...  13.6 us
    ppermute x9, starting transfers between devices, along(): return lax.ppermute(array, axis, [(i, (i + step) % 4) for i in range(4)])  13.2 us
    all_to_all x2, starting transfers between devices, exchange(): return lax.all_to_all(array, axes, split_axis=0, concat_axis=0, tiled=True)  12.8 us
    ppermute x3, waiting for transfers between devices, along_y(): lax.ppermute(array, ('y_lo', 'y_hi'), [(place(y), place((y + step) % 4))...  7.76 us
    ppermute x5, starting transfers between devices, other_core(): return lax.ppermute(array, 'core', [(0, 1), (1, 0)])  7.14 us
  transfers between devices with their start and end apart: 19, of which 13 were waited for; matrix products, arithmetic and copies ran while one was open for 0% of the time, Pallas kernels for 12%

profile of v3, /device:TPU:1, one launch (start us, length us, event | category | flops | bytes accessed | tf_op | source)
XLA Modules:
  0.0 175.8 jit_solution(14514768805747396059)
XLA Ops:
  0.6 6.9 %pack_by_head.1 = bf16[16,4,88,256]{3,2,1,0:T(8,128)(2,1)} custom-call(bf16[4,64,1408]{2,1,0:T(8,128)(2,1)} %q_ref.1, bf16[4,64,1408]{2,1,0:T(8,128)(2,1)} %k_ref.1, bf16[4,64,1408]{2,1,0:T(8,128)(2,1)} %v_ref.1, bf16[4,64,1408]{2,1,0:T(8,128)(2,1)} %refs_0_.1, bf16[1408,1408]{1,0:T(8,128)(2,1)} %w_hbm.1), custom_call_target="tpu_custom_call" | custom-call | flops 1015021568 | bytes 10000000 | tf_op jit(solution)/shard_map/pack_by_head/pallas_call | solution.py:74
  7.5 45.3 %all_to_all.15.x_ref = bf16[16,4,88,256]{3,2,1,0:T(8,128)(2,1)} all-to-all(bf16[16,4,88,256]{3,2,1,0:T(8,128)(2,1)} %pack_by_head.1), channel_id=1, replica_groups=mesh['y_lo'=2,'z'=4,'y_hi'=2,'x'=4,'core'=2] {'y_hi','x','core'}, dimensions={0} | all-to-all | bytes 5767168 | tf_op jit(solution)/shard_map/all_to_all | solution.py:311
  52.9 15.6 %spatial_forward.1 = (bf16[4,8,2,24,256]{4,3,2,1,0:T(8,128)(2,1)}, bf16[4,1024,1024]{2,1,0:T(8,128)(2,1)}, f32[4,8,1024]{2,1,0:T(8,128)}) custom-call(bf16[16,4,88,256]{3,2,1,0:T(8,128)(2,1)} %all_to_all.15.x_ref), custom_call_target="tpu_custom_call" | custom-call | flops 4294967296 | bytes 12000000 | tf_op jit(solution)/shard_map/spatial_forward/pallas_call | solution.py:119
  68.5 6.6 %all-to-all-start.2 = ((bf16[32,2,24,256]{3,2,1,0:T(8,128)(2,1)}), bf16[32,2,24,256]{3,2,1,0:T(8,128)(2,1)S(1)}, u32[]{:S(2)}, u32[]{:S(2)}) async-start(bf16[32,2,24,256]{3,2,1,0:T(8,128)(2,1)} %bitcast.5), calls=%async_computation.2 | async-start | bytes 1572864 | tf_op jit(solution)/shard_map/all_to_all | solution.py:311
  75.0 13.6 %spatial_backward.1 = bf16[16,3,88,256]{3,2,1,0:T(8,128)(2,1)} custom-call(bf16[16,4,88,256]{3,2,1,0:T(8,128)(2,1)} %all_to_all.15.x_ref, bf16[4,1024,1024]{2,1,0:T(8,128)(2,1)} %get-tuple-element.24.e_ref, f32[4,8,1024]{2,1,0:T(8,128)} %get-tuple-element.25.row_ref), custom_call_target="tpu_custom_call" | custom-call | flops 8589934592 | bytes 14000000 | tf_op jit(solution)/shard_map/spatial_backward/pallas_call | solution.py:161
  88.7 1.1 all-to-all-done.2.refs_8_
  89.8 6.3 %all-to-all-start.1 = ((bf16[16,3,88,256]{3,2,1,0:T(8,128)(2,1)}), bf16[16,3,88,256]{3,2,1,0:T(8,128)(2,1)S(1)}, u32[]{:S(2)}, u32[]{:S(2)}) async-start(bf16[16,3,88,256]{3,2,1,0:T(8,128)(2,1)} %spatial_backward.1), calls=%async_computation.1 | async-start | bytes 4325376 | tf_op jit(solution)/shard_map/all_to_all | solution.py:311
  96.0 1.2 collective-permute-start
  97.2 2.5 %collective-permute-start.1 = (bf16[4,64,1408]{2,1,0:T(8,128)(2,1)}, bf16[4,64,1408]{2,1,0:T(8,128)(2,1)}, u32[]{:S(2)}, u32[]{:S(2)}) collective-permute-start(bf16[4,64,1408]{2,1,0:T(8,128)(2,1)} %refs_0_.1), channel_id=1, source_target_pairs={{0,32},{16,48},{32,0},{48,16},{1,33},{17,49},{33,1},{49,17},{2,34}... | collective-permute-start | bytes 2162696 | tf_op jit(solution)/shard_map/ppermute | solution.py:315
  99.7 1.1 collective-permute-start.2
  100.8 1.0 collective-permute-start.3
  101.8 13.3 %collective-permute-done.refs_1_ = bf16[4,64,1408]{2,1,0:T(8,128)(2,1)} collective-permute-done((bf16[4,64,1408]{2,1,0:T(8,128)(2,1)}, bf16[4,64,1408]{2,1,0:T(8,128)(2,1)}, u32[]{:S(2)}, u32[]{:S(2)}) %collective-permute-start) | collective-permute-done | bytes 720928 | tf_op jit(solution)/shard_map/ppermute | solution.py:315
  115.1 1.0 collective-permute-start.4
  116.1 15.4 %collective-permute-done.1.refs_2_ = bf16[4,64,1408]{2,1,0:T(8,128)(2,1)} collective-permute-done((bf16[4,64,1408]{2,1,0:T(8,128)(2,1)}, bf16[4,64,1408]{2,1,0:T(8,128)(2,1)}, u32[]{:S(2)}, u32[]{:S(2)}) %collective-permute-start.1) | collective-permute-done | bytes 720928 | tf_op jit(solution)/shard_map/ppermute | solution.py:315
  131.5 1.0 collective-permute-start.5
  132.6 0.0 collective-permute-done.2.refs_3_
  132.6 0.0 collective-permute-start.6
  132.6 0.1 pad_add_fusion.place_ref
  132.6 0.0 collective-permute-done.3.refs_4_
  132.6 0.0 collective-permute-done.4.refs_5_
  132.6 2.1 %collective-permute-done.5.refs_6_ = bf16[4,64,1408]{2,1,0:T(8,128)(2,1)} collective-permute-done((bf16[4,64,1408]{2,1,0:T(8,128)(2,1)}, bf16[4,64,1408]{2,1,0:T(8,128)(2,1)}, u32[]{:S(2)}, u32[]{:S(2)}) %collective-permute-start.5) | collective-permute-done | bytes 720928 | tf_op jit(solution)/shard_map/ppermute | solution.py:324
  134.7 1.0 collective-permute-done.6.refs_7_
  135.7 0.0 copy-start
  135.7 1.1 copy-done
  136.9 4.2 %weight_terms.1 = (f32[4,4,22,176]{3,2,1,0:T(8,128)S(1)}, bf16[4,4,22,176]{3,2,1,0:T(8,128)(2,1)S(1)}, bf16[4,4,22,176]{3,2,1,0:T(8,128)(2,1)S(1)}, bf16[4,4,22,176]{3,2,1,0:T(8,128)(2,1)S(1)}) custom-call(s32[4]{0:T(128)S(1)} %pad_add_fusion.place_ref, bf16[4,64,1408]{2,1,0:T(8,128)(2,1)S(1)} %copy-done, bf16[4,64,1408]{2,1,0:T(8,128)(2,1)} %collective-permute-done.refs_1_, ...), custom_call_target="tpu_custom_call" | custom-call | flops 1015021568 | bytes 8000000 | tf_op jit(solution)/shard_map/weight_terms/pallas_call | solution.py:205
  141.0 0.5 collective-permute-start.7
  141.5 3.5 %collective-permute-start.8 = (bf16[4,4,22,176]{3,2,1,0:T(8,128)(2,1)S(1)}, bf16[4,4,22,176]{3,2,1,0:T(8,128)(2,1)S(1)}, u32[]{:S(2)}, u32[]{:S(2)}) collective-permute-start(bf16[4,4,22,176]{3,2,1,0:T(8,128)(2,1)S(1)} %get-tuple-element.32), channel_id=1, source_target_pairs={{0,8},{64,72},{8,0},{72,64},{1,9},{65,73},{9,1},{73,65},{2,10},{66... | collective-permute-start | bytes 371720 | tf_op jit(solution)/shard_map/ppermute | solution.py:320
  145.0 1.1 collective-permute-start.9
  146.0 2.4 %collective-permute-done.7.refs_1_ = bf16[4,4,22,176]{3,2,1,0:T(8,128)(2,1)S(1)} collective-permute-done((bf16[4,4,22,176]{3,2,1,0:T(8,128)(2,1)S(1)}, bf16[4,4,22,176]{3,2,1,0:T(8,128)(2,1)S(1)}, u32[]{:S(2)}, u32[]{:S(2)}) %collective-permute-start.7) | collective-permute-done | bytes 123936 | tf_op jit(solution)/shard_map/ppermute | solution.py:320
  148.4 5.4 %collective-permute-done.8.refs_2_ = bf16[4,4,22,176]{3,2,1,0:T(8,128)(2,1)S(1)} collective-permute-done((bf16[4,4,22,176]{3,2,1,0:T(8,128)(2,1)S(1)}, bf16[4,4,22,176]{3,2,1,0:T(8,128)(2,1)S(1)}, u32[]{:S(2)}, u32[]{:S(2)}) %collective-permute-start.8) | collective-permute-done | bytes 123936 | tf_op jit(solution)/shard_map/ppermute | solution.py:320
  153.8 0.0 collective-permute-done.9.refs_3_
  153.8 0.7 block_sums.2
  154.5 1.3 collective-permute-start.10
  155.8 2.4 %collective-permute-start.11 = (bf16[4,22,176]{2,1,0:T(8,128)(2,1)S(1)}, bf16[4,22,176]{2,1,0:T(8,128)(2,1)S(1)}, u32[]{:S(2)}, u32[]{:S(2)}) collective-permute-start(bf16[4,22,176]{2,1,0:T(8,128)(2,1)S(1)} %get-tuple-element.36), channel_id=1, source_target_pairs={{0,4},{2,6},{4,0},{6,2},{1,5},{3,7},{5,1},{7,3},{8,12},{10,14},{12... | collective-permute-start | bytes 92936 | tf_op jit(solution)/shard_map/ppermute | solution.py:315
  158.1 1.2 collective-permute-start.12
  159.3 0.0 collective-permute-done.10.refs_1_
  159.3 0.9 collective-permute-done.11.refs_2_
  160.2 1.5 collective-permute-done.12.refs_3_
  161.7 0.6 block_sums.3
  162.3 0.2 collective-permute-start.13
  162.4 2.1 %collective-permute-start.14 = (f32[22,176]{1,0:T(8,128)S(1)}, f32[22,176]{1,0:T(8,128)S(1)}, u32[]{:S(2)}, u32[]{:S(2)}) collective-permute-start(f32[22,176]{1,0:T(8,128)S(1)} %get-tuple-element.40), channel_id=1, source_target_pairs={{0,32},{16,48},{32,0},{48,16},{1,33},{17,49},{33,1},{49,17},{2,34}... | collective-permute-start | bytes 46472 | tf_op jit(solution)/shard_map/ppermute | solution.py:315
  164.6 1.3 collective-permute-start.15
  165.8 0.4 collective-permute-done.13.refs_1_
  166.2 0.4 collective-permute-done.14.refs_2_
  166.6 0.6 collective-permute-done.15.refs_3_
  167.2 0.6 pick_rows.1
  167.8 4.1 %collective-permute-start.16 = (f32[4,11,176]{2,1,0:T(8,128)S(1)}, f32[4,11,176]{2,1,0:T(8,128)S(1)}, u32[]{:S(2)}, u32[]{:S(2)}) collective-permute-start(f32[4,11,176]{2,1,0:T(8,128)S(1)} %get-tuple-element.43), channel_id=1, source_target_pairs={{0,1},{1,0},{2,3},{3,2},{4,5},{5,4},{6,7},{7,6},{8,9},{9,8},{10,11... | collective-permute-start | bytes 92936 | tf_op jit(solution)/shard_map/ppermute | solution.py:324
  171.9 0.9 collective-permute-done.16.theirs
  172.8 1.4 join_columns.1
  174.2 0.0 all-to-all-done.1.x_ref
  174.2 1.6 unpack_by_token.1
Async XLA Ops:
  68.5 21.3 %all-to-all-start.2 = ((bf16[32,2,24,256]{3,2,1,0:T(8,128)(2,1)}), bf16[32,2,24,256]{3,2,1,0:T(8,128)(2,1)S(1)}, u32[]{:S(2)}, u32[]{:S(2)}) async-start(bf16[32,2,24,256]{3,2,1,0:T(8,128)(2,1)} %bitcast.5), calls=%async_computation.2 | async-start | bytes 1572864 | tf_op jit(solution)/shard_map/all_to_all | solution.py:311
  89.8 84.4 %all-to-all-start.1 = ((bf16[16,3,88,256]{3,2,1,0:T(8,128)(2,1)}), bf16[16,3,88,256]{3,2,1,0:T(8,128)(2,1)S(1)}, u32[]{:S(2)}, u32[]{:S(2)}) async-start(bf16[16,3,88,256]{3,2,1,0:T(8,128)(2,1)} %spatial_backward.1), calls=%async_computation.1 | async-start | bytes 4325376 | tf_op jit(solution)/shard_map/all_to_all | solution.py:311
  96.0 19.1 %collective-permute-start = (bf16[4,64,1408]{2,1,0:T(8,128)(2,1)}, bf16[4,64,1408]{2,1,0:T(8,128)(2,1)}, u32[]{:S(2)}, u32[]{:S(2)}) collective-permute-start(bf16[4,64,1408]{2,1,0:T(8,128)(2,1)} %refs_0_.1), channel_id=1, source_target_pairs={{0,16},{16,32},{32,48},{48,0},{1,17},{17,33},{33,49},{49,1},{2,18}... | collective-permute-start | bytes 2162696 | tf_op jit(solution)/shard_map/ppermute | solution.py:315
  97.2 34.3 %collective-permute-start.1 = (bf16[4,64,1408]{2,1,0:T(8,128)(2,1)}, bf16[4,64,1408]{2,1,0:T(8,128)(2,1)}, u32[]{:S(2)}, u32[]{:S(2)}) collective-permute-start(bf16[4,64,1408]{2,1,0:T(8,128)(2,1)} %refs_0_.1), channel_id=1, source_target_pairs={{0,32},{16,48},{32,0},{48,16},{1,33},{17,49},{33,1},{49,17},{2,34}... | collective-permute-start | bytes 2162696 | tf_op jit(solution)/shard_map/ppermute | solution.py:315
  99.7 32.9 %collective-permute-start.2 = (bf16[4,64,1408]{2,1,0:T(8,128)(2,1)}, bf16[4,64,1408]{2,1,0:T(8,128)(2,1)}, u32[]{:S(2)}, u32[]{:S(2)}) collective-permute-start(bf16[4,64,1408]{2,1,0:T(8,128)(2,1)} %refs_0_.1), channel_id=1, source_target_pairs={{0,48},{16,0},{32,16},{48,32},{1,49},{17,1},{33,17},{49,33},{2,50}... | collective-permute-start | bytes 2162696 | tf_op jit(solution)/shard_map/ppermute | solution.py:315
  100.8 31.8 %collective-permute-start.3 = (bf16[4,64,1408]{2,1,0:T(8,128)(2,1)}, bf16[4,64,1408]{2,1,0:T(8,128)(2,1)}, u32[]{:S(2)}, u32[]{:S(2)}) collective-permute-start(bf16[4,64,1408]{2,1,0:T(8,128)(2,1)} %refs_0_.1), channel_id=1, source_target_pairs={{0,1},{1,0},{2,3},{3,2},{4,5},{5,4},{6,7},{7,6},{8,9},{9,8},{10,11... | collective-permute-start | bytes 2162696 | tf_op jit(solution)/shard_map/ppermute | solution.py:324
  115.1 17.5 %collective-permute-start.4 = (bf16[4,64,1408]{2,1,0:T(8,128)(2,1)}, bf16[4,64,1408]{2,1,0:T(8,128)(2,1)}, u32[]{:S(2)}, u32[]{:S(2)}) collective-permute-start(bf16[4,64,1408]{2,1,0:T(8,128)(2,1)} %collective-permute-done.refs_1_), channel_id=1, source_target_pairs={{0,1},{1,0},{2,3},{3,2},{4,5},{5,4},{6,7},{7,6},{8,9},{9,8},{10,11... | collective-permute-start | bytes 2162696 | tf_op jit(solution)/shard_map/ppermute | solution.py:324
  131.5 3.2 %collective-permute-start.5 = (bf16[4,64,1408]{2,1,0:T(8,128)(2,1)}, bf16[4,64,1408]{2,1,0:T(8,128)(2,1)}, u32[]{:S(2)}, u32[]{:S(2)}) collective-permute-start(bf16[4,64,1408]{2,1,0:T(8,128)(2,1)} %collective-permute-done.1.refs_2_), channel_id=1, source_target_pairs={{0,1},{1,0},{2,3},{3,2},{4,5},{5,4},{6,7},{7,6},{8,9},{9,8},{10,11... | collective-permute-start | bytes 2162696 | tf_op jit(solution)/shard_map/ppermute | solution.py:324
  132.6 3.2 %collective-permute-start.6 = (bf16[4,64,1408]{2,1,0:T(8,128)(2,1)}, bf16[4,64,1408]{2,1,0:T(8,128)(2,1)}, u32[]{:S(2)}, u32[]{:S(2)}) collective-permute-start(bf16[4,64,1408]{2,1,0:T(8,128)(2,1)} %collective-permute-done.2.refs_3_), channel_id=1, source_target_pairs={{0,1},{1,0},{2,3},{3,2},{4,5},{5,4},{6,7},{7,6},{8,9},{9,8},{10,11... | collective-permute-start | bytes 2162696 | tf_op jit(solution)/shard_map/ppermute | solution.py:324
  135.7 1.1 copy-start
  141.0 7.4 %collective-permute-start.7 = (bf16[4,4,22,176]{3,2,1,0:T(8,128)(2,1)S(1)}, bf16[4,4,22,176]{3,2,1,0:T(8,128)(2,1)S(1)}, u32[]{:S(2)}, u32[]{:S(2)}) collective-permute-start(bf16[4,4,22,176]{3,2,1,0:T(8,128)(2,1)S(1)} %get-tuple-element.31), channel_id=1, source_target_pairs={{0,64},{64,8},{8,72},{72,0},{1,65},{65,9},{9,73},{73,1},{2,66},{66... | collective-permute-start | bytes 371720 | tf_op jit(solution)/shard_map/ppermute | solution.py:320
  141.5 12.3 %collective-permute-start.8 = (bf16[4,4,22,176]{3,2,1,0:T(8,128)(2,1)S(1)}, bf16[4,4,22,176]{3,2,1,0:T(8,128)(2,1)S(1)}, u32[]{:S(2)}, u32[]{:S(2)}) collective-permute-start(bf16[4,4,22,176]{3,2,1,0:T(8,128)(2,1)S(1)} %get-tuple-element.32), channel_id=1, source_target_pairs={{0,8},{64,72},{8,0},{72,64},{1,9},{65,73},{9,1},{73,65},{2,10},{66... | collective-permute-start | bytes 371720 | tf_op jit(solution)/shard_map/ppermute | solution.py:320
  145.0 8.8 %collective-permute-start.9 = (bf16[4,4,22,176]{3,2,1,0:T(8,128)(2,1)S(1)}, bf16[4,4,22,176]{3,2,1,0:T(8,128)(2,1)S(1)}, u32[]{:S(2)}, u32[]{:S(2)}) collective-permute-start(bf16[4,4,22,176]{3,2,1,0:T(8,128)(2,1)S(1)} %get-tuple-element.33), channel_id=1, source_target_pairs={{0,72},{64,0},{8,64},{72,8},{1,73},{65,1},{9,65},{73,9},{2,74},{66... | collective-permute-start | bytes 371720 | tf_op jit(solution)/shard_map/ppermute | solution.py:320
  154.5 4.8 %collective-permute-start.10 = (bf16[4,22,176]{2,1,0:T(8,128)(2,1)S(1)}, bf16[4,22,176]{2,1,0:T(8,128)(2,1)S(1)}, u32[]{:S(2)}, u32[]{:S(2)}) collective-permute-start(bf16[4,22,176]{2,1,0:T(8,128)(2,1)S(1)} %get-tuple-element.35), channel_id=1, source_target_pairs={{0,2},{2,4},{4,6},{6,0},{1,3},{3,5},{5,7},{7,1},{8,10},{10,12},{12... | collective-permute-start | bytes 92936 | tf_op jit(solution)/shard_map/ppermute | solution.py:315
  155.8 4.5 %collective-permute-start.11 = (bf16[4,22,176]{2,1,0:T(8,128)(2,1)S(1)}, bf16[4,22,176]{2,1,0:T(8,128)(2,1)S(1)}, u32[]{:S(2)}, u32[]{:S(2)}) collective-permute-start(bf16[4,22,176]{2,1,0:T(8,128)(2,1)S(1)} %get-tuple-element.36), channel_id=1, source_target_pairs={{0,4},{2,6},{4,0},{6,2},{1,5},{3,7},{5,1},{7,3},{8,12},{10,14},{12... | collective-permute-start | bytes 92936 | tf_op jit(solution)/shard_map/ppermute | solution.py:315
  158.1 3.6 %collective-permute-start.12 = (bf16[4,22,176]{2,1,0:T(8,128)(2,1)S(1)}, bf16[4,22,176]{2,1,0:T(8,128)(2,1)S(1)}, u32[]{:S(2)}, u32[]{:S(2)}) collective-permute-start(bf16[4,22,176]{2,1,0:T(8,128)(2,1)S(1)} %get-tuple-element.37), channel_id=1, source_target_pairs={{0,6},{2,0},{4,2},{6,4},{1,7},{3,1},{5,3},{7,5},{8,14},{10,8},{12,... | collective-permute-start | bytes 92936 | tf_op jit(solution)/shard_map/ppermute | solution.py:315
  162.3 4.0 %collective-permute-start.13 = (f32[22,176]{1,0:T(8,128)S(1)}, f32[22,176]{1,0:T(8,128)S(1)}, u32[]{:S(2)}, u32[]{:S(2)}) collective-permute-start(f32[22,176]{1,0:T(8,128)S(1)} %get-tuple-element.39), channel_id=1, source_target_pairs={{0,16},{16,32},{32,48},{48,0},{1,17},{17,33},{33,49},{49,1},{2,18}... | collective-permute-start | bytes 46472 | tf_op jit(solution)/shard_map/ppermute | solution.py:315
  162.4 4.2 %collective-permute-start.14 = (f32[22,176]{1,0:T(8,128)S(1)}, f32[22,176]{1,0:T(8,128)S(1)}, u32[]{:S(2)}, u32[]{:S(2)}) collective-permute-start(f32[22,176]{1,0:T(8,128)S(1)} %get-tuple-element.40), channel_id=1, source_target_pairs={{0,32},{16,48},{32,0},{48,16},{1,33},{17,49},{33,1},{49,17},{2,34}... | collective-permute-start | bytes 46472 | tf_op jit(solution)/shard_map/ppermute | solution.py:315
  164.6 2.7 %collective-permute-start.15 = (f32[22,176]{1,0:T(8,128)S(1)}, f32[22,176]{1,0:T(8,128)S(1)}, u32[]{:S(2)}, u32[]{:S(2)}) collective-permute-start(f32[22,176]{1,0:T(8,128)S(1)} %get-tuple-element.41), channel_id=1, source_target_pairs={{0,48},{16,0},{32,16},{48,32},{1,49},{17,1},{33,17},{49,33},{2,50}... | collective-permute-start | bytes 46472 | tf_op jit(solution)/shard_map/ppermute | solution.py:315
  167.8 5.0 %collective-permute-start.16 = (f32[4,11,176]{2,1,0:T(8,128)S(1)}, f32[4,11,176]{2,1,0:T(8,128)S(1)}, u32[]{:S(2)}, u32[]{:S(2)}) collective-permute-start(f32[4,11,176]{2,1,0:T(8,128)S(1)} %get-tuple-element.43), channel_id=1, source_target_pairs={{0,1},{1,0},{2,3},{3,2},{4,5},{5,4},{6,7},{7,6},{8,9},{9,8},{10,11... | collective-permute-start | bytes 92936 | tf_op jit(solution)/shard_map/ppermute | solution.py:324

commit v4 on v3

--- a/solution.py
+++ b/solution.py
@@ -1,5 +1,3 @@
-import functools
-
 import jax
 import jax.numpy as jnp
 from jax import lax
@@ -128,7 +126,7 @@
         ],
         scratch_shapes=[pltpu.VMEM((2, HEAD_DIM, 1024), F32)],
         cost_estimate=pl.CostEstimate(flops=4 * 4 * 1024 * 1024 * 256, bytes_accessed=12_000_000, transcendentals=1 << 22),
-        compiler_params=pltpu.CompilerParams(vmem_limit_bytes=60 << 20),
+        compiler_params=pltpu.CompilerParams(vmem_limit_bytes=56 << 20),
         name="spatial_forward",
     )(x)
 
@@ -214,73 +212,56 @@
     )(place, *grads, att)
 
 
-def sums_kernel(coordinate, place_ref, *refs):
+def small(kernel, place, operands, shapes, scratch=()):
+    return pl.pallas_call(
+        kernel,
+        in_specs=[SM] + [VM] * len(operands),
+        out_specs=[VM] * len(shapes),
+        out_shape=shapes,
+        scratch_shapes=list(scratch),
+        cost_estimate=pl.CostEstimate(flops=1_000_000, bytes_accessed=2_000_000, transcendentals=0),
+        compiler_params=pltpu.CompilerParams(vmem_limit_bytes=8 << 20),
+    )(place, *operands)
+
+
+def sums_kernel(place_ref, *refs):
     parts, outs, total = refs[:4], refs[4:8], refs[8]
-    total[...] = sum(part[...].astype(F32) for part in parts[1:]) + parts[0][...]
+    for x in range(4):
+        for z in range(4):
+            total[z, x] = sum(part[x, z].astype(F32) for part in parts)
     for s, out in enumerate(outs):
-        out[...] = total[lax.rem(place_ref[coordinate] + s, 4)].astype(out.dtype)
-
-
-def block_sums(place, parts, coordinate, sent):
-    shape = parts[0].shape
-    return pl.pallas_call(
-        functools.partial(sums_kernel, coordinate),
-        in_specs=[SM] + [VM] * 4,
-        out_specs=[VM] * 4,
-        out_shape=[jax.ShapeDtypeStruct(shape[1:], F32)] + [jax.ShapeDtypeStruct(shape[1:], sent)] * 3,
-        scratch_shapes=[pltpu.VMEM(shape, F32)],
-        cost_estimate=pl.CostEstimate(flops=1_000_000, bytes_accessed=3_000_000, transcendentals=0),
-        compiler_params=pltpu.CompilerParams(vmem_limit_bytes=8 << 20),
-        name="block_sums",
-    )(place, *parts)
+        out[...] = total[lax.rem(place_ref[1] + s, 4)]
 
 
 def pick_kernel(place_ref, *refs):
     parts, mine, theirs = refs[:4], refs[4], refs[5]
     core, z = place_ref[0], place_ref[1]
     for r, part in enumerate(parts):
-        both = part[...]
-        first, second = both[:11], both[11:]
         source = lax.rem(z + 4 - r, 4)
-        mine[source] = jnp.where(core == 0, first, second)
-        theirs[source] = jnp.where(core == 0, second, first)
-
-
-def pick(place, parts):
-    shape = jax.ShapeDtypeStruct((4, 11, 8 * QUARTER), F32)
-    return pl.pallas_call(
-        pick_kernel,
-        in_specs=[SM] + [VM] * 4,
-        out_specs=[VM] * 2,
-        out_shape=[shape] * 2,
-        cost_estimate=pl.CostEstimate(flops=1_000, bytes_accessed=200_000, transcendentals=0),
-        compiler_params=pltpu.CompilerParams(vmem_limit_bytes=4 << 20),
-        name="pick_rows",
-    )(place, *parts)
-
-
-def join_kernel(place_ref, mine, theirs, out, scratch):
-    core = place_ref[0]
+        for x in range(4):
+            both = part[x]
+            first, second = both[:11], both[11:]
+            mine[source, x] = jnp.where(core == 0, first, second)
+            theirs[source, x] = jnp.where(core == 0, second, first)
+
+
+def join_kernel(place_ref, mine, theirs, *refs):
+    outs, scratch, joined = refs[:4], refs[4], refs[5]
+    core, place = place_ref[0], place_ref[3]
     scratch[core] = mine[...]
     scratch[1 - core] = theirs[...]
     for head in range(HEADS):
         i = head % 8
         for z in range(4):
             at = head * HEAD_DIM + z * QUARTER
-            out[:, at : at + QUARTER] = scratch[head // 8, z][:, QUARTER * i : QUARTER * (i + 1)]
-
-
-def join(place, mine, theirs):
-    return pl.pallas_call(
-        join_kernel,
-        in_specs=[SM, VM, VM],
-        out_specs=VM,
-        out_shape=jax.ShapeDtypeStruct((11, HEADS * HEAD_DIM), F32),
-        scratch_shapes=[pltpu.VMEM((2, 4, 11, 8 * QUARTER), F32)],
-        cost_estimate=pl.CostEstimate(flops=1_000, bytes_accessed=200_000, transcendentals=0),
-        compiler_params=pltpu.CompilerParams(vmem_limit_bytes=4 << 20),
-        name="join_columns",
-    )(place, mine, theirs)
+            for x in range(4):
+                joined[x, :, at : at + QUARTER] = scratch[head // 8, z, x][:, QUARTER * i : QUARTER * (i + 1)]
+    for s, out in enumerate(outs):
+        out[...] = joined[lax.rem(place + s, 4)].astype(out.dtype)
+
+
+def final_kernel(place_ref, *refs):
+    refs[4][...] = sum(part[...].astype(F32) for part in refs[:4])
 
 
 def unpack_kernel(x_ref, q_ref, k_ref, v_ref, t_ref):
@@ -333,16 +314,26 @@
     attended, raised, per_row = forward(x)
     att = exchange(attended.reshape(32, 2, PADDED, 256), ("z", "y_hi", "x"))
     grads = backward(x, raised, per_row)
-    home = exchange(grads, PATCH)
     own, *sent = weight_terms(place, gathered, att)
     parts = [own] + [along_y(part, s) for s, part in enumerate(sent, 1)]
-    own, *sent = block_sums(place, parts, 3, BF16)
+    home = exchange(grads, PATCH)
+    columns, array = 8 * QUARTER, jax.ShapeDtypeStruct
+    own, *sent = small(
+        sums_kernel, place, parts, [array((4, QUARTER, columns), F32)] * 4, [pltpu.VMEM((4, 4, QUARTER, columns), F32)]
+    )
+    parts = [own] + [along(part, "z", s) for s, part in enumerate(sent, 1)]
+    mine, theirs = small(pick_kernel, place, parts, [array((4, 4, 11, columns), F32)] * 2)
+    theirs = other_core(theirs)
+    features = grad_out.shape[-1]
+    own, *sent = small(
+        join_kernel,
+        place,
+        (mine, theirs),
+        [array((11, features), F32)] + [array((11, features), BF16)] * 3,
+        [pltpu.VMEM((2, 4, 4, 11, columns), F32), pltpu.VMEM((4, 11, features), F32)],
+    )
     parts = [own] + [along(part, "x", s) for s, part in enumerate(sent, 1)]
-    own, *sent = block_sums(place, parts, 1, F32)
-    parts = [own] + [along(part, "z", s) for s, part in enumerate(sent, 1)]
-    mine, theirs = pick(place, parts)
-    theirs = other_core(theirs)
-    grad_weight = join(place, mine, theirs)
+    (grad_weight,) = small(final_kernel, place, parts, [array((11, features), F32)])
     outs = unpack(home, query_rows.shape)
     return (*outs, grad_weight)
 

time: 176 us -> 177 us (level)
  waiting for transfers between devices: 45.3 us -> 47.1 us
  transfers between devices with their start and end apart: 19 -> 19, of which waited for: 13 -> 12; matrix products, arithmetic and copies ran while one was open for 0% -> 0% of each run, Pallas kernels for 12% -> 12%
where the time goes in v4:
time: 177 us; the launch traced here: 176 us
  waiting for transfers between devices  47.1 us (27%)
  Pallas kernels  45.6 us (26%)
  blocking collectives  45.3 us (26%)
  starting transfers between devices  36.4 us (21%)
    all_to_all x1, blocking collectives, exchange(): return lax.all_to_all(array, axes, split_axis=0, concat_axis=0, tiled=True)  45.3 us
    ppermute x9, waiting for transfers between devices, along(): return lax.ppermute(array, axis, [(i, (i + step) % 4) for i in range(4)])  34 us
    pallas_call x1, Pallas kernels, forward(): pl.pallas_call(forward_kernel, grid=(2,), in_specs=[PAIR], out_specs=[pl....  15.6 us
    pallas_call x1, Pallas kernels, backward(): pl.pallas_call(backward_kernel, grid=(2,), in_specs=[PAIR, RAISED, PER_RO...  13.6 us
    ppermute x9, starting transfers between devices, along(): return lax.ppermute(array, axis, [(i, (i + step) % 4) for i in range(4)])  13.1 us
    all_to_all x2, starting transfers between devices, exchange(): return lax.all_to_all(array, axes, split_axis=0, concat_axis=0, tiled=True)  12.8 us
    ppermute x3, waiting for transfers between devices, along_y(): lax.ppermute(array, ('y_lo', 'y_hi'), [(place(y), place((y + step) % 4))...  7.76 us
    pallas_call x1, Pallas kernels, pack(): pl.pallas_call(pack_kernel, in_specs=[pl.BlockSpec(memory_space=pltpu.VME...  6.9 us
  transfers between devices with their start and end apart: 19, of which 12 were waited for; matrix products, arithmetic and copies ran while one was open for 0% of the time, Pallas kernels for 12%

profile of v4, /device:TPU:1, one launch (start us, length us, event | category | flops | bytes accessed | tf_op | source)
XLA Modules:
  0.0 176.3 jit_solution(6066929284856928154)
XLA Ops:
  0.6 6.9 %pack_by_head.1 = bf16[16,4,88,256]{3,2,1,0:T(8,128)(2,1)} custom-call(bf16[4,64,1408]{2,1,0:T(8,128)(2,1)} %q_ref.1, bf16[4,64,1408]{2,1,0:T(8,128)(2,1)} %k_ref.1, bf16[4,64,1408]{2,1,0:T(8,128)(2,1)} %v_ref.1, bf16[4,64,1408]{2,1,0:T(8,128)(2,1)} %refs_0_.1, bf16[1408,1408]{1,0:T(8,128)(2,1)} %w_hbm.1), custom_call_target="tpu_custom_call" | custom-call | flops 1015021568 | bytes 10000000 | tf_op jit(solution)/shard_map/pack_by_head/pallas_call | solution.py:72
  7.5 45.3 %all_to_all.15.x_ref = bf16[16,4,88,256]{3,2,1,0:T(8,128)(2,1)} all-to-all(bf16[16,4,88,256]{3,2,1,0:T(8,128)(2,1)} %pack_by_head.1), channel_id=1, replica_groups=mesh['y_lo'=2,'z'=4,'y_hi'=2,'x'=4,'core'=2] {'y_hi','x','core'}, dimensions={0} | all-to-all | bytes 5767168 | tf_op jit(solution)/shard_map/all_to_all | solution.py:292
  52.9 15.6 %spatial_forward.1 = (bf16[4,8,2,24,256]{4,3,2,1,0:T(8,128)(2,1)}, bf16[4,1024,1024]{2,1,0:T(8,128)(2,1)}, f32[4,8,1024]{2,1,0:T(8,128)}) custom-call(bf16[16,4,88,256]{3,2,1,0:T(8,128)(2,1)} %all_to_all.15.x_ref), custom_call_target="tpu_custom_call" | custom-call | flops 4294967296 | bytes 12000000 | tf_op jit(solution)/shard_map/spatial_forward/pallas_call | solution.py:117
  68.5 6.6 %all-to-all-start.2 = ((bf16[32,2,24,256]{3,2,1,0:T(8,128)(2,1)}), bf16[32,2,24,256]{3,2,1,0:T(8,128)(2,1)S(1)}, u32[]{:S(2)}, u32[]{:S(2)}) async-start(bf16[32,2,24,256]{3,2,1,0:T(8,128)(2,1)} %bitcast.5), calls=%async_computation.2 | async-start | bytes 1572864 | tf_op jit(solution)/shard_map/all_to_all | solution.py:292
  75.0 13.6 %spatial_backward.1 = bf16[16,3,88,256]{3,2,1,0:T(8,128)(2,1)} custom-call(bf16[16,4,88,256]{3,2,1,0:T(8,128)(2,1)} %all_to_all.15.x_ref, bf16[4,1024,1024]{2,1,0:T(8,128)(2,1)} %get-tuple-element.24.e_ref, f32[4,8,1024]{2,1,0:T(8,128)} %get-tuple-element.25.row_ref), custom_call_target="tpu_custom_call" | custom-call | flops 8589934592 | bytes 14000000 | tf_op jit(solution)/shard_map/spatial_backward/pallas_call | solution.py:159
  88.7 1.1 all-to-all-done.2.refs_8_
  89.8 6.3 %all-to-all-start.1 = ((bf16[16,3,88,256]{3,2,1,0:T(8,128)(2,1)}), bf16[16,3,88,256]{3,2,1,0:T(8,128)(2,1)S(1)}, u32[]{:S(2)}, u32[]{:S(2)}) async-start(bf16[16,3,88,256]{3,2,1,0:T(8,128)(2,1)} %spatial_backward.1), calls=%async_computation.1 | async-start | bytes 4325376 | tf_op jit(solution)/shard_map/all_to_all | solution.py:292
  96.0 1.2 collective-permute-start
  97.2 2.5 %collective-permute-start.1 = (bf16[4,64,1408]{2,1,0:T(8,128)(2,1)}, bf16[4,64,1408]{2,1,0:T(8,128)(2,1)}, u32[]{:S(2)}, u32[]{:S(2)}) collective-permute-start(bf16[4,64,1408]{2,1,0:T(8,128)(2,1)} %refs_0_.1), channel_id=1, source_target_pairs={{0,32},{16,48},{32,0},{48,16},{1,33},{17,49},{33,1},{49,17},{2,34}... | collective-permute-start | bytes 2162696 | tf_op jit(solution)/shard_map/ppermute | solution.py:296
  99.7 1.1 collective-permute-start.2
  100.8 1.0 collective-permute-start.3
  101.8 13.3 %collective-permute-done.refs_1_ = bf16[4,64,1408]{2,1,0:T(8,128)(2,1)} collective-permute-done((bf16[4,64,1408]{2,1,0:T(8,128)(2,1)}, bf16[4,64,1408]{2,1,0:T(8,128)(2,1)}, u32[]{:S(2)}, u32[]{:S(2)}) %collective-permute-start) | collective-permute-done | bytes 720928 | tf_op jit(solution)/shard_map/ppermute | solution.py:296
  115.1 1.0 collective-permute-start.4
  116.1 15.4 %collective-permute-done.1.refs_2_ = bf16[4,64,1408]{2,1,0:T(8,128)(2,1)} collective-permute-done((bf16[4,64,1408]{2,1,0:T(8,128)(2,1)}, bf16[4,64,1408]{2,1,0:T(8,128)(2,1)}, u32[]{:S(2)}, u32[]{:S(2)}) %collective-permute-start.1) | collective-permute-done | bytes 720928 | tf_op jit(solution)/shard_map/ppermute | solution.py:296
  131.5 1.0 collective-permute-start.5
  132.6 0.0 collective-permute-done.2.refs_3_
  132.6 0.0 collective-permute-start.6
  132.6 0.1 pad_add_fusion.place_ref
  132.6 0.0 collective-permute-done.3.refs_4_
  132.6 0.0 collective-permute-done.4.refs_5_
  132.6 2.1 %collective-permute-done.5.refs_6_ = bf16[4,64,1408]{2,1,0:T(8,128)(2,1)} collective-permute-done((bf16[4,64,1408]{2,1,0:T(8,128)(2,1)}, bf16[4,64,1408]{2,1,0:T(8,128)(2,1)}, u32[]{:S(2)}, u32[]{:S(2)}) %collective-permute-start.5) | collective-permute-done | bytes 720928 | tf_op jit(solution)/shard_map/ppermute | solution.py:305
  134.7 1.0 collective-permute-done.6.refs_7_
  135.7 0.0 copy-start
  135.7 1.1 copy-done
  136.9 4.2 %weight_terms.1 = (f32[4,4,22,176]{3,2,1,0:T(8,128)S(1)}, bf16[4,4,22,176]{3,2,1,0:T(8,128)(2,1)S(1)}, bf16[4,4,22,176]{3,2,1,0:T(8,128)(2,1)S(1)}, bf16[4,4,22,176]{3,2,1,0:T(8,128)(2,1)S(1)}) custom-call(s32[4]{0:T(128)S(1)} %pad_add_fusion.place_ref, bf16[4,64,1408]{2,1,0:T(8,128)(2,1)S(1)} %copy-done, bf16[4,64,1408]{2,1,0:T(8,128)(2,1)} %collective-permute-done.refs_1_, ...), custom_call_target="tpu_custom_call" | custom-call | flops 1015021568 | bytes 8000000 | tf_op jit(solution)/shard_map/weight_terms/pallas_call | solution.py:203
  141.0 0.5 collective-permute-start.7
  141.5 3.5 %collective-permute-start.8 = (bf16[4,4,22,176]{3,2,1,0:T(8,128)(2,1)S(1)}, bf16[4,4,22,176]{3,2,1,0:T(8,128)(2,1)S(1)}, u32[]{:S(2)}, u32[]{:S(2)}) collective-permute-start(bf16[4,4,22,176]{3,2,1,0:T(8,128)(2,1)S(1)} %get-tuple-element.32), channel_id=1, source_target_pairs={{0,8},{64,72},{8,0},{72,64},{1,9},{65,73},{9,1},{73,65},{2,10},{66... | collective-permute-start | bytes 371720 | tf_op jit(solution)/shard_map/ppermute | solution.py:301
  145.0 1.1 collective-permute-start.9
  146.0 2.4 %collective-permute-done.7.refs_1_ = bf16[4,4,22,176]{3,2,1,0:T(8,128)(2,1)S(1)} collective-permute-done((bf16[4,4,22,176]{3,2,1,0:T(8,128)(2,1)S(1)}, bf16[4,4,22,176]{3,2,1,0:T(8,128)(2,1)S(1)}, u32[]{:S(2)}, u32[]{:S(2)}) %collective-permute-start.7) | collective-permute-done | bytes 123936 | tf_op jit(solution)/shard_map/ppermute | solution.py:301
  148.4 5.4 %collective-permute-done.8.refs_2_ = bf16[4,4,22,176]{3,2,1,0:T(8,128)(2,1)S(1)} collective-permute-done((bf16[4,4,22,176]{3,2,1,0:T(8,128)(2,1)S(1)}, bf16[4,4,22,176]{3,2,1,0:T(8,128)(2,1)S(1)}, u32[]{:S(2)}, u32[]{:S(2)}) %collective-permute-start.8) | collective-permute-done | bytes 123936 | tf_op jit(solution)/shard_map/ppermute | solution.py:301
  153.8 0.0 collective-permute-done.9.refs_3_
  153.8 0.6 shard_map.84
  154.4 0.1 collective-permute-start.10
  154.6 2.1 %collective-permute-start.11 = (f32[4,22,176]{2,1,0:T(8,128)S(1)}, f32[4,22,176]{2,1,0:T(8,128)S(1)}, u32[]{:S(2)}, u32[]{:S(2)}) collective-permute-start(f32[4,22,176]{2,1,0:T(8,128)S(1)} %get-tuple-element.36), channel_id=1, source_target_pairs={{0,32},{16,48},{32,0},{48,16},{1,33},{17,49},{33,1},{49,17},{2,34}... | collective-permute-start | bytes 185864 | tf_op jit(solution)/shard_map/ppermute | solution.py:296
  156.7 1.2 collective-permute-start.12
  157.9 2.9 %collective-permute-done.10.refs_1_ = f32[4,22,176]{2,1,0:T(8,128)S(1)} collective-permute-done((f32[4,22,176]{2,1,0:T(8,128)S(1)}, f32[4,22,176]{2,1,0:T(8,128)S(1)}, u32[]{:S(2)}, u32[]{:S(2)}) %collective-permute-start.10) | collective-permute-done | bytes 61984 | tf_op jit(solution)/shard_map/ppermute | solution.py:296
  160.8 0.0 collective-permute-done.11.refs_2_
  160.8 0.5 collective-permute-done.12.refs_3_
  161.2 0.6 shard_map.85
  161.9 2.4 %collective-permute-start.13 = (f32[4,4,11,176]{3,2,1,0:T(8,128)S(1)}, f32[4,4,11,176]{3,2,1,0:T(8,128)S(1)}, u32[]{:S(2)}, u32[]{:S(2)}) collective-permute-start(f32[4,4,11,176]{3,2,1,0:T(8,128)S(1)} %get-tuple-element.39), channel_id=1, source_target_pairs={{0,1},{1,0},{2,3},{3,2},{4,5},{5,4},{6,7},{7,6},{8,9},{9,8},{10,11... | collective-permute-start | bytes 371720 | tf_op jit(solution)/shard_map/ppermute | solution.py:305
  164.3 1.2 collective-permute-done.13.theirs
  165.5 1.3 shard_map.86
  166.7 1.3 collective-permute-start.14
  168.0 2.4 %collective-permute-start.15 = (bf16[11,1408]{1,0:T(8,128)(2,1)S(1)}, bf16[11,1408]{1,0:T(8,128)(2,1)S(1)}, u32[]{:S(2)}, u32[]{:S(2)}) collective-permute-start(bf16[11,1408]{1,0:T(8,128)(2,1)S(1)} %get-tuple-element.42), channel_id=1, source_target_pairs={{0,4},{2,6},{4,0},{6,2},{1,5},{3,7},{5,1},{7,3},{8,12},{10,14},{12... | collective-permute-start | bytes 92936 | tf_op jit(solution)/shard_map/ppermute | solution.py:296
  170.4 1.2 collective-permute-start.16
  171.6 0.0 collective-permute-done.14.refs_1_
  171.6 1.1 collective-permute-done.15.refs_2_
  172.6 0.9 collective-permute-done.16.refs_3_
  173.6 1.2 shard_map.87
  174.8 0.0 all-to-all-done.1.x_ref
  174.8 1.6 unpack_by_token.1
Async XLA Ops:
  68.5 21.3 %all-to-all-start.2 = ((bf16[32,2,24,256]{3,2,1,0:T(8,128)(2,1)}), bf16[32,2,24,256]{3,2,1,0:T(8,128)(2,1)S(1)}, u32[]{:S(2)}, u32[]{:S(2)}) async-start(bf16[32,2,24,256]{3,2,1,0:T(8,128)(2,1)} %bitcast.5), calls=%async_computation.2 | async-start | bytes 1572864 | tf_op jit(solution)/shard_map/all_to_all | solution.py:292
  89.8 85.0 %all-to-all-start.1 = ((bf16[16,3,88,256]{3,2,1,0:T(8,128)(2,1)}), bf16[16,3,88,256]{3,2,1,0:T(8,128)(2,1)S(1)}, u32[]{:S(2)}, u32[]{:S(2)}) async-start(bf16[16,3,88,256]{3,2,1,0:T(8,128)(2,1)} %spatial_backward.1), calls=%async_computation.1 | async-start | bytes 4325376 | tf_op jit(solution)/shard_map/all_to_all | solution.py:292
  96.0 19.1 %collective-permute-start = (bf16[4,64,1408]{2,1,0:T(8,128)(2,1)}, bf16[4,64,1408]{2,1,0:T(8,128)(2,1)}, u32[]{:S(2)}, u32[]{:S(2)}) collective-permute-start(bf16[4,64,1408]{2,1,0:T(8,128)(2,1)} %refs_0_.1), channel_id=1, source_target_pairs={{0,16},{16,32},{32,48},{48,0},{1,17},{17,33},{33,49},{49,1},{2,18}... | collective-permute-start | bytes 2162696 | tf_op jit(solution)/shard_map/ppermute | solution.py:296
  97.2 34.3 %collective-permute-start.1 = (bf16[4,64,1408]{2,1,0:T(8,128)(2,1)}, bf16[4,64,1408]{2,1,0:T(8,128)(2,1)}, u32[]{:S(2)}, u32[]{:S(2)}) collective-permute-start(bf16[4,64,1408]{2,1,0:T(8,128)(2,1)} %refs_0_.1), channel_id=1, source_target_pairs={{0,32},{16,48},{32,0},{48,16},{1,33},{17,49},{33,1},{49,17},{2,34}... | collective-permute-start | bytes 2162696 | tf_op jit(solution)/shard_map/ppermute | solution.py:296
  99.7 32.9 %collective-permute-start.2 = (bf16[4,64,1408]{2,1,0:T(8,128)(2,1)}, bf16[4,64,1408]{2,1,0:T(8,128)(2,1)}, u32[]{:S(2)}, u32[]{:S(2)}) collective-permute-start(bf16[4,64,1408]{2,1,0:T(8,128)(2,1)} %refs_0_.1), channel_id=1, source_target_pairs={{0,48},{16,0},{32,16},{48,32},{1,49},{17,1},{33,17},{49,33},{2,50}... | collective-permute-start | bytes 2162696 | tf_op jit(solution)/shard_map/ppermute | solution.py:296
  100.8 31.8 %collective-permute-start.3 = (bf16[4,64,1408]{2,1,0:T(8,128)(2,1)}, bf16[4,64,1408]{2,1,0:T(8,128)(2,1)}, u32[]{:S(2)}, u32[]{:S(2)}) collective-permute-start(bf16[4,64,1408]{2,1,0:T(8,128)(2,1)} %refs_0_.1), channel_id=1, source_target_pairs={{0,1},{1,0},{2,3},{3,2},{4,5},{5,4},{6,7},{7,6},{8,9},{9,8},{10,11... | collective-permute-start | bytes 2162696 | tf_op jit(solution)/shard_map/ppermute | solution.py:305
  115.1 17.5 %collective-permute-start.4 = (bf16[4,64,1408]{2,1,0:T(8,128)(2,1)}, bf16[4,64,1408]{2,1,0:T(8,128)(2,1)}, u32[]{:S(2)}, u32[]{:S(2)}) collective-permute-start(bf16[4,64,1408]{2,1,0:T(8,128)(2,1)} %collective-permute-done.refs_1_), channel_id=1, source_target_pairs={{0,1},{1,0},{2,3},{3,2},{4,5},{5,4},{6,7},{7,6},{8,9},{9,8},{10,11... | collective-permute-start | bytes 2162696 | tf_op jit(solution)/shard_map/ppermute | solution.py:305
  131.5 3.2 %collective-permute-start.5 = (bf16[4,64,1408]{2,1,0:T(8,128)(2,1)}, bf16[4,64,1408]{2,1,0:T(8,128)(2,1)}, u32[]{:S(2)}, u32[]{:S(2)}) collective-permute-start(bf16[4,64,1408]{2,1,0:T(8,128)(2,1)} %collective-permute-done.1.refs_2_), channel_id=1, source_target_pairs={{0,1},{1,0},{2,3},{3,2},{4,5},{5,4},{6,7},{7,6},{8,9},{9,8},{10,11... | collective-permute-start | bytes 2162696 | tf_op jit(solution)/shard_map/ppermute | solution.py:305
  132.6 3.2 %collective-permute-start.6 = (bf16[4,64,1408]{2,1,0:T(8,128)(2,1)}, bf16[4,64,1408]{2,1,0:T(8,128)(2,1)}, u32[]{:S(2)}, u32[]{:S(2)}) collective-permute-start(bf16[4,64,1408]{2,1,0:T(8,128)(2,1)} %collective-permute-done.2.refs_3_), channel_id=1, source_target_pairs={{0,1},{1,0},{2,3},{3,2},{4,5},{5,4},{6,7},{7,6},{8,9},{9,8},{10,11... | collective-permute-start | bytes 2162696 | tf_op jit(solution)/shard_map/ppermute | solution.py:305
  135.7 1.1 copy-start
  141.0 7.4 %collective-permute-start.7 = (bf16[4,4,22,176]{3,2,1,0:T(8,128)(2,1)S(1)}, bf16[4,4,22,176]{3,2,1,0:T(8,128)(2,1)S(1)}, u32[]{:S(2)}, u32[]{:S(2)}) collective-permute-start(bf16[4,4,22,176]{3,2,1,0:T(8,128)(2,1)S(1)} %get-tuple-element.31), channel_id=1, source_target_pairs={{0,64},{64,8},{8,72},{72,0},{1,65},{65,9},{9,73},{73,1},{2,66},{66... | collective-permute-start | bytes 371720 | tf_op jit(solution)/shard_map/ppermute | solution.py:301
  141.5 12.3 %collective-permute-start.8 = (bf16[4,4,22,176]{3,2,1,0:T(8,128)(2,1)S(1)}, bf16[4,4,22,176]{3,2,1,0:T(8,128)(2,1)S(1)}, u32[]{:S(2)}, u32[]{:S(2)}) collective-permute-start(bf16[4,4,22,176]{3,2,1,0:T(8,128)(2,1)S(1)} %get-tuple-element.32), channel_id=1, source_target_pairs={{0,8},{64,72},{8,0},{72,64},{1,9},{65,73},{9,1},{73,65},{2,10},{66... | collective-permute-start | bytes 371720 | tf_op jit(solution)/shard_map/ppermute | solution.py:301
  145.0 8.8 %collective-permute-start.9 = (bf16[4,4,22,176]{3,2,1,0:T(8,128)(2,1)S(1)}, bf16[4,4,22,176]{3,2,1,0:T(8,128)(2,1)S(1)}, u32[]{:S(2)}, u32[]{:S(2)}) collective-permute-start(bf16[4,4,22,176]{3,2,1,0:T(8,128)(2,1)S(1)} %get-tuple-element.33), channel_id=1, source_target_pairs={{0,72},{64,0},{8,64},{72,8},{1,73},{65,1},{9,65},{73,9},{2,74},{66... | collective-permute-start | bytes 371720 | tf_op jit(solution)/shard_map/ppermute | solution.py:301
  154.4 6.3 %collective-permute-start.10 = (f32[4,22,176]{2,1,0:T(8,128)S(1)}, f32[4,22,176]{2,1,0:T(8,128)S(1)}, u32[]{:S(2)}, u32[]{:S(2)}) collective-permute-start(f32[4,22,176]{2,1,0:T(8,128)S(1)} %get-tuple-element.35), channel_id=1, source_target_pairs={{0,16},{16,32},{32,48},{48,0},{1,17},{17,33},{33,49},{49,1},{2,18}... | collective-permute-start | bytes 185864 | tf_op jit(solution)/shard_map/ppermute | solution.py:296
  154.6 6.2 %collective-permute-start.11 = (f32[4,22,176]{2,1,0:T(8,128)S(1)}, f32[4,22,176]{2,1,0:T(8,128)S(1)}, u32[]{:S(2)}, u32[]{:S(2)}) collective-permute-start(f32[4,22,176]{2,1,0:T(8,128)S(1)} %get-tuple-element.36), channel_id=1, source_target_pairs={{0,32},{16,48},{32,0},{48,16},{1,33},{17,49},{33,1},{49,17},{2,34}... | collective-permute-start | bytes 185864 | tf_op jit(solution)/shard_map/ppermute | solution.py:296
  156.7 4.6 %collective-permute-start.12 = (f32[4,22,176]{2,1,0:T(8,128)S(1)}, f32[4,22,176]{2,1,0:T(8,128)S(1)}, u32[]{:S(2)}, u32[]{:S(2)}) collective-permute-start(f32[4,22,176]{2,1,0:T(8,128)S(1)} %get-tuple-element.37), channel_id=1, source_target_pairs={{0,48},{16,0},{32,16},{48,32},{1,49},{17,1},{33,17},{49,33},{2,50}... | collective-permute-start | bytes 185864 | tf_op jit(solution)/shard_map/ppermute | solution.py:296
  161.9 3.6 %collective-permute-start.13 = (f32[4,4,11,176]{3,2,1,0:T(8,128)S(1)}, f32[4,4,11,176]{3,2,1,0:T(8,128)S(1)}, u32[]{:S(2)}, u32[]{:S(2)}) collective-permute-start(f32[4,4,11,176]{3,2,1,0:T(8,128)S(1)} %get-tuple-element.39), channel_id=1, source_target_pairs={{0,1},{1,0},{2,3},{3,2},{4,5},{5,4},{6,7},{7,6},{8,9},{9,8},{10,11... | collective-permute-start | bytes 371720 | tf_op jit(solution)/shard_map/ppermute | solution.py:305
  166.7 4.8 %collective-permute-start.14 = (bf16[11,1408]{1,0:T(8,128)(2,1)S(1)}, bf16[11,1408]{1,0:T(8,128)(2,1)S(1)}, u32[]{:S(2)}, u32[]{:S(2)}) collective-permute-start(bf16[11,1408]{1,0:T(8,128)(2,1)S(1)} %get-tuple-element.41), channel_id=1, source_target_pairs={{0,2},{2,4},{4,6},{6,0},{1,3},{3,5},{5,7},{7,1},{8,10},{10,12},{12... | collective-permute-start | bytes 92936 | tf_op jit(solution)/shard_map/ppermute | solution.py:296
  168.0 4.6 %collective-permute-start.15 = (bf16[11,1408]{1,0:T(8,128)(2,1)S(1)}, bf16[11,1408]{1,0:T(8,128)(2,1)S(1)}, u32[]{:S(2)}, u32[]{:S(2)}) collective-permute-start(bf16[11,1408]{1,0:T(8,128)(2,1)S(1)} %get-tuple-element.42), channel_id=1, source_target_pairs={{0,4},{2,6},{4,0},{6,2},{1,5},{3,7},{5,1},{7,3},{8,12},{10,14},{12... | collective-permute-start | bytes 92936 | tf_op jit(solution)/shard_map/ppermute | solution.py:296
  170.4 3.2 %collective-permute-start.16 = (bf16[11,1408]{1,0:T(8,128)(2,1)S(1)}, bf16[11,1408]{1,0:T(8,128)(2,1)S(1)}, u32[]{:S(2)}, u32[]{:S(2)}) collective-permute-start(bf16[11,1408]{1,0:T(8,128)(2,1)S(1)} %get-tuple-element.43), channel_id=1, source_target_pairs={{0,6},{2,0},{4,2},{6,4},{1,7},{3,1},{5,3},{7,5},{8,14},{10,8},{12,... | collective-permute-start | bytes 92936 | tf_op jit(solution)/shard_map/ppermute | solution.py:296

commit v5 on v4

--- a/solution.py
+++ b/solution.py
@@ -47,34 +47,51 @@
         ref[s + 8, n] = jnp.where(low, turned(a), b).astype(BF16)
 
 
-def pack_kernel(q_ref, k_ref, v_ref, g_ref, w_hbm, out_ref, w_ref, sem):
-    fetch = pltpu.make_async_copy(w_hbm, w_ref, sem)
-    fetch.start()
+def pack_kernel(*refs):
+    ins, w_hbm, out_hbm, (in_ref, w_ref, out_ref, in_sem, w_sem, out_sem) = refs[:4], refs[4], refs[5], refs[6:]
+    weight_load = pltpu.make_async_copy(w_hbm, w_ref, w_sem)
+    loads = [pltpu.make_async_copy(ref, in_ref.at[n], in_sem.at[n]) for n, ref in enumerate(ins)]
+    stores = [pltpu.make_async_copy(out_ref.at[n], out_hbm.at[:, n], out_sem.at[n]) for n in range(4)]
+    for copy in (weight_load, *loads):
+        copy.start()
+
+    def rows_of(n):
+        loads[n].wait()
+        return in_ref[n].reshape(-1, in_ref.shape[-1])
 
     def place(n, rows):
         turned_rows = rows.T
         for slot in range(HEADS):
             at = HEAD_DIM * head_of(slot)
-            out_ref[slot, n] = turned_rows[at : at + HEAD_DIM].astype(BF16)
-
-    features = q_ref.shape[-1]
-    for n, ref in enumerate((q_ref, k_ref, v_ref)):
-        place(n, ref[...].reshape(-1, features))
-    fetch.wait()
-    place(
-        3,
-        jnp.dot(g_ref[...].reshape(-1, features), w_ref[...], preferred_element_type=F32).astype(BF16),
-    )
+            out_ref[n, slot] = turned_rows[at : at + HEAD_DIM]
+        stores[n].start()
+
+    for n in range(3):
+        place(n, rows_of(n))
+    upstream = rows_of(3)
+    weight_load.wait()
+    place(3, jnp.dot(upstream, w_ref[...], preferred_element_type=F32).astype(BF16))
+    for copy in stores:
+        copy.wait()
 
 
 def pack(query, key, value, upstream, weight):
     tokens = query.shape[0] * query.shape[1]
+    hbm = pl.BlockSpec(memory_space=pl.ANY)
+    dma = pltpu.SemaphoreType.DMA
     return pl.pallas_call(
         pack_kernel,
-        in_specs=[pl.BlockSpec(memory_space=pltpu.VMEM)] * 4 + [pl.BlockSpec(memory_space=pl.ANY)],
-        out_specs=pl.BlockSpec(memory_space=pltpu.VMEM),
+        in_specs=[hbm] * 5,
+        out_specs=hbm,
         out_shape=jax.ShapeDtypeStruct((HEADS, 4, HEAD_DIM, tokens), BF16),
-        scratch_shapes=[pltpu.VMEM(weight.shape, BF16), pltpu.SemaphoreType.DMA],
+        scratch_shapes=[
+            pltpu.VMEM((4, *query.shape), BF16),
+            pltpu.VMEM(weight.shape, BF16),
+            pltpu.VMEM((4, HEADS, HEAD_DIM, tokens), BF16),
+            dma((4,)),
+            dma,
+            dma((4,)),
+        ],
         cost_estimate=pl.CostEstimate(flops=2 * tokens * weight.size, bytes_accessed=10_000_000, transcendentals=0),
         compiler_params=pltpu.CompilerParams(vmem_limit_bytes=62 << 20),
         name="pack_by_head",
@@ -84,20 +101,16 @@
 def forward_kernel(x_ref, att_ref, e_ref, row_ref, o_ref):
     qs, ks, vs, gs = (frame_pair(x_ref, n) for n in range(4))
     for f in range(2):
-        q_t, k, v_t = qs[f], ks[f].T, vs[f]
-        for b in range(1024 // BLOCK):
-            cols = slice(b * BLOCK, (b + 1) * BLOCK)
-            scores = jnp.dot(k, q_t[:, cols], preferred_element_type=F32)
-            row_max = jnp.max(scores, axis=0, keepdims=True)
-            raised = jnp.exp2(scores * EXP2_SCALE - row_max * EXP2_SCALE)
-            inverse = 1.0 / jnp.sum(raised, axis=0, keepdims=True)
-            raised = raised.astype(BF16)
-            e_ref[f, :, cols] = raised
-            attended = jnp.dot(v_t, raised, preferred_element_type=F32) * inverse
-            o_ref[f, :, cols] = attended
-            row_dot = jnp.sum(gs[f][:, cols].astype(F32) * attended, axis=0, keepdims=True) * inverse
-            row_ref[f, 0:1, cols] = inverse
-            row_ref[f, 1:2, cols] = row_dot
+        scores = jnp.dot(ks[f].T, qs[f], preferred_element_type=F32)
+        row_max = jnp.max(scores, axis=0, keepdims=True)
+        raised = jnp.exp2(scores * EXP2_SCALE - row_max * EXP2_SCALE)
+        inverse = 1.0 / jnp.sum(raised, axis=0, keepdims=True)
+        raised = raised.astype(BF16)
+        e_ref[f] = raised
+        attended = jnp.dot(vs[f], raised, preferred_element_type=F32) * inverse
+        o_ref[f] = attended
+        row_ref[f, 0:1] = inverse
+        row_ref[f, 1:2] = jnp.sum(gs[f].astype(F32) * attended, axis=0, keepdims=True) * inverse
     for s in range(8):
         a, b = o_ref[0, :, 128 * s : 128 * (s + 1)], o_ref[1, :, 128 * s : 128 * (s + 1)]
         low = low_lanes(a.shape)
@@ -260,29 +273,27 @@
         out[...] = joined[lax.rem(place + s, 4)].astype(out.dtype)
 
 
-def final_kernel(place_ref, *refs):
-    refs[4][...] = sum(part[...].astype(F32) for part in refs[:4])
-
-
-def unpack_kernel(x_ref, q_ref, k_ref, v_ref, t_ref):
-    for n, ref in enumerate((q_ref, k_ref, v_ref)):
+def unpack_kernel(x_ref, *refs):
+    parts, outs, total_ref, t_ref = refs[:4], refs[4:7], refs[7], refs[8]
+    for n, ref in enumerate(outs):
         for slot in range(HEADS):
             at = HEAD_DIM * head_of(slot)
             t_ref[at : at + HEAD_DIM] = x_ref[slot, n]
         ref[...] = t_ref[...].T.reshape(ref.shape)
-
-
-def unpack(x, shape):
+    total_ref[...] = sum(part[...].astype(F32) for part in parts)
+
+
+def unpack(x, parts, shape):
     return pl.pallas_call(
         unpack_kernel,
-        in_specs=[pl.BlockSpec(memory_space=pltpu.VMEM)],
-        out_specs=[pl.BlockSpec(memory_space=pltpu.VMEM)] * 3,
-        out_shape=[jax.ShapeDtypeStruct(shape, BF16)] * 3,
+        in_specs=[VM] * 5,
+        out_specs=[VM] * 4,
+        out_shape=[jax.ShapeDtypeStruct(shape, BF16)] * 3 + [jax.ShapeDtypeStruct(parts[0].shape, F32)],
         scratch_shapes=[pltpu.VMEM((shape[-1], shape[0] * shape[1]), BF16)],
         cost_estimate=pl.CostEstimate(flops=0, bytes_accessed=5_000_000, transcendentals=0),
         compiler_params=pltpu.CompilerParams(vmem_limit_bytes=20 << 20),
         name="unpack_by_token",
-    )(x)
+    )(x, *parts)
 
 
 FRAME, PATCH = ("y_lo", "z"), ("y_hi", "x", "core")
@@ -333,8 +344,7 @@
         [pltpu.VMEM((2, 4, 4, 11, columns), F32), pltpu.VMEM((4, 11, features), F32)],
     )
     parts = [own] + [along(part, "x", s) for s, part in enumerate(sent, 1)]
-    (grad_weight,) = small(final_kernel, place, parts, [array((11, features), F32)])
-    outs = unpack(home, query_rows.shape)
+    *outs, grad_weight = unpack(home, parts, query_rows.shape)
     return (*outs, grad_weight)
 
 

time: 177 us -> 171 us (0.966)
  Pallas kernels: 45.6 us -> 39.6 us
    pallas_call x1, Pallas kernels: 15.6 us -> 11.6 us  [forward(): pl.pallas_call(forward_kernel, grid=(2,), in_specs=[PAIR], out_specs=[pl....]
    pallas_call x4 -> x3, Pallas kernels: 3.71 us -> 2.51 us  [small(): pl.pallas_call(kernel, in_specs=[SM] + [VM] * len(operands), out_specs=[V...]
where the time goes in v5:
time: 171 us; the launch traced here: 170 us
  waiting for transfers between devices  47.1 us (28%)
  blocking collectives  45.3 us (26%)
  Pallas kernels  39.6 us (23%)
  starting transfers between devices  36.5 us (21%)
    all_to_all x1, blocking collectives, exchange(): return lax.all_to_all(array, axes, split_axis=0, concat_axis=0, tiled=True)  45.3 us
    ppermute x9, waiting for transfers between devices, along(): return lax.ppermute(array, axis, [(i, (i + step) % 4) for i in range(4)])  34 us
    pallas_call x1, Pallas kernels, backward(): pl.pallas_call(backward_kernel, grid=(2,), in_specs=[PAIR, RAISED, PER_RO...  13.6 us
    ppermute x9, starting transfers between devices, along(): return lax.ppermute(array, axis, [(i, (i + step) % 4) for i in range(4)])  13.1 us
    all_to_all x2, starting transfers between devices, exchange(): return lax.all_to_all(array, axes, split_axis=0, concat_axis=0, tiled=True)  12.8 us
    pallas_call x1, Pallas kernels, forward(): pl.pallas_call(forward_kernel, grid=(2,), in_specs=[PAIR], out_specs=[pl....  11.6 us
    ppermute x3, waiting for transfers between devices, along_y(): lax.ppermute(array, ('y_lo', 'y_hi'), [(place(y), place((y + step) % 4))...  7.75 us
    pallas_call x1, Pallas kernels, pack(): pl.pallas_call(pack_kernel, in_specs=[hbm] * 5, out_specs=hbm, out_shape=...  6.15 us
  transfers between devices with their start and end apart: 19, of which 12 were waited for; matrix products, arithmetic and copies ran while one was open for 0% of the time, Pallas kernels for 12%

profile of v5, /device:TPU:1, one launch (start us, length us, event | category | flops | bytes accessed | tf_op | source)
XLA Modules:
  0.0 170.4 jit_solution(15895308008578582256)
XLA Ops:
  0.6 6.1 %pack_by_head.1 = bf16[16,4,88,256]{3,2,1,0:T(8,128)(2,1)} custom-call(bf16[4,64,1408]{2,1,0:T(8,128)(2,1)} %refs_0_.2, bf16[4,64,1408]{2,1,0:T(8,128)(2,1)} %refs_1_.1, bf16[4,64,1408]{2,1,0:T(8,128)(2,1)} %refs_2_.1, bf16[4,64,1408]{2,1,0:T(8,128)(2,1)} %refs_0_.3, bf16[1408,1408]{1,0:T(8,128)(2,1)} %refs_4_.1), custom_call_target="tpu_custom_call" | custom-call | flops 1015021568 | bytes 10000000 | tf_op jit(solution)/shard_map/pack_by_head/pallas_call | solution.py:82
  6.8 45.3 %all_to_all.15.x_ref = bf16[16,4,88,256]{3,2,1,0:T(8,128)(2,1)} all-to-all(bf16[16,4,88,256]{3,2,1,0:T(8,128)(2,1)} %pack_by_head.1), channel_id=1, replica_groups=mesh['y_lo'=2,'z'=4,'y_hi'=2,'x'=4,'core'=2] {'y_hi','x','core'}, dimensions={0} | all-to-all | bytes 5767168 | tf_op jit(solution)/shard_map/all_to_all | solution.py:303
  52.1 11.6 %spatial_forward.1 = (bf16[4,8,2,24,256]{4,3,2,1,0:T(8,128)(2,1)}, bf16[4,1024,1024]{2,1,0:T(8,128)(2,1)}, f32[4,8,1024]{2,1,0:T(8,128)}) custom-call(bf16[16,4,88,256]{3,2,1,0:T(8,128)(2,1)} %all_to_all.15.x_ref), custom_call_target="tpu_custom_call" | custom-call | flops 4294967296 | bytes 12000000 | tf_op jit(solution)/shard_map/spatial_forward/pallas_call | solution.py:130
  63.7 6.6 %all-to-all-start.2 = ((bf16[32,2,24,256]{3,2,1,0:T(8,128)(2,1)}), bf16[32,2,24,256]{3,2,1,0:T(8,128)(2,1)S(1)}, u32[]{:S(2)}, u32[]{:S(2)}) async-start(bf16[32,2,24,256]{3,2,1,0:T(8,128)(2,1)} %bitcast.5), calls=%async_computation.2 | async-start | bytes 1572864 | tf_op jit(solution)/shard_map/all_to_all | solution.py:303
  70.3 13.6 %spatial_backward.1 = bf16[16,3,88,256]{3,2,1,0:T(8,128)(2,1)} custom-call(bf16[16,4,88,256]{3,2,1,0:T(8,128)(2,1)} %all_to_all.15.x_ref, bf16[4,1024,1024]{2,1,0:T(8,128)(2,1)} %get-tuple-element.21.e_ref, f32[4,8,1024]{2,1,0:T(8,128)} %get-tuple-element.22.row_ref), custom_call_target="tpu_custom_call" | custom-call | flops 8589934592 | bytes 14000000 | tf_op jit(solution)/shard_map/spatial_backward/pallas_call | solution.py:172
  83.9 1.1 all-to-all-done.2.refs_8_
  85.0 6.3 %all-to-all-start.1 = ((bf16[16,3,88,256]{3,2,1,0:T(8,128)(2,1)}), bf16[16,3,88,256]{3,2,1,0:T(8,128)(2,1)S(1)}, u32[]{:S(2)}, u32[]{:S(2)}) async-start(bf16[16,3,88,256]{3,2,1,0:T(8,128)(2,1)} %spatial_backward.1), calls=%async_computation.1 | async-start | bytes 4325376 | tf_op jit(solution)/shard_map/all_to_all | solution.py:303
  91.3 1.2 collective-permute-start
  92.5 2.5 %collective-permute-start.1 = (bf16[4,64,1408]{2,1,0:T(8,128)(2,1)}, bf16[4,64,1408]{2,1,0:T(8,128)(2,1)}, u32[]{:S(2)}, u32[]{:S(2)}) collective-permute-start(bf16[4,64,1408]{2,1,0:T(8,128)(2,1)} %refs_0_.3), channel_id=1, source_target_pairs={{0,32},{16,48},{32,0},{48,16},{1,33},{17,49},{33,1},{49,17},{2,34}... | collective-permute-start | bytes 2162696 | tf_op jit(solution)/shard_map/ppermute | solution.py:307
  94.9 1.1 collective-permute-start.2
  96.1 1.0 collective-permute-start.3
  97.1 13.3 %collective-permute-done.refs_1_ = bf16[4,64,1408]{2,1,0:T(8,128)(2,1)} collective-permute-done((bf16[4,64,1408]{2,1,0:T(8,128)(2,1)}, bf16[4,64,1408]{2,1,0:T(8,128)(2,1)}, u32[]{:S(2)}, u32[]{:S(2)}) %collective-permute-start) | collective-permute-done | bytes 720928 | tf_op jit(solution)/shard_map/ppermute | solution.py:307
  110.3 1.0 collective-permute-start.4
  111.4 15.4 %collective-permute-done.1.refs_2_ = bf16[4,64,1408]{2,1,0:T(8,128)(2,1)} collective-permute-done((bf16[4,64,1408]{2,1,0:T(8,128)(2,1)}, bf16[4,64,1408]{2,1,0:T(8,128)(2,1)}, u32[]{:S(2)}, u32[]{:S(2)}) %collective-permute-start.1) | collective-permute-done | bytes 720928 | tf_op jit(solution)/shard_map/ppermute | solution.py:307
  126.8 1.0 collective-permute-start.5
  127.8 0.0 collective-permute-done.2.refs_3_
  127.8 0.0 collective-permute-start.6
  127.8 0.1 pad_add_fusion.place_ref
  127.9 0.0 collective-permute-done.3.refs_4_
  127.9 0.0 collective-permute-done.4.refs_5_
  127.9 2.1 %collective-permute-done.5.refs_6_ = bf16[4,64,1408]{2,1,0:T(8,128)(2,1)} collective-permute-done((bf16[4,64,1408]{2,1,0:T(8,128)(2,1)}, bf16[4,64,1408]{2,1,0:T(8,128)(2,1)}, u32[]{:S(2)}, u32[]{:S(2)}) %collective-permute-start.5) | collective-permute-done | bytes 720928 | tf_op jit(solution)/shard_map/ppermute | solution.py:316
  129.9 1.0 collective-permute-done.6.refs_7_
  131.0 0.0 copy-start
  131.0 1.1 copy-done
  132.1 4.2 %weight_terms.1 = (f32[4,4,22,176]{3,2,1,0:T(8,128)S(1)}, bf16[4,4,22,176]{3,2,1,0:T(8,128)(2,1)S(1)}, bf16[4,4,22,176]{3,2,1,0:T(8,128)(2,1)S(1)}, bf16[4,4,22,176]{3,2,1,0:T(8,128)(2,1)S(1)}) custom-call(s32[4]{0:T(128)S(1)} %pad_add_fusion.place_ref, bf16[4,64,1408]{2,1,0:T(8,128)(2,1)S(1)} %copy-done, bf16[4,64,1408]{2,1,0:T(8,128)(2,1)} %collective-permute-done.refs_1_, ...), custom_call_target="tpu_custom_call" | custom-call | flops 1015021568 | bytes 8000000 | tf_op jit(solution)/shard_map/weight_terms/pallas_call | solution.py:216
  136.3 0.5 collective-permute-start.7
  136.7 3.5 %collective-permute-start.8 = (bf16[4,4,22,176]{3,2,1,0:T(8,128)(2,1)S(1)}, bf16[4,4,22,176]{3,2,1,0:T(8,128)(2,1)S(1)}, u32[]{:S(2)}, u32[]{:S(2)}) collective-permute-start(bf16[4,4,22,176]{3,2,1,0:T(8,128)(2,1)S(1)} %get-tuple-element.26), channel_id=1, source_target_pairs={{0,8},{64,72},{8,0},{72,64},{1,9},{65,73},{9,1},{73,65},{2,10},{66... | collective-permute-start | bytes 371720 | tf_op jit(solution)/shard_map/ppermute | solution.py:312
  140.2 1.1 collective-permute-start.9
  141.2 2.4 %collective-permute-done.7.refs_1_ = bf16[4,4,22,176]{3,2,1,0:T(8,128)(2,1)S(1)} collective-permute-done((bf16[4,4,22,176]{3,2,1,0:T(8,128)(2,1)S(1)}, bf16[4,4,22,176]{3,2,1,0:T(8,128)(2,1)S(1)}, u32[]{:S(2)}, u32[]{:S(2)}) %collective-permute-start.7) | collective-permute-done | bytes 123936 | tf_op jit(solution)/shard_map/ppermute | solution.py:312
  143.6 5.4 %collective-permute-done.8.refs_2_ = bf16[4,4,22,176]{3,2,1,0:T(8,128)(2,1)S(1)} collective-permute-done((bf16[4,4,22,176]{3,2,1,0:T(8,128)(2,1)S(1)}, bf16[4,4,22,176]{3,2,1,0:T(8,128)(2,1)S(1)}, u32[]{:S(2)}, u32[]{:S(2)}) %collective-permute-start.8) | collective-permute-done | bytes 123936 | tf_op jit(solution)/shard_map/ppermute | solution.py:312
  149.0 0.0 collective-permute-done.9.refs_3_
  149.0 0.6 shard_map.84
  149.6 0.1 collective-permute-start.10
  149.8 2.1 %collective-permute-start.11 = (f32[4,22,176]{2,1,0:T(8,128)S(1)}, f32[4,22,176]{2,1,0:T(8,128)S(1)}, u32[]{:S(2)}, u32[]{:S(2)}) collective-permute-start(f32[4,22,176]{2,1,0:T(8,128)S(1)} %get-tuple-element.30), channel_id=1, source_target_pairs={{0,32},{16,48},{32,0},{48,16},{1,33},{17,49},{33,1},{49,17},{2,34}... | collective-permute-start | bytes 185864 | tf_op jit(solution)/shard_map/ppermute | solution.py:307
  151.9 1.3 collective-permute-start.12
  153.2 2.8 %collective-permute-done.10.refs_1_ = f32[4,22,176]{2,1,0:T(8,128)S(1)} collective-permute-done((f32[4,22,176]{2,1,0:T(8,128)S(1)}, f32[4,22,176]{2,1,0:T(8,128)S(1)}, u32[]{:S(2)}, u32[]{:S(2)}) %collective-permute-start.10) | collective-permute-done | bytes 61984 | tf_op jit(solution)/shard_map/ppermute | solution.py:307
  156.0 0.0 collective-permute-done.11.refs_2_
  156.0 0.5 collective-permute-done.12.refs_3_
  156.4 0.6 shard_map.85
  157.1 2.5 %collective-permute-start.13 = (f32[4,4,11,176]{3,2,1,0:T(8,128)S(1)}, f32[4,4,11,176]{3,2,1,0:T(8,128)S(1)}, u32[]{:S(2)}, u32[]{:S(2)}) collective-permute-start(f32[4,4,11,176]{3,2,1,0:T(8,128)S(1)} %get-tuple-element.33), channel_id=1, source_target_pairs={{0,1},{1,0},{2,3},{3,2},{4,5},{5,4},{6,7},{7,6},{8,9},{9,8},{10,11... | collective-permute-start | bytes 371720 | tf_op jit(solution)/shard_map/ppermute | solution.py:316
  159.5 1.2 collective-permute-done.13.theirs
  160.7 1.3 shard_map.86
  161.9 1.3 collective-permute-start.14
  163.2 2.4 %collective-permute-start.15 = (bf16[11,1408]{1,0:T(8,128)(2,1)S(1)}, bf16[11,1408]{1,0:T(8,128)(2,1)S(1)}, u32[]{:S(2)}, u32[]{:S(2)}) collective-permute-start(bf16[11,1408]{1,0:T(8,128)(2,1)S(1)} %get-tuple-element.36), channel_id=1, source_target_pairs={{0,4},{2,6},{4,0},{6,2},{1,5},{3,7},{5,1},{7,3},{8,12},{10,14},{12... | collective-permute-start | bytes 92936 | tf_op jit(solution)/shard_map/ppermute | solution.py:307
  165.6 1.2 collective-permute-start.16
  166.8 0.0 collective-permute-done.14.refs_1_
  166.8 1.0 collective-permute-done.15.refs_2_
  167.8 1.0 collective-permute-done.16.refs_3_
  168.8 0.0 all-to-all-done.1.x_ref
  168.8 1.6 unpack_by_token.1
Async XLA Ops:
  63.7 21.3 %all-to-all-start.2 = ((bf16[32,2,24,256]{3,2,1,0:T(8,128)(2,1)}), bf16[32,2,24,256]{3,2,1,0:T(8,128)(2,1)S(1)}, u32[]{:S(2)}, u32[]{:S(2)}) async-start(bf16[32,2,24,256]{3,2,1,0:T(8,128)(2,1)} %bitcast.5), calls=%async_computation.2 | async-start | bytes 1572864 | tf_op jit(solution)/shard_map/all_to_all | solution.py:303
  85.0 83.8 %all-to-all-start.1 = ((bf16[16,3,88,256]{3,2,1,0:T(8,128)(2,1)}), bf16[16,3,88,256]{3,2,1,0:T(8,128)(2,1)S(1)}, u32[]{:S(2)}, u32[]{:S(2)}) async-start(bf16[16,3,88,256]{3,2,1,0:T(8,128)(2,1)} %spatial_backward.1), calls=%async_computation.1 | async-start | bytes 4325376 | tf_op jit(solution)/shard_map/all_to_all | solution.py:303
  91.3 19.1 %collective-permute-start = (bf16[4,64,1408]{2,1,0:T(8,128)(2,1)}, bf16[4,64,1408]{2,1,0:T(8,128)(2,1)}, u32[]{:S(2)}, u32[]{:S(2)}) collective-permute-start(bf16[4,64,1408]{2,1,0:T(8,128)(2,1)} %refs_0_.3), channel_id=1, source_target_pairs={{0,16},{16,32},{32,48},{48,0},{1,17},{17,33},{33,49},{49,1},{2,18}... | collective-permute-start | bytes 2162696 | tf_op jit(solution)/shard_map/ppermute | solution.py:307
  92.5 34.3 %collective-permute-start.1 = (bf16[4,64,1408]{2,1,0:T(8,128)(2,1)}, bf16[4,64,1408]{2,1,0:T(8,128)(2,1)}, u32[]{:S(2)}, u32[]{:S(2)}) collective-permute-start(bf16[4,64,1408]{2,1,0:T(8,128)(2,1)} %refs_0_.3), channel_id=1, source_target_pairs={{0,32},{16,48},{32,0},{48,16},{1,33},{17,49},{33,1},{49,17},{2,34}... | collective-permute-start | bytes 2162696 | tf_op jit(solution)/shard_map/ppermute | solution.py:307
  94.9 32.9 %collective-permute-start.2 = (bf16[4,64,1408]{2,1,0:T(8,128)(2,1)}, bf16[4,64,1408]{2,1,0:T(8,128)(2,1)}, u32[]{:S(2)}, u32[]{:S(2)}) collective-permute-start(bf16[4,64,1408]{2,1,0:T(8,128)(2,1)} %refs_0_.3), channel_id=1, source_target_pairs={{0,48},{16,0},{32,16},{48,32},{1,49},{17,1},{33,17},{49,33},{2,50}... | collective-permute-start | bytes 2162696 | tf_op jit(solution)/shard_map/ppermute | solution.py:307
  96.1 31.8 %collective-permute-start.3 = (bf16[4,64,1408]{2,1,0:T(8,128)(2,1)}, bf16[4,64,1408]{2,1,0:T(8,128)(2,1)}, u32[]{:S(2)}, u32[]{:S(2)}) collective-permute-start(bf16[4,64,1408]{2,1,0:T(8,128)(2,1)} %refs_0_.3), channel_id=1, source_target_pairs={{0,1},{1,0},{2,3},{3,2},{4,5},{5,4},{6,7},{7,6},{8,9},{9,8},{10,11... | collective-permute-start | bytes 2162696 | tf_op jit(solution)/shard_map/ppermute | solution.py:316
  110.3 17.5 %collective-permute-start.4 = (bf16[4,64,1408]{2,1,0:T(8,128)(2,1)}, bf16[4,64,1408]{2,1,0:T(8,128)(2,1)}, u32[]{:S(2)}, u32[]{:S(2)}) collective-permute-start(bf16[4,64,1408]{2,1,0:T(8,128)(2,1)} %collective-permute-done.refs_1_), channel_id=1, source_target_pairs={{0,1},{1,0},{2,3},{3,2},{4,5},{5,4},{6,7},{7,6},{8,9},{9,8},{10,11... | collective-permute-start | bytes 2162696 | tf_op jit(solution)/shard_map/ppermute | solution.py:316
  126.8 3.2 %collective-permute-start.5 = (bf16[4,64,1408]{2,1,0:T(8,128)(2,1)}, bf16[4,64,1408]{2,1,0:T(8,128)(2,1)}, u32[]{:S(2)}, u32[]{:S(2)}) collective-permute-start(bf16[4,64,1408]{2,1,0:T(8,128)(2,1)} %collective-permute-done.1.refs_2_), channel_id=1, source_target_pairs={{0,1},{1,0},{2,3},{3,2},{4,5},{5,4},{6,7},{7,6},{8,9},{9,8},{10,11... | collective-permute-start | bytes 2162696 | tf_op jit(solution)/shard_map/ppermute | solution.py:316
  127.8 3.2 %collective-permute-start.6 = (bf16[4,64,1408]{2,1,0:T(8,128)(2,1)}, bf16[4,64,1408]{2,1,0:T(8,128)(2,1)}, u32[]{:S(2)}, u32[]{:S(2)}) collective-permute-start(bf16[4,64,1408]{2,1,0:T(8,128)(2,1)} %collective-permute-done.2.refs_3_), channel_id=1, source_target_pairs={{0,1},{1,0},{2,3},{3,2},{4,5},{5,4},{6,7},{7,6},{8,9},{9,8},{10,11... | collective-permute-start | bytes 2162696 | tf_op jit(solution)/shard_map/ppermute | solution.py:316
  131.0 1.1 copy-start
  136.3 7.4 %collective-permute-start.7 = (bf16[4,4,22,176]{3,2,1,0:T(8,128)(2,1)S(1)}, bf16[4,4,22,176]{3,2,1,0:T(8,128)(2,1)S(1)}, u32[]{:S(2)}, u32[]{:S(2)}) collective-permute-start(bf16[4,4,22,176]{3,2,1,0:T(8,128)(2,1)S(1)} %get-tuple-element.25), channel_id=1, source_target_pairs={{0,64},{64,8},{8,72},{72,0},{1,65},{65,9},{9,73},{73,1},{2,66},{66... | collective-permute-start | bytes 371720 | tf_op jit(solution)/shard_map/ppermute | solution.py:312
  136.7 12.3 %collective-permute-start.8 = (bf16[4,4,22,176]{3,2,1,0:T(8,128)(2,1)S(1)}, bf16[4,4,22,176]{3,2,1,0:T(8,128)(2,1)S(1)}, u32[]{:S(2)}, u32[]{:S(2)}) collective-permute-start(bf16[4,4,22,176]{3,2,1,0:T(8,128)(2,1)S(1)} %get-tuple-element.26), channel_id=1, source_target_pairs={{0,8},{64,72},{8,0},{72,64},{1,9},{65,73},{9,1},{73,65},{2,10},{66... | collective-permute-start | bytes 371720 | tf_op jit(solution)/shard_map/ppermute | solution.py:312
  140.2 8.8 %collective-permute-start.9 = (bf16[4,4,22,176]{3,2,1,0:T(8,128)(2,1)S(1)}, bf16[4,4,22,176]{3,2,1,0:T(8,128)(2,1)S(1)}, u32[]{:S(2)}, u32[]{:S(2)}) collective-permute-start(bf16[4,4,22,176]{3,2,1,0:T(8,128)(2,1)S(1)} %get-tuple-element.27), channel_id=1, source_target_pairs={{0,72},{64,0},{8,64},{72,8},{1,73},{65,1},{9,65},{73,9},{2,74},{66... | collective-permute-start | bytes 371720 | tf_op jit(solution)/shard_map/ppermute | solution.py:312
  149.6 6.3 %collective-permute-start.10 = (f32[4,22,176]{2,1,0:T(8,128)S(1)}, f32[4,22,176]{2,1,0:T(8,128)S(1)}, u32[]{:S(2)}, u32[]{:S(2)}) collective-permute-start(f32[4,22,176]{2,1,0:T(8,128)S(1)} %get-tuple-element.29), channel_id=1, source_target_pairs={{0,16},{16,32},{32,48},{48,0},{1,17},{17,33},{33,49},{49,1},{2,18}... | collective-permute-start | bytes 185864 | tf_op jit(solution)/shard_map/ppermute | solution.py:307
  149.8 6.2 %collective-permute-start.11 = (f32[4,22,176]{2,1,0:T(8,128)S(1)}, f32[4,22,176]{2,1,0:T(8,128)S(1)}, u32[]{:S(2)}, u32[]{:S(2)}) collective-permute-start(f32[4,22,176]{2,1,0:T(8,128)S(1)} %get-tuple-element.30), channel_id=1, source_target_pairs={{0,32},{16,48},{32,0},{48,16},{1,33},{17,49},{33,1},{49,17},{2,34}... | collective-permute-start | bytes 185864 | tf_op jit(solution)/shard_map/ppermute | solution.py:307
  151.9 4.5 %collective-permute-start.12 = (f32[4,22,176]{2,1,0:T(8,128)S(1)}, f32[4,22,176]{2,1,0:T(8,128)S(1)}, u32[]{:S(2)}, u32[]{:S(2)}) collective-permute-start(f32[4,22,176]{2,1,0:T(8,128)S(1)} %get-tuple-element.31), channel_id=1, source_target_pairs={{0,48},{16,0},{32,16},{48,32},{1,49},{17,1},{33,17},{49,33},{2,50}... | collective-permute-start | bytes 185864 | tf_op jit(solution)/shard_map/ppermute | solution.py:307
  157.1 3.6 %collective-permute-start.13 = (f32[4,4,11,176]{3,2,1,0:T(8,128)S(1)}, f32[4,4,11,176]{3,2,1,0:T(8,128)S(1)}, u32[]{:S(2)}, u32[]{:S(2)}) collective-permute-start(f32[4,4,11,176]{3,2,1,0:T(8,128)S(1)} %get-tuple-element.33), channel_id=1, source_target_pairs={{0,1},{1,0},{2,3},{3,2},{4,5},{5,4},{6,7},{7,6},{8,9},{9,8},{10,11... | collective-permute-start | bytes 371720 | tf_op jit(solution)/shard_map/ppermute | solution.py:316
  161.9 4.8 %collective-permute-start.14 = (bf16[11,1408]{1,0:T(8,128)(2,1)S(1)}, bf16[11,1408]{1,0:T(8,128)(2,1)S(1)}, u32[]{:S(2)}, u32[]{:S(2)}) collective-permute-start(bf16[11,1408]{1,0:T(8,128)(2,1)S(1)} %get-tuple-element.35), channel_id=1, source_target_pairs={{0,2},{2,4},{4,6},{6,0},{1,3},{3,5},{5,7},{7,1},{8,10},{10,12},{12... | collective-permute-start | bytes 92936 | tf_op jit(solution)/shard_map/ppermute | solution.py:307
  163.2 4.6 %collective-permute-start.15 = (bf16[11,1408]{1,0:T(8,128)(2,1)S(1)}, bf16[11,1408]{1,0:T(8,128)(2,1)S(1)}, u32[]{:S(2)}, u32[]{:S(2)}) collective-permute-start(bf16[11,1408]{1,0:T(8,128)(2,1)S(1)} %get-tuple-element.36), channel_id=1, source_target_pairs={{0,4},{2,6},{4,0},{6,2},{1,5},{3,7},{5,1},{7,3},{8,12},{10,14},{12... | collective-permute-start | bytes 92936 | tf_op jit(solution)/shard_map/ppermute | solution.py:307
  165.6 3.2 %collective-permute-start.16 = (bf16[11,1408]{1,0:T(8,128)(2,1)S(1)}, bf16[11,1408]{1,0:T(8,128)(2,1)S(1)}, u32[]{:S(2)}, u32[]{:S(2)}) collective-permute-start(bf16[11,1408]{1,0:T(8,128)(2,1)S(1)} %get-tuple-element.37), channel_id=1, source_target_pairs={{0,6},{2,0},{4,2},{6,4},{1,7},{3,1},{5,3},{7,5},{8,14},{10,8},{12,... | collective-permute-start | bytes 92936 | tf_op jit(solution)/shard_map/ppermute | solution.py:307

commit v6 on v5

--- a/solution.py
+++ b/solution.py
@@ -11,6 +11,7 @@
 HALF = 64
 QUARTER = 22
 PADDED = 24
+PIECES = 8
 BLOCK = 256
 SOFTMAX_SCALE = HEAD_DIM ** (-0.5)
 EXP2_SCALE = SOFTMAX_SCALE * 1.4426950408889634
@@ -29,10 +30,15 @@
     return pltpu.roll(tile, HALF, 1)
 
 
-def frame_pair(ref, n):
+def pair_lanes(pair):
+    return slice(pair * 128, (pair + 1) * 128)
+
+
+def frame_pair(ref, n, pair):
     first, second = [], []
+    lanes = pair_lanes(pair)
     for s in range(8):
-        a, b = ref[s, n].astype(F32), ref[s + 8, n].astype(F32)
+        a, b = ref[s, n, :, lanes].astype(F32), ref[s + 8, n, :, lanes].astype(F32)
         low = low_lanes(a.shape)
         first.append(jnp.where(low, a, turned(b)).astype(BF16))
         second.append(jnp.where(low, turned(a), b).astype(BF16))
@@ -49,10 +55,12 @@
 
 def pack_kernel(*refs):
     ins, w_hbm, out_hbm, (in_ref, w_ref, out_ref, in_sem, w_sem, out_sem) = refs[:4], refs[4], refs[5], refs[6:]
-    weight_load = pltpu.make_async_copy(w_hbm, w_ref, w_sem)
+    rows = w_ref.shape[0] // PIECES
+    spans = [pl.ds(n * rows, rows) for n in range(PIECES)]
+    weight_loads = [pltpu.make_async_copy(w_hbm.at[span], w_ref.at[span], w_sem.at[n]) for n, span in enumerate(spans)]
     loads = [pltpu.make_async_copy(ref, in_ref.at[n], in_sem.at[n]) for n, ref in enumerate(ins)]
     stores = [pltpu.make_async_copy(out_ref.at[n], out_hbm.at[:, n], out_sem.at[n]) for n in range(4)]
-    for copy in (weight_load, *loads):
+    for copy in (*loads, *weight_loads):
         copy.start()
 
     def rows_of(n):
@@ -69,7 +77,8 @@
     for n in range(3):
         place(n, rows_of(n))
     upstream = rows_of(3)
-    weight_load.wait()
+    for copy in weight_loads:
+        copy.wait()
     place(3, jnp.dot(upstream, w_ref[...], preferred_element_type=F32).astype(BF16))
     for copy in stores:
         copy.wait()
@@ -89,7 +98,7 @@
             pltpu.VMEM(weight.shape, BF16),
             pltpu.VMEM((4, HEADS, HEAD_DIM, tokens), BF16),
             dma((4,)),
-            dma,
+            dma((PIECES,)),
             dma((4,)),
         ],
         cost_estimate=pl.CostEstimate(flops=2 * tokens * weight.size, bytes_accessed=10_000_000, transcendentals=0),
@@ -98,54 +107,78 @@
     )(query, key, value, upstream, weight)
 
 
-def forward_kernel(x_ref, att_ref, e_ref, row_ref, o_ref):
-    qs, ks, vs, gs = (frame_pair(x_ref, n) for n in range(4))
-    for f in range(2):
-        scores = jnp.dot(ks[f].T, qs[f], preferred_element_type=F32)
-        row_max = jnp.max(scores, axis=0, keepdims=True)
-        raised = jnp.exp2(scores * EXP2_SCALE - row_max * EXP2_SCALE)
-        inverse = 1.0 / jnp.sum(raised, axis=0, keepdims=True)
-        raised = raised.astype(BF16)
-        e_ref[f] = raised
-        attended = jnp.dot(vs[f], raised, preferred_element_type=F32) * inverse
-        o_ref[f] = attended
-        row_ref[f, 0:1] = inverse
-        row_ref[f, 1:2] = jnp.sum(gs[f].astype(F32) * attended, axis=0, keepdims=True) * inverse
-    for s in range(8):
-        a, b = o_ref[0, :, 128 * s : 128 * (s + 1)], o_ref[1, :, 128 * s : 128 * (s + 1)]
-        low = low_lanes(a.shape)
-        for slot, tile in ((s, jnp.where(low, a, turned(b))), (s + 8, jnp.where(low, turned(a), b))):
-            for quarter in range(4):
-                rows = tile[QUARTER * quarter : QUARTER * (quarter + 1)]
-                rows = jnp.concatenate([rows, jnp.zeros((PADDED - QUARTER, 128), F32)], axis=0)
-                att_ref[quarter, slot // 2, slot % 2] = rows.astype(BF16)
-
-
-PAIR = pl.BlockSpec((HEADS, 4, HEAD_DIM, 128), lambda i: (0, 0, 0, i))
-RAISED = pl.BlockSpec((2, 1024, 1024), lambda i: (i, 0, 0))
-PER_ROW = pl.BlockSpec((2, 8, 1024), lambda i: (i, 0, 0))
+def stored(buffer, hbm, sem, pair):
+    lead = (slice(None),) * (len(hbm.shape) - 1)
+    return pltpu.make_async_copy(buffer.at[pair], hbm.at[(*lead, pair_lanes(pair))], sem.at[pair])
+
+
+def forward_kernel(x_ref, att_hbm, e_hbm, row_ref, o_ref, att_ref, e_ref, sem, e_sem):
+    def kept(frame):
+        return pltpu.make_async_copy(e_ref.at[frame], e_hbm.at[frame], e_sem.at[frame])
+
+    def step(pair, carry):
+        qs, ks, vs, gs = (frame_pair(x_ref, n, pair) for n in range(4))
+        for f in range(2):
+            frame = 2 * pair + f
+            scores = jnp.dot(ks[f].T, qs[f], preferred_element_type=F32)
+            row_max = jnp.max(scores, axis=0, keepdims=True)
+            raised = jnp.exp2(scores * EXP2_SCALE - row_max * EXP2_SCALE)
+            inverse = 1.0 / jnp.sum(raised, axis=0, keepdims=True)
+            raised = raised.astype(BF16)
+            e_ref[frame] = raised
+            kept(frame).start()
+            attended = jnp.dot(vs[f], raised, preferred_element_type=F32) * inverse
+            o_ref[f] = attended
+            row_ref[frame, 0:1] = inverse
+            row_ref[frame, 1:2] = jnp.sum(gs[f].astype(F32) * attended, axis=0, keepdims=True) * inverse
+        for s in range(8):
+            a, b = o_ref[0, :, 128 * s : 128 * (s + 1)], o_ref[1, :, 128 * s : 128 * (s + 1)]
+            low = low_lanes(a.shape)
+            for slot, tile in ((s, jnp.where(low, a, turned(b))), (s + 8, jnp.where(low, turned(a), b))):
+                for quarter in range(4):
+                    rows = tile[QUARTER * quarter : QUARTER * (quarter + 1)]
+                    rows = jnp.concatenate([rows, jnp.zeros((PADDED - QUARTER, 128), F32)], axis=0)
+                    att_ref[pair, quarter * 8 + slot // 2, slot % 2] = rows.astype(BF16)
+        stored(att_ref, att_hbm, sem, pair).start()
+        return carry
+
+    for pair in range(2):
+        step(pair, 0)
+    for pair in range(2):
+        stored(att_ref, att_hbm, sem, pair).wait()
+    for frame in range(4):
+        kept(frame).wait()
+
+
+VM, SM = pl.BlockSpec(memory_space=pltpu.VMEM), pl.BlockSpec(memory_space=pltpu.SMEM)
+HB = pl.BlockSpec(memory_space=pltpu.HBM)
 
 
 def forward(x):
     return pl.pallas_call(
         forward_kernel,
-        grid=(2,),
-        in_specs=[PAIR],
-        out_specs=[pl.BlockSpec((4, 8, 2, PADDED, 128), lambda i: (0, 0, 0, 0, i)), RAISED, PER_ROW],
+        in_specs=[VM],
+        out_specs=[HB, HB, VM],
         out_shape=[
-            jax.ShapeDtypeStruct((4, 8, 2, PADDED, 256), BF16),
-            jax.ShapeDtypeStruct((4, 1024, 1024), BF16),
+            pltpu.HBM((32, 2, PADDED, 256), BF16),
+            pltpu.HBM((4, 1024, 1024), BF16),
             jax.ShapeDtypeStruct((4, 8, 1024), F32),
         ],
-        scratch_shapes=[pltpu.VMEM((2, HEAD_DIM, 1024), F32)],
+        scratch_shapes=[
+            pltpu.VMEM((2, HEAD_DIM, 1024), F32),
+            pltpu.VMEM((2, 32, 2, PADDED, 128), BF16),
+            pltpu.VMEM((4, 1024, 1024), BF16),
+            pltpu.SemaphoreType.DMA((2,)),
+            pltpu.SemaphoreType.DMA((4,)),
+        ],
         cost_estimate=pl.CostEstimate(flops=4 * 4 * 1024 * 1024 * 256, bytes_accessed=12_000_000, transcendentals=1 << 22),
-        compiler_params=pltpu.CompilerParams(vmem_limit_bytes=56 << 20),
+        compiler_params=pltpu.CompilerParams(vmem_limit_bytes=40 << 20),
         name="spatial_forward",
     )(x)
 
 
 def backward_kernel(x_ref, e_ref, row_ref, out_ref, dq_ref, dk_ref, dv_ref):
-    qs, ks, vs, gs = (frame_pair(x_ref, n) for n in range(4))
+    qs, ks, vs, gs = (frame_pair(x_ref, n, 0) for n in range(4))
     for f in range(2):
         q_t, k_t, v = qs[f], ks[f], vs[f].T
         g_t = (gs[f].astype(F32) * row_ref[f, 0:1, :]).astype(BF16)
@@ -172,7 +205,11 @@
     return pl.pallas_call(
         backward_kernel,
         grid=(2,),
-        in_specs=[PAIR, RAISED, PER_ROW],
+        in_specs=[
+            pl.BlockSpec((HEADS, 4, HEAD_DIM, 128), lambda i: (0, 0, 0, i)),
+            pl.BlockSpec((2, 1024, 1024), lambda i: (i, 0, 0)),
+            pl.BlockSpec((2, 8, 1024), lambda i: (i, 0, 0)),
+        ],
         out_specs=pl.BlockSpec((HEADS, 3, HEAD_DIM, 128), lambda i: (0, 0, 0, i)),
         out_shape=jax.ShapeDtypeStruct((HEADS, 3, HEAD_DIM, 256), BF16),
         scratch_shapes=[pltpu.VMEM((2, HEAD_DIM, 1024), F32)] * 3,
@@ -207,9 +244,6 @@
                 out[x, depth] = block[QUARTER * x : QUARTER * (x + 1)].astype(out.dtype)
 
 
-VM, SM = pl.BlockSpec(memory_space=pltpu.VMEM), pl.BlockSpec(memory_space=pltpu.SMEM)
-
-
 def weight_terms(place, grads, att):
     shape = (4, 4, QUARTER, 8 * QUARTER)
     features = grads[0].shape[-1]
@@ -323,7 +357,7 @@
     gathered = [grad_out] + [along(grad_out, "z", r) for r in (1, 2, 3)]
     gathered += [other_core(array) for array in gathered]
     attended, raised, per_row = forward(x)
-    att = exchange(attended.reshape(32, 2, PADDED, 256), ("z", "y_hi", "x"))
+    att = exchange(attended, ("z", "y_hi", "x"))
     grads = backward(x, raised, per_row)
     own, *sent = weight_terms(place, gathered, att)
     parts = [own] + [along_y(part, s) for s, part in enumerate(sent, 1)]

time: 171 us -> 170 us (level)
  Pallas kernels: 39.6 us -> 37.4 us
where the time goes in v6:
time: 170 us; the launch traced here: 169 us
  waiting for transfers between devices  47 us (28%)
  blocking collectives  45.2 us (27%)
  Pallas kernels  37.4 us (22%)
  starting transfers between devices  36.6 us (22%)
  local copies, waits for them, and re-layouts  1.76 us (1%)
    all_to_all x1, blocking collectives, exchange(): return lax.all_to_all(array, axes, split_axis=0, concat_axis=0, tiled=True)  45.2 us
    ppermute x9, waiting for transfers between devices, along(): return lax.ppermute(array, axis, [(i, (i + step) % 4) for i in range(4)])  34 us
    pallas_call x1, Pallas kernels, backward(): pl.pallas_call(backward_kernel, grid=(2,), in_specs=[pl.BlockSpec((HEADS,...  13.6 us
    ppermute x9, starting transfers between devices, along(): return lax.ppermute(array, axis, [(i, (i + step) % 4) for i in range(4)])  13.1 us
    all_to_all x2, starting transfers between devices, exchange(): return lax.all_to_all(array, axes, split_axis=0, concat_axis=0, tiled=True)  13 us
    pallas_call x1, Pallas kernels, forward(): pl.pallas_call(forward_kernel, in_specs=[VM], out_specs=[HB, HB, VM], out...  9.85 us
    ppermute x3, waiting for transfers between devices, along_y(): lax.ppermute(array, ('y_lo', 'y_hi'), [(place(y), place((y + step) % 4))...  7.78 us
    pallas_call x1, Pallas kernels, pack(): pl.pallas_call(pack_kernel, in_specs=[hbm] * 5, out_specs=hbm, out_shape=...  5.59 us
  transfers between devices with their start and end apart: 19, of which 12 were waited for; matrix products, arithmetic and copies ran while one was open for 0% of the time, Pallas kernels for 12%

profile of v6, /device:TPU:1, one launch (start us, length us, event | category | flops | bytes accessed | tf_op | source)
XLA Modules:
  0.0 168.7 jit_solution(12256457224340542526)
XLA Ops:
  0.6 5.6 %pack_by_head.1 = bf16[16,4,88,256]{3,2,1,0:T(8,128)(2,1)} custom-call(bf16[4,64,1408]{2,1,0:T(8,128)(2,1)} %refs_0_.2, bf16[4,64,1408]{2,1,0:T(8,128)(2,1)} %refs_1_.1, bf16[4,64,1408]{2,1,0:T(8,128)(2,1)} %refs_2_.1, bf16[4,64,1408]{2,1,0:T(8,128)(2,1)} %refs_0_.3, bf16[1408,1408]{1,0:T(8,128)(2,1)} %refs_4_.1), custom_call_target="tpu_custom_call" | custom-call | flops 1015021568 | bytes 10000000 | tf_op jit(solution)/shard_map/pack_by_head/pallas_call | solution.py:91
  6.2 45.2 %all_to_all.15.x_ref = bf16[16,4,88,256]{3,2,1,0:T(8,128)(2,1)S(1)} all-to-all(bf16[16,4,88,256]{3,2,1,0:T(8,128)(2,1)} %pack_by_head.1), channel_id=1, replica_groups=mesh['y_lo'=2,'z'=4,'y_hi'=2,'x'=4,'core'=2] {'y_hi','x','core'}, dimensions={0} | all-to-all | bytes 5767168 | tf_op jit(solution)/shard_map/all_to_all | solution.py:337
  51.5 0.0 copy-start
  51.5 9.8 %spatial_forward.1 = (bf16[32,2,24,256]{3,2,1,0:T(8,128)(2,1)}, bf16[4,1024,1024]{2,1,0:T(8,128)(2,1)}, f32[4,8,1024]{2,1,0:T(8,128)S(1)}) custom-call(bf16[16,4,88,256]{3,2,1,0:T(8,128)(2,1)S(1)} %all_to_all.15.x_ref), custom_call_target="tpu_custom_call" | custom-call | flops 4294967296 | bytes 12000000 | tf_op jit(solution)/shard_map/spatial_forward/pallas_call | solution.py:158
  61.3 0.0 copy-done
  61.3 0.0 copy-start.2
  61.3 0.6 copy-done.2
  62.0 6.7 %all-to-all-start.2 = ((bf16[32,2,24,256]{3,2,1,0:T(8,128)(2,1)}), bf16[32,2,24,256]{3,2,1,0:T(8,128)(2,1)S(1)}, u32[]{:S(2)}, u32[]{:S(2)}) async-start(bf16[32,2,24,256]{3,2,1,0:T(8,128)(2,1)} %get-tuple-element.23), calls=%async_computation.2 | async-start | bytes 1572864 | tf_op jit(solution)/shard_map/all_to_all | solution.py:337
  68.7 13.6 %spatial_backward.1 = bf16[16,3,88,256]{3,2,1,0:T(8,128)(2,1)} custom-call(bf16[16,4,88,256]{3,2,1,0:T(8,128)(2,1)} %copy-done, bf16[4,1024,1024]{2,1,0:T(8,128)(2,1)} %get-tuple-element.21.e_ref, f32[4,8,1024]{2,1,0:T(8,128)} %copy-done.2), custom_call_target="tpu_custom_call" | custom-call | flops 8589934592 | bytes 14000000 | tf_op jit(solution)/shard_map/spatial_backward/pallas_call | solution.py:205
  82.4 0.9 all-to-all-done.2.refs_8_
  83.3 6.3 %all-to-all-start.1 = ((bf16[16,3,88,256]{3,2,1,0:T(8,128)(2,1)}), bf16[16,3,88,256]{3,2,1,0:T(8,128)(2,1)S(1)}, u32[]{:S(2)}, u32[]{:S(2)}) async-start(bf16[16,3,88,256]{3,2,1,0:T(8,128)(2,1)} %spatial_backward.1), calls=%async_computation.1 | async-start | bytes 4325376 | tf_op jit(solution)/shard_map/all_to_all | solution.py:337
  89.6 1.2 collective-permute-start
  90.8 2.5 %collective-permute-start.1 = (bf16[4,64,1408]{2,1,0:T(8,128)(2,1)}, bf16[4,64,1408]{2,1,0:T(8,128)(2,1)}, u32[]{:S(2)}, u32[]{:S(2)}) collective-permute-start(bf16[4,64,1408]{2,1,0:T(8,128)(2,1)} %refs_0_.3), channel_id=1, source_target_pairs={{0,32},{16,48},{32,0},{48,16},{1,33},{17,49},{33,1},{49,17},{2,34}... | collective-permute-start | bytes 2162696 | tf_op jit(solution)/shard_map/ppermute | solution.py:341
  93.2 1.1 collective-permute-start.2
  94.4 1.0 collective-permute-start.3
  95.4 13.2 %collective-permute-done.refs_1_ = bf16[4,64,1408]{2,1,0:T(8,128)(2,1)} collective-permute-done((bf16[4,64,1408]{2,1,0:T(8,128)(2,1)}, bf16[4,64,1408]{2,1,0:T(8,128)(2,1)}, u32[]{:S(2)}, u32[]{:S(2)}) %collective-permute-start) | collective-permute-done | bytes 720928 | tf_op jit(solution)/shard_map/ppermute | solution.py:341
  108.6 1.0 collective-permute-start.4
  109.6 15.4 %collective-permute-done.1.refs_2_ = bf16[4,64,1408]{2,1,0:T(8,128)(2,1)} collective-permute-done((bf16[4,64,1408]{2,1,0:T(8,128)(2,1)}, bf16[4,64,1408]{2,1,0:T(8,128)(2,1)}, u32[]{:S(2)}, u32[]{:S(2)}) %collective-permute-start.1) | collective-permute-done | bytes 720928 | tf_op jit(solution)/shard_map/ppermute | solution.py:341
  125.1 1.0 collective-permute-start.5
  126.1 0.0 collective-permute-done.2.refs_3_
  126.1 0.0 collective-permute-start.6
  126.1 0.1 pad_add_fusion.place_ref
  126.2 0.0 collective-permute-done.3.refs_4_
  126.2 0.0 collective-permute-done.4.refs_5_
  126.2 2.1 %collective-permute-done.5.refs_6_ = bf16[4,64,1408]{2,1,0:T(8,128)(2,1)} collective-permute-done((bf16[4,64,1408]{2,1,0:T(8,128)(2,1)}, bf16[4,64,1408]{2,1,0:T(8,128)(2,1)}, u32[]{:S(2)}, u32[]{:S(2)}) %collective-permute-start.5) | collective-permute-done | bytes 720928 | tf_op jit(solution)/shard_map/ppermute | solution.py:350
  128.2 1.0 collective-permute-done.6.refs_7_
  129.3 0.0 copy-start.1
  129.3 1.1 copy-done.1
  130.4 4.2 %weight_terms.1 = (f32[4,4,22,176]{3,2,1,0:T(8,128)S(1)}, bf16[4,4,22,176]{3,2,1,0:T(8,128)(2,1)S(1)}, bf16[4,4,22,176]{3,2,1,0:T(8,128)(2,1)S(1)}, bf16[4,4,22,176]{3,2,1,0:T(8,128)(2,1)S(1)}) custom-call(s32[4]{0:T(128)S(1)} %pad_add_fusion.place_ref, bf16[4,64,1408]{2,1,0:T(8,128)(2,1)S(1)} %copy-done.1, ...), custom_call_target="tpu_custom_call" | custom-call | flops 1015021568 | bytes 8000000 | tf_op jit(solution)/shard_map/weight_terms/pallas_call | solution.py:250
  134.6 0.5 collective-permute-start.7
  135.0 3.5 %collective-permute-start.8 = (bf16[4,4,22,176]{3,2,1,0:T(8,128)(2,1)S(1)}, bf16[4,4,22,176]{3,2,1,0:T(8,128)(2,1)S(1)}, u32[]{:S(2)}, u32[]{:S(2)}) collective-permute-start(bf16[4,4,22,176]{3,2,1,0:T(8,128)(2,1)S(1)} %get-tuple-element.26), channel_id=1, source_target_pairs={{0,8},{64,72},{8,0},{72,64},{1,9},{65,73},{9,1},{73,65},{2,10},{66... | collective-permute-start | bytes 371720 | tf_op jit(solution)/shard_map/ppermute | solution.py:346
  138.5 1.1 collective-permute-start.9
  139.6 2.4 %collective-permute-done.7.refs_1_ = bf16[4,4,22,176]{3,2,1,0:T(8,128)(2,1)S(1)} collective-permute-done((bf16[4,4,22,176]{3,2,1,0:T(8,128)(2,1)S(1)}, bf16[4,4,22,176]{3,2,1,0:T(8,128)(2,1)S(1)}, u32[]{:S(2)}, u32[]{:S(2)}) %collective-permute-start.7) | collective-permute-done | bytes 123936 | tf_op jit(solution)/shard_map/ppermute | solution.py:346
  141.9 5.4 %collective-permute-done.8.refs_2_ = bf16[4,4,22,176]{3,2,1,0:T(8,128)(2,1)S(1)} collective-permute-done((bf16[4,4,22,176]{3,2,1,0:T(8,128)(2,1)S(1)}, bf16[4,4,22,176]{3,2,1,0:T(8,128)(2,1)S(1)}, u32[]{:S(2)}, u32[]{:S(2)}) %collective-permute-start.8) | collective-permute-done | bytes 123936 | tf_op jit(solution)/shard_map/ppermute | solution.py:346
  147.3 0.0 collective-permute-done.9.refs_3_
  147.3 0.6 shard_map.84
  148.0 0.1 collective-permute-start.10
  148.1 2.1 %collective-permute-start.11 = (f32[4,22,176]{2,1,0:T(8,128)S(1)}, f32[4,22,176]{2,1,0:T(8,128)S(1)}, u32[]{:S(2)}, u32[]{:S(2)}) collective-permute-start(f32[4,22,176]{2,1,0:T(8,128)S(1)} %get-tuple-element.30), channel_id=1, source_target_pairs={{0,32},{16,48},{32,0},{48,16},{1,33},{17,49},{33,1},{49,17},{2,34}... | collective-permute-start | bytes 185864 | tf_op jit(solution)/shard_map/ppermute | solution.py:341
  150.2 1.3 collective-permute-start.12
  151.5 2.9 %collective-permute-done.10.refs_1_ = f32[4,22,176]{2,1,0:T(8,128)S(1)} collective-permute-done((f32[4,22,176]{2,1,0:T(8,128)S(1)}, f32[4,22,176]{2,1,0:T(8,128)S(1)}, u32[]{:S(2)}, u32[]{:S(2)}) %collective-permute-start.10) | collective-permute-done | bytes 61984 | tf_op jit(solution)/shard_map/ppermute | solution.py:341
  154.4 0.0 collective-permute-done.11.refs_2_
  154.4 0.5 collective-permute-done.12.refs_3_
  154.8 0.6 shard_map.85
  155.4 2.4 %collective-permute-start.13 = (f32[4,4,11,176]{3,2,1,0:T(8,128)S(1)}, f32[4,4,11,176]{3,2,1,0:T(8,128)S(1)}, u32[]{:S(2)}, u32[]{:S(2)}) collective-permute-start(f32[4,4,11,176]{3,2,1,0:T(8,128)S(1)} %get-tuple-element.33), channel_id=1, source_target_pairs={{0,1},{1,0},{2,3},{3,2},{4,5},{5,4},{6,7},{7,6},{8,9},{9,8},{10,11... | collective-permute-start | bytes 371720 | tf_op jit(solution)/shard_map/ppermute | solution.py:350
  157.9 1.2 collective-permute-done.13.theirs
  159.0 1.3 shard_map.86
  160.3 1.3 collective-permute-start.14
  161.5 2.4 %collective-permute-start.15 = (bf16[11,1408]{1,0:T(8,128)(2,1)S(1)}, bf16[11,1408]{1,0:T(8,128)(2,1)S(1)}, u32[]{:S(2)}, u32[]{:S(2)}) collective-permute-start(bf16[11,1408]{1,0:T(8,128)(2,1)S(1)} %get-tuple-element.36), channel_id=1, source_target_pairs={{0,4},{2,6},{4,0},{6,2},{1,5},{3,7},{5,1},{7,3},{8,12},{10,14},{12... | collective-permute-start | bytes 92936 | tf_op jit(solution)/shard_map/ppermute | solution.py:341
  163.9 1.2 collective-permute-start.16
  165.1 0.0 collective-permute-done.14.refs_1_
  165.1 1.0 collective-permute-done.15.refs_2_
  166.2 1.0 collective-permute-done.16.refs_3_
  167.1 0.0 all-to-all-done.1.x_ref
  167.1 1.6 unpack_by_token.1
Async XLA Ops:
  51.5 9.9 %copy-start = (bf16[16,4,88,256]{3,2,1,0:T(8,128)(2,1)}, bf16[16,4,88,256]{3,2,1,0:T(8,128)(2,1)S(1)}, u32[]{:S(2)}) copy-start(bf16[16,4,88,256]{3,2,1,0:T(8,128)(2,1)S(1)} %all_to_all.15.x_ref) | copy-start | bytes 8650756
  61.3 0.7 copy-start.2
  62.0 21.3 %all-to-all-start.2 = ((bf16[32,2,24,256]{3,2,1,0:T(8,128)(2,1)}), bf16[32,2,24,256]{3,2,1,0:T(8,128)(2,1)S(1)}, u32[]{:S(2)}, u32[]{:S(2)}) async-start(bf16[32,2,24,256]{3,2,1,0:T(8,128)(2,1)} %get-tuple-element.23), calls=%async_computation.2 | async-start | bytes 1572864 | tf_op jit(solution)/shard_map/all_to_all | solution.py:337
  83.3 83.8 %all-to-all-start.1 = ((bf16[16,3,88,256]{3,2,1,0:T(8,128)(2,1)}), bf16[16,3,88,256]{3,2,1,0:T(8,128)(2,1)S(1)}, u32[]{:S(2)}, u32[]{:S(2)}) async-start(bf16[16,3,88,256]{3,2,1,0:T(8,128)(2,1)} %spatial_backward.1), calls=%async_computation.1 | async-start | bytes 4325376 | tf_op jit(solution)/shard_map/all_to_all | solution.py:337
  89.6 19.1 %collective-permute-start = (bf16[4,64,1408]{2,1,0:T(8,128)(2,1)}, bf16[4,64,1408]{2,1,0:T(8,128)(2,1)}, u32[]{:S(2)}, u32[]{:S(2)}) collective-permute-start(bf16[4,64,1408]{2,1,0:T(8,128)(2,1)} %refs_0_.3), channel_id=1, source_target_pairs={{0,16},{16,32},{32,48},{48,0},{1,17},{17,33},{33,49},{49,1},{2,18}... | collective-permute-start | bytes 2162696 | tf_op jit(solution)/shard_map/ppermute | solution.py:341
  90.8 34.3 %collective-permute-start.1 = (bf16[4,64,1408]{2,1,0:T(8,128)(2,1)}, bf16[4,64,1408]{2,1,0:T(8,128)(2,1)}, u32[]{:S(2)}, u32[]{:S(2)}) collective-permute-start(bf16[4,64,1408]{2,1,0:T(8,128)(2,1)} %refs_0_.3), channel_id=1, source_target_pairs={{0,32},{16,48},{32,0},{48,16},{1,33},{17,49},{33,1},{49,17},{2,34}... | collective-permute-start | bytes 2162696 | tf_op jit(solution)/shard_map/ppermute | solution.py:341
  93.2 32.9 %collective-permute-start.2 = (bf16[4,64,1408]{2,1,0:T(8,128)(2,1)}, bf16[4,64,1408]{2,1,0:T(8,128)(2,1)}, u32[]{:S(2)}, u32[]{:S(2)}) collective-permute-start(bf16[4,64,1408]{2,1,0:T(8,128)(2,1)} %refs_0_.3), channel_id=1, source_target_pairs={{0,48},{16,0},{32,16},{48,32},{1,49},{17,1},{33,17},{49,33},{2,50}... | collective-permute-start | bytes 2162696 | tf_op jit(solution)/shard_map/ppermute | solution.py:341
  94.4 31.8 %collective-permute-start.3 = (bf16[4,64,1408]{2,1,0:T(8,128)(2,1)}, bf16[4,64,1408]{2,1,0:T(8,128)(2,1)}, u32[]{:S(2)}, u32[]{:S(2)}) collective-permute-start(bf16[4,64,1408]{2,1,0:T(8,128)(2,1)} %refs_0_.3), channel_id=1, source_target_pairs={{0,1},{1,0},{2,3},{3,2},{4,5},{5,4},{6,7},{7,6},{8,9},{9,8},{10,11... | collective-permute-start | bytes 2162696 | tf_op jit(solution)/shard_map/ppermute | solution.py:350
  108.6 17.6 %collective-permute-start.4 = (bf16[4,64,1408]{2,1,0:T(8,128)(2,1)}, bf16[4,64,1408]{2,1,0:T(8,128)(2,1)}, u32[]{:S(2)}, u32[]{:S(2)}) collective-permute-start(bf16[4,64,1408]{2,1,0:T(8,128)(2,1)} %collective-permute-done.refs_1_), channel_id=1, source_target_pairs={{0,1},{1,0},{2,3},{3,2},{4,5},{5,4},{6,7},{7,6},{8,9},{9,8},{10,11... | collective-permute-start | bytes 2162696 | tf_op jit(solution)/shard_map/ppermute | solution.py:350
  125.1 3.2 %collective-permute-start.5 = (bf16[4,64,1408]{2,1,0:T(8,128)(2,1)}, bf16[4,64,1408]{2,1,0:T(8,128)(2,1)}, u32[]{:S(2)}, u32[]{:S(2)}) collective-permute-start(bf16[4,64,1408]{2,1,0:T(8,128)(2,1)} %collective-permute-done.1.refs_2_), channel_id=1, source_target_pairs={{0,1},{1,0},{2,3},{3,2},{4,5},{5,4},{6,7},{7,6},{8,9},{9,8},{10,11... | collective-permute-start | bytes 2162696 | tf_op jit(solution)/shard_map/ppermute | solution.py:350
  126.1 3.2 %collective-permute-start.6 = (bf16[4,64,1408]{2,1,0:T(8,128)(2,1)}, bf16[4,64,1408]{2,1,0:T(8,128)(2,1)}, u32[]{:S(2)}, u32[]{:S(2)}) collective-permute-start(bf16[4,64,1408]{2,1,0:T(8,128)(2,1)} %collective-permute-done.2.refs_3_), channel_id=1, source_target_pairs={{0,1},{1,0},{2,3},{3,2},{4,5},{5,4},{6,7},{7,6},{8,9},{9,8},{10,11... | collective-permute-start | bytes 2162696 | tf_op jit(solution)/shard_map/ppermute | solution.py:350
  129.3 1.1 copy-start.1
  134.6 7.4 %collective-permute-start.7 = (bf16[4,4,22,176]{3,2,1,0:T(8,128)(2,1)S(1)}, bf16[4,4,22,176]{3,2,1,0:T(8,128)(2,1)S(1)}, u32[]{:S(2)}, u32[]{:S(2)}) collective-permute-start(bf16[4,4,22,176]{3,2,1,0:T(8,128)(2,1)S(1)} %get-tuple-element.25), channel_id=1, source_target_pairs={{0,64},{64,8},{8,72},{72,0},{1,65},{65,9},{9,73},{73,1},{2,66},{66... | collective-permute-start | bytes 371720 | tf_op jit(solution)/shard_map/ppermute | solution.py:346
  135.0 12.3 %collective-permute-start.8 = (bf16[4,4,22,176]{3,2,1,0:T(8,128)(2,1)S(1)}, bf16[4,4,22,176]{3,2,1,0:T(8,128)(2,1)S(1)}, u32[]{:S(2)}, u32[]{:S(2)}) collective-permute-start(bf16[4,4,22,176]{3,2,1,0:T(8,128)(2,1)S(1)} %get-tuple-element.26), channel_id=1, source_target_pairs={{0,8},{64,72},{8,0},{72,64},{1,9},{65,73},{9,1},{73,65},{2,10},{66... | collective-permute-start | bytes 371720 | tf_op jit(solution)/shard_map/ppermute | solution.py:346
  138.5 8.8 %collective-permute-start.9 = (bf16[4,4,22,176]{3,2,1,0:T(8,128)(2,1)S(1)}, bf16[4,4,22,176]{3,2,1,0:T(8,128)(2,1)S(1)}, u32[]{:S(2)}, u32[]{:S(2)}) collective-permute-start(bf16[4,4,22,176]{3,2,1,0:T(8,128)(2,1)S(1)} %get-tuple-element.27), channel_id=1, source_target_pairs={{0,72},{64,0},{8,64},{72,8},{1,73},{65,1},{9,65},{73,9},{2,74},{66... | collective-permute-start | bytes 371720 | tf_op jit(solution)/shard_map/ppermute | solution.py:346
  148.0 6.4 %collective-permute-start.10 = (f32[4,22,176]{2,1,0:T(8,128)S(1)}, f32[4,22,176]{2,1,0:T(8,128)S(1)}, u32[]{:S(2)}, u32[]{:S(2)}) collective-permute-start(f32[4,22,176]{2,1,0:T(8,128)S(1)} %get-tuple-element.29), channel_id=1, source_target_pairs={{0,16},{16,32},{32,48},{48,0},{1,17},{17,33},{33,49},{49,1},{2,18}... | collective-permute-start | bytes 185864 | tf_op jit(solution)/shard_map/ppermute | solution.py:341
  148.1 6.3 %collective-permute-start.11 = (f32[4,22,176]{2,1,0:T(8,128)S(1)}, f32[4,22,176]{2,1,0:T(8,128)S(1)}, u32[]{:S(2)}, u32[]{:S(2)}) collective-permute-start(f32[4,22,176]{2,1,0:T(8,128)S(1)} %get-tuple-element.30), channel_id=1, source_target_pairs={{0,32},{16,48},{32,0},{48,16},{1,33},{17,49},{33,1},{49,17},{2,34}... | collective-permute-start | bytes 185864 | tf_op jit(solution)/shard_map/ppermute | solution.py:341
  150.2 4.6 %collective-permute-start.12 = (f32[4,22,176]{2,1,0:T(8,128)S(1)}, f32[4,22,176]{2,1,0:T(8,128)S(1)}, u32[]{:S(2)}, u32[]{:S(2)}) collective-permute-start(f32[4,22,176]{2,1,0:T(8,128)S(1)} %get-tuple-element.31), channel_id=1, source_target_pairs={{0,48},{16,0},{32,16},{48,32},{1,49},{17,1},{33,17},{49,33},{2,50}... | collective-permute-start | bytes 185864 | tf_op jit(solution)/shard_map/ppermute | solution.py:341
  155.4 3.6 %collective-permute-start.13 = (f32[4,4,11,176]{3,2,1,0:T(8,128)S(1)}, f32[4,4,11,176]{3,2,1,0:T(8,128)S(1)}, u32[]{:S(2)}, u32[]{:S(2)}) collective-permute-start(f32[4,4,11,176]{3,2,1,0:T(8,128)S(1)} %get-tuple-element.33), channel_id=1, source_target_pairs={{0,1},{1,0},{2,3},{3,2},{4,5},{5,4},{6,7},{7,6},{8,9},{9,8},{10,11... | collective-permute-start | bytes 371720 | tf_op jit(solution)/shard_map/ppermute | solution.py:350
  160.3 4.8 %collective-permute-start.14 = (bf16[11,1408]{1,0:T(8,128)(2,1)S(1)}, bf16[11,1408]{1,0:T(8,128)(2,1)S(1)}, u32[]{:S(2)}, u32[]{:S(2)}) collective-permute-start(bf16[11,1408]{1,0:T(8,128)(2,1)S(1)} %get-tuple-element.35), channel_id=1, source_target_pairs={{0,2},{2,4},{4,6},{6,0},{1,3},{3,5},{5,7},{7,1},{8,10},{10,12},{12... | collective-permute-start | bytes 92936 | tf_op jit(solution)/shard_map/ppermute | solution.py:341
  161.5 4.6 %collective-permute-start.15 = (bf16[11,1408]{1,0:T(8,128)(2,1)S(1)}, bf16[11,1408]{1,0:T(8,128)(2,1)S(1)}, u32[]{:S(2)}, u32[]{:S(2)}) collective-permute-start(bf16[11,1408]{1,0:T(8,128)(2,1)S(1)} %get-tuple-element.36), channel_id=1, source_target_pairs={{0,4},{2,6},{4,0},{6,2},{1,5},{3,7},{5,1},{7,3},{8,12},{10,14},{12... | collective-permute-start | bytes 92936 | tf_op jit(solution)/shard_map/ppermute | solution.py:341
  163.9 3.2 %collective-permute-start.16 = (bf16[11,1408]{1,0:T(8,128)(2,1)S(1)}, bf16[11,1408]{1,0:T(8,128)(2,1)S(1)}, u32[]{:S(2)}, u32[]{:S(2)}) collective-permute-start(bf16[11,1408]{1,0:T(8,128)(2,1)S(1)} %get-tuple-element.37), channel_id=1, source_target_pairs={{0,6},{2,0},{4,2},{6,4},{1,7},{3,1},{5,3},{7,5},{8,14},{10,8},{12,... | collective-permute-start | bytes 92936 | tf_op jit(solution)/shard_map/ppermute | solution.py:341

commit v7 on v6

--- a/solution.py
+++ b/solution.py
@@ -11,7 +11,8 @@
 HALF = 64
 QUARTER = 22
 PADDED = 24
-PIECES = 8
+COLUMNS = 8 * PADDED
+PIECES = 11
 BLOCK = 256
 SOFTMAX_SCALE = HEAD_DIM ** (-0.5)
 EXP2_SCALE = SOFTMAX_SCALE * 1.4426950408889634
@@ -112,15 +113,18 @@
     return pltpu.make_async_copy(buffer.at[pair], hbm.at[(*lead, pair_lanes(pair))], sem.at[pair])
 
 
-def forward_kernel(x_ref, att_hbm, e_hbm, row_ref, o_ref, att_ref, e_ref, sem, e_sem):
+def forward_kernel(x_ref, att_hbm, e_hbm, row_hbm, o_ref, att_ref, e_ref, row_ref, sem, e_sem, row_sem):
+    row_copy = pltpu.make_async_copy(row_ref, row_hbm, row_sem)
+
     def kept(frame):
         return pltpu.make_async_copy(e_ref.at[frame], e_hbm.at[frame], e_sem.at[frame])
 
     def step(pair, carry):
         qs, ks, vs, gs = (frame_pair(x_ref, n, pair) for n in range(4))
+        raw = [jnp.dot(ks[f].T, qs[f], preferred_element_type=F32) for f in range(2)]
         for f in range(2):
             frame = 2 * pair + f
-            scores = jnp.dot(ks[f].T, qs[f], preferred_element_type=F32)
+            scores = raw[f]
             row_max = jnp.max(scores, axis=0, keepdims=True)
             raised = jnp.exp2(scores * EXP2_SCALE - row_max * EXP2_SCALE)
             inverse = 1.0 / jnp.sum(raised, axis=0, keepdims=True)
@@ -131,6 +135,8 @@
             o_ref[f] = attended
             row_ref[frame, 0:1] = inverse
             row_ref[frame, 1:2] = jnp.sum(gs[f].astype(F32) * attended, axis=0, keepdims=True) * inverse
+        if pair == 1:
+            row_copy.start()
         for s in range(8):
             a, b = o_ref[0, :, 128 * s : 128 * (s + 1)], o_ref[1, :, 128 * s : 128 * (s + 1)]
             low = low_lanes(a.shape)
@@ -148,6 +154,7 @@
         stored(att_ref, att_hbm, sem, pair).wait()
     for frame in range(4):
         kept(frame).wait()
+    row_copy.wait()
 
 
 VM, SM = pl.BlockSpec(memory_space=pltpu.VMEM), pl.BlockSpec(memory_space=pltpu.SMEM)
@@ -158,18 +165,20 @@
     return pl.pallas_call(
         forward_kernel,
         in_specs=[VM],
-        out_specs=[HB, HB, VM],
+        out_specs=[HB, HB, HB],
         out_shape=[
             pltpu.HBM((32, 2, PADDED, 256), BF16),
             pltpu.HBM((4, 1024, 1024), BF16),
-            jax.ShapeDtypeStruct((4, 8, 1024), F32),
+            pltpu.HBM((4, 8, 1024), F32),
         ],
         scratch_shapes=[
             pltpu.VMEM((2, HEAD_DIM, 1024), F32),
             pltpu.VMEM((2, 32, 2, PADDED, 128), BF16),
             pltpu.VMEM((4, 1024, 1024), BF16),
+            pltpu.VMEM((4, 8, 1024), F32),
             pltpu.SemaphoreType.DMA((2,)),
             pltpu.SemaphoreType.DMA((4,)),
+            pltpu.SemaphoreType.DMA,
         ],
         cost_estimate=pl.CostEstimate(flops=4 * 4 * 1024 * 1024 * 256, bytes_accessed=12_000_000, transcendentals=1 << 22),
         compiler_params=pltpu.CompilerParams(vmem_limit_bytes=40 << 20),
@@ -219,21 +228,25 @@
     )(x, raised, per_row)
 
 
+def in_hbm(array):
+    return pltpu.with_memory_space_constraint(array, pltpu.HBM)
+
+
 def weight_kernel(place_ref, *refs):
-    grads, att_ref, outs, (a_ref, t_ref) = refs[:8], refs[8], refs[9:13], refs[13:]
+    grads, att_ref, outs, (g_ref, t_ref, sem) = refs[:8], refs[8], refs[9:13], refs[13:]
     core, z, y = place_ref[0], place_ref[1], place_ref[2]
+    loads = [pltpu.make_async_copy(grads[n], g_ref.at[n], sem.at[n]) for n in range(8)]
+    for copy in loads:
+        copy.start()
     total = None
-    for r in range(4):
-        source = lax.rem(z + 4 - r, 4)
-        for side in range(2):
-            spot = lax.rem(core + side, 2)
-            for i in range(8):
-                a_ref[QUARTER * i : QUARTER * (i + 1)] = att_ref[source * 8 + i, spot].astype(F32)[:QUARTER]
-            grad = grads[4 * side + r][...]
-            term = jnp.dot(
-                a_ref[...].astype(BF16), grad.reshape(-1, grad.shape[-1]), preferred_element_type=F32
-            )
-            total = term if total is None else total + term
+    for n in range(8):
+        if n % 2 == 0:
+            loads[n].wait()
+            loads[n + 1].wait()
+        source, spot = lax.rem(z + 4 - n % 4, 4), lax.rem(core + n // 4, 2)
+        block = att_ref[pl.ds(source * 8, 8), spot].reshape(COLUMNS, 256)
+        term = jnp.dot(block, g_ref[n].reshape(256, g_ref.shape[-1]), preferred_element_type=F32)
+        total = term if total is None else total + term
     t_ref[...] = total.T
     for s, out in enumerate(outs):
         to = lax.rem(y + s, 4)
@@ -241,22 +254,26 @@
             start = lax.rem(to, 2) * 704 + depth * 176 + (to // 2) * 88
             block = t_ref[pl.ds(pl.multiple_of(start, 8), 88), :]
             for x in range(4):
-                out[x, depth] = block[QUARTER * x : QUARTER * (x + 1)].astype(out.dtype)
+                rows = block[QUARTER * x : QUARTER * (x + 1)].astype(out.dtype)
+                out[depth, x // 2, :, COLUMNS * (x % 2) : COLUMNS * (x % 2 + 1)] = rows
 
 
 def weight_terms(place, grads, att):
-    shape = (4, 4, QUARTER, 8 * QUARTER)
-    features = grads[0].shape[-1]
+    shape = (4, 2, QUARTER, 2 * COLUMNS)
     return pl.pallas_call(
         weight_kernel,
-        in_specs=[SM] + [VM] * 9,
+        in_specs=[SM] + [HB] * 8 + [VM],
         out_specs=[VM] * 4,
         out_shape=[jax.ShapeDtypeStruct(shape, F32)] + [jax.ShapeDtypeStruct(shape, BF16)] * 3,
-        scratch_shapes=[pltpu.VMEM((8 * QUARTER, 256), F32), pltpu.VMEM((features, 8 * QUARTER), F32)],
+        scratch_shapes=[
+            pltpu.VMEM((8, *grads[0].shape), BF16),
+            pltpu.VMEM((grads[0].shape[-1], COLUMNS), F32),
+            pltpu.SemaphoreType.DMA((8,)),
+        ],
         cost_estimate=pl.CostEstimate(flops=2 * 2048 * 1408 * 176, bytes_accessed=8_000_000, transcendentals=0),
         compiler_params=pltpu.CompilerParams(vmem_limit_bytes=24 << 20),
         name="weight_terms",
-    )(place, *grads, att)
+    )(place, *map(in_hbm, grads), att)
 
 
 def small(kernel, place, operands, shapes, scratch=()):
@@ -275,7 +292,8 @@
     parts, outs, total = refs[:4], refs[4:8], refs[8]
     for x in range(4):
         for z in range(4):
-            total[z, x] = sum(part[x, z].astype(F32) for part in parts)
+            columns = slice(COLUMNS * (x % 2), COLUMNS * (x % 2 + 1))
+            total[z, x] = sum(part[z, x // 2, :, columns].astype(F32) for part in parts)
     for s, out in enumerate(outs):
         out[...] = total[lax.rem(place_ref[1] + s, 4)]
 
@@ -302,7 +320,7 @@
         for z in range(4):
             at = head * HEAD_DIM + z * QUARTER
             for x in range(4):
-                joined[x, :, at : at + QUARTER] = scratch[head // 8, z, x][:, QUARTER * i : QUARTER * (i + 1)]
+                joined[x, :, at : at + QUARTER] = scratch[head // 8, z, x][:, PADDED * i : PADDED * i + QUARTER]
     for s, out in enumerate(outs):
         out[...] = joined[lax.rem(place + s, 4)].astype(out.dtype)
 
@@ -362,7 +380,7 @@
     own, *sent = weight_terms(place, gathered, att)
     parts = [own] + [along_y(part, s) for s, part in enumerate(sent, 1)]
     home = exchange(grads, PATCH)
-    columns, array = 8 * QUARTER, jax.ShapeDtypeStruct
+    columns, array = COLUMNS, jax.ShapeDtypeStruct
     own, *sent = small(
         sums_kernel, place, parts, [array((4, QUARTER, columns), F32)] * 4, [pltpu.VMEM((4, 4, QUARTER, columns), F32)]
     )

time: 170 us -> 165 us (0.971)
  waiting for transfers between devices: 47 us -> 44.9 us
  local copies, waits for them, and re-layouts: 1.76 us -> 0.01 us
    ppermute x3, waiting for transfers between devices: 7.78 us -> 5.67 us  [along_y(): lax.ppermute(array, ('y_lo', 'y_hi'), [(place(y), place((y + step) % 4))...]
    unnamed x6 -> x2, local copies, waits for them, and re-layouts: 1.76 us -> 0.01 us
where the time goes in v7:
time: 165 us
  blocking collectives  45.2 us (27%)
  waiting for transfers between devices  44.9 us (27%)
  Pallas kernels  37.1 us (22%)
  starting transfers between devices  36.6 us (22%)
    all_to_all x1, blocking collectives, exchange(): return lax.all_to_all(array, axes, split_axis=0, concat_axis=0, tiled=True)  45.2 us
    ppermute x9, waiting for transfers between devices, along(): return lax.ppermute(array, axis, [(i, (i + step) % 4) for i in range(4)])  34 us
    pallas_call x1, Pallas kernels, backward(): pl.pallas_call(backward_kernel, grid=(2,), in_specs=[pl.BlockSpec((HEADS,...  13.6 us
    ppermute x9, starting transfers between devices, along(): return lax.ppermute(array, axis, [(i, (i + step) % 4) for i in range(4)])  13.1 us
    all_to_all x2, starting transfers between devices, exchange(): return lax.all_to_all(array, axes, split_axis=0, concat_axis=0, tiled=True)  13 us
    pallas_call x1, Pallas kernels, forward(): pl.pallas_call(forward_kernel, in_specs=[VM], out_specs=[HB, HB, HB], out...  9.56 us
    ppermute x3, waiting for transfers between devices, along_y(): lax.ppermute(array, ('y_lo', 'y_hi'), [(place(y), place((y + step) % 4))...  5.67 us
    ppermute x5, starting transfers between devices, other_core(): return lax.ppermute(array, 'core', [(0, 1), (1, 0)])  5.5 us
  transfers between devices with their start and end apart: 19, of which 12 were waited for; matrix products, arithmetic and copies ran while one was open for 0% of the time, Pallas kernels for 12%

profile of v7, /device:TPU:1, one launch (start us, length us, event | category | flops | bytes accessed | tf_op | source)
XLA Modules:
  0.0 164.6 jit_solution(4239868904844913646)
XLA Ops:
  0.6 5.4 %pack_by_head.1 = bf16[16,4,88,256]{3,2,1,0:T(8,128)(2,1)} custom-call(bf16[4,64,1408]{2,1,0:T(8,128)(2,1)} %refs_0_.2, bf16[4,64,1408]{2,1,0:T(8,128)(2,1)} %refs_1_.1, bf16[4,64,1408]{2,1,0:T(8,128)(2,1)} %refs_2_.1, bf16[4,64,1408]{2,1,0:T(8,128)(2,1)} %refs_0_.3, bf16[1408,1408]{1,0:T(8,128)(2,1)} %refs_4_.1), custom_call_target="tpu_custom_call" | custom-call | flops 1015021568 | bytes 10000000 | tf_op jit(solution)/shard_map/pack_by_head/pallas_call | solution.py:92
  6.1 45.2 %all_to_all.15.x_ref = bf16[16,4,88,256]{3,2,1,0:T(8,128)(2,1)S(1)} all-to-all(bf16[16,4,88,256]{3,2,1,0:T(8,128)(2,1)} %pack_by_head.1), channel_id=1, replica_groups=mesh['y_lo'=2,'z'=4,'y_hi'=2,'x'=4,'core'=2] {'y_hi','x','core'}, dimensions={0} | all-to-all | bytes 5767168 | tf_op jit(solution)/shard_map/all_to_all | solution.py:355
  51.3 0.0 copy-start
  51.3 9.6 %spatial_forward.1 = (bf16[32,2,24,256]{3,2,1,0:T(8,128)(2,1)}, bf16[4,1024,1024]{2,1,0:T(8,128)(2,1)}, f32[4,8,1024]{2,1,0:T(8,128)}) custom-call(bf16[16,4,88,256]{3,2,1,0:T(8,128)(2,1)S(1)} %all_to_all.15.x_ref), custom_call_target="tpu_custom_call" | custom-call | flops 4294967296 | bytes 12000000 | tf_op jit(solution)/shard_map/spatial_forward/pallas_call | solution.py:165
  60.9 0.0 copy-done
  60.9 6.7 %all-to-all-start.2 = ((bf16[32,2,24,256]{3,2,1,0:T(8,128)(2,1)}), bf16[32,2,24,256]{3,2,1,0:T(8,128)(2,1)S(1)}, u32[]{:S(2)}, u32[]{:S(2)}) async-start(bf16[32,2,24,256]{3,2,1,0:T(8,128)(2,1)} %get-tuple-element.23), calls=%async_computation.2 | async-start | bytes 1572864 | tf_op jit(solution)/shard_map/all_to_all | solution.py:355
  67.6 13.6 %spatial_backward.1 = bf16[16,3,88,256]{3,2,1,0:T(8,128)(2,1)} custom-call(bf16[16,4,88,256]{3,2,1,0:T(8,128)(2,1)} %copy-done, bf16[4,1024,1024]{2,1,0:T(8,128)(2,1)} %get-tuple-element.21.e_ref, f32[4,8,1024]{2,1,0:T(8,128)} %get-tuple-element.22.row_ref), custom_call_target="tpu_custom_call" | custom-call | flops 8589934592 | bytes 14000000 | tf_op jit(solution)/shard_map/spatial_backward/pallas_call | solution.py:214
  81.2 0.9 all-to-all-done.2.refs_8_
  82.2 6.3 %all-to-all-start.1 = ((bf16[16,3,88,256]{3,2,1,0:T(8,128)(2,1)}), bf16[16,3,88,256]{3,2,1,0:T(8,128)(2,1)S(1)}, u32[]{:S(2)}, u32[]{:S(2)}) async-start(bf16[16,3,88,256]{3,2,1,0:T(8,128)(2,1)} %spatial_backward.1), calls=%async_computation.1 | async-start | bytes 4325376 | tf_op jit(solution)/shard_map/all_to_all | solution.py:355
  88.5 1.2 collective-permute-start
  89.6 2.5 %collective-permute-start.1 = (bf16[4,64,1408]{2,1,0:T(8,128)(2,1)}, bf16[4,64,1408]{2,1,0:T(8,128)(2,1)}, u32[]{:S(2)}, u32[]{:S(2)}) collective-permute-start(bf16[4,64,1408]{2,1,0:T(8,128)(2,1)} %refs_0_.3), channel_id=1, source_target_pairs={{0,32},{16,48},{32,0},{48,16},{1,33},{17,49},{33,1},{49,17},{2,34}... | collective-permute-start | bytes 2162696 | tf_op jit(solution)/shard_map/ppermute | solution.py:359
  92.1 1.1 collective-permute-start.2
  93.2 1.0 collective-permute-start.3
  94.3 13.3 %collective-permute-done.refs_1_ = bf16[4,64,1408]{2,1,0:T(8,128)(2,1)} collective-permute-done((bf16[4,64,1408]{2,1,0:T(8,128)(2,1)}, bf16[4,64,1408]{2,1,0:T(8,128)(2,1)}, u32[]{:S(2)}, u32[]{:S(2)}) %collective-permute-start) | collective-permute-done | bytes 720928 | tf_op jit(solution)/shard_map/ppermute | solution.py:359
  107.5 1.0 collective-permute-start.4
  108.5 15.4 %collective-permute-done.1.refs_2_ = bf16[4,64,1408]{2,1,0:T(8,128)(2,1)} collective-permute-done((bf16[4,64,1408]{2,1,0:T(8,128)(2,1)}, bf16[4,64,1408]{2,1,0:T(8,128)(2,1)}, u32[]{:S(2)}, u32[]{:S(2)}) %collective-permute-start.1) | collective-permute-done | bytes 720928 | tf_op jit(solution)/shard_map/ppermute | solution.py:359
  123.9 1.0 collective-permute-start.5
  125.0 0.0 collective-permute-done.2.refs_3_
  125.0 0.0 collective-permute-start.6
  125.0 0.1 pad_add_fusion.place_ref
  125.1 0.0 collective-permute-done.3.refs_4_
  125.1 0.0 collective-permute-done.4.refs_5_
  125.1 2.1 %collective-permute-done.5.refs_6_ = bf16[4,64,1408]{2,1,0:T(8,128)(2,1)} collective-permute-done((bf16[4,64,1408]{2,1,0:T(8,128)(2,1)}, bf16[4,64,1408]{2,1,0:T(8,128)(2,1)}, u32[]{:S(2)}, u32[]{:S(2)}) %collective-permute-start.5) | collective-permute-done | bytes 720928 | tf_op jit(solution)/shard_map/ppermute | solution.py:368
  127.1 1.0 collective-permute-done.6.refs_7_
  128.2 4.3 %weight_terms.1 = (f32[4,2,22,384]{3,2,1,0:T(8,128)S(1)}, bf16[4,2,22,384]{3,2,1,0:T(8,128)(2,1)S(1)}, bf16[4,2,22,384]{3,2,1,0:T(8,128)(2,1)S(1)}, bf16[4,2,22,384]{3,2,1,0:T(8,128)(2,1)S(1)}) custom-call(s32[4]{0:T(128)S(1)} %pad_add_fusion.place_ref, bf16[4,64,1408]{2,1,0:T(8,128)(2,1)} %refs_0_.3, bf16[4,64,1408]{2,1,0:T(8,128)(2,1)} %collective-permute-done.refs_1_, ...), custom_call_target="tpu_custom_call" | custom-call | flops 1015021568 | bytes 8000000 | tf_op jit(solution)/shard_map/weight_terms/pallas_call | solution.py:263
  132.5 0.5 collective-permute-start.7
  133.0 3.5 %collective-permute-start.8 = (bf16[4,2,22,384]{3,2,1,0:T(8,128)(2,1)S(1)}, bf16[4,2,22,384]{3,2,1,0:T(8,128)(2,1)S(1)}, u32[]{:S(2)}, u32[]{:S(2)}) collective-permute-start(bf16[4,2,22,384]{3,2,1,0:T(8,128)(2,1)S(1)} %get-tuple-element.26), channel_id=1, source_target_pairs={{0,8},{64,72},{8,0},{72,64},{1,9},{65,73},{9,1},{73,65},{2,10},{66... | collective-permute-start | bytes 405512 | tf_op jit(solution)/shard_map/ppermute | solution.py:364
  136.4 1.1 collective-permute-start.9
  137.5 1.3 collective-permute-done.7.refs_1_
  138.8 4.3 %collective-permute-done.8.refs_2_ = bf16[4,2,22,384]{3,2,1,0:T(8,128)(2,1)S(1)} collective-permute-done((bf16[4,2,22,384]{3,2,1,0:T(8,128)(2,1)S(1)}, bf16[4,2,22,384]{3,2,1,0:T(8,128)(2,1)S(1)}, u32[]{:S(2)}, u32[]{:S(2)}) %collective-permute-start.8) | collective-permute-done | bytes 135200 | tf_op jit(solution)/shard_map/ppermute | solution.py:364
  143.2 0.0 collective-permute-done.9.refs_3_
  143.2 0.7 shard_map.84
  143.9 0.1 collective-permute-start.10
  144.0 2.1 %collective-permute-start.11 = (f32[4,22,192]{2,1,0:T(8,128)S(1)}, f32[4,22,192]{2,1,0:T(8,128)S(1)}, u32[]{:S(2)}, u32[]{:S(2)}) collective-permute-start(f32[4,22,192]{2,1,0:T(8,128)S(1)} %get-tuple-element.30), channel_id=1, source_target_pairs={{0,32},{16,48},{32,0},{48,16},{1,33},{17,49},{33,1},{49,17},{2,34}... | collective-permute-start | bytes 202760 | tf_op jit(solution)/shard_map/ppermute | solution.py:359
  146.1 1.3 collective-permute-start.12
  147.3 2.9 %collective-permute-done.10.refs_1_ = f32[4,22,192]{2,1,0:T(8,128)S(1)} collective-permute-done((f32[4,22,192]{2,1,0:T(8,128)S(1)}, f32[4,22,192]{2,1,0:T(8,128)S(1)}, u32[]{:S(2)}, u32[]{:S(2)}) %collective-permute-start.10) | collective-permute-done | bytes 67616 | tf_op jit(solution)/shard_map/ppermute | solution.py:359
  150.2 0.0 collective-permute-done.11.refs_2_
  150.2 0.4 collective-permute-done.12.refs_3_
  150.7 0.6 shard_map.85
  151.3 2.4 %collective-permute-start.13 = (f32[4,4,11,192]{3,2,1,0:T(8,128)S(1)}, f32[4,4,11,192]{3,2,1,0:T(8,128)S(1)}, u32[]{:S(2)}, u32[]{:S(2)}) collective-permute-start(f32[4,4,11,192]{3,2,1,0:T(8,128)S(1)} %get-tuple-element.33), channel_id=1, source_target_pairs={{0,1},{1,0},{2,3},{3,2},{4,5},{5,4},{6,7},{7,6},{8,9},{9,8},{10,11... | collective-permute-start | bytes 405512 | tf_op jit(solution)/shard_map/ppermute | solution.py:368
  153.7 1.2 collective-permute-done.13.theirs
  154.9 1.2 shard_map.86
  156.1 1.3 collective-permute-start.14
  157.4 2.4 %collective-permute-start.15 = (bf16[11,1408]{1,0:T(8,128)(2,1)S(1)}, bf16[11,1408]{1,0:T(8,128)(2,1)S(1)}, u32[]{:S(2)}, u32[]{:S(2)}) collective-permute-start(bf16[11,1408]{1,0:T(8,128)(2,1)S(1)} %get-tuple-element.36), channel_id=1, source_target_pairs={{0,4},{2,6},{4,0},{6,2},{1,5},{3,7},{5,1},{7,3},{8,12},{10,14},{12... | collective-permute-start | bytes 92936 | tf_op jit(solution)/shard_map/ppermute | solution.py:359
  159.8 1.2 collective-permute-start.16
  161.0 0.0 collective-permute-done.14.refs_1_
  161.0 1.0 collective-permute-done.15.refs_2_
  162.0 0.9 collective-permute-done.16.refs_3_
  163.0 0.0 all-to-all-done.1.x_ref
  163.0 1.6 unpack_by_token.1
Async XLA Ops:
  51.3 9.6 %copy-start = (bf16[16,4,88,256]{3,2,1,0:T(8,128)(2,1)}, bf16[16,4,88,256]{3,2,1,0:T(8,128)(2,1)S(1)}, u32[]{:S(2)}) copy-start(bf16[16,4,88,256]{3,2,1,0:T(8,128)(2,1)S(1)} %all_to_all.15.x_ref) | copy-start | bytes 8650756
  60.9 21.3 %all-to-all-start.2 = ((bf16[32,2,24,256]{3,2,1,0:T(8,128)(2,1)}), bf16[32,2,24,256]{3,2,1,0:T(8,128)(2,1)S(1)}, u32[]{:S(2)}, u32[]{:S(2)}) async-start(bf16[32,2,24,256]{3,2,1,0:T(8,128)(2,1)} %get-tuple-element.23), calls=%async_computation.2 | async-start | bytes 1572864 | tf_op jit(solution)/shard_map/all_to_all | solution.py:355
  82.2 80.8 %all-to-all-start.1 = ((bf16[16,3,88,256]{3,2,1,0:T(8,128)(2,1)}), bf16[16,3,88,256]{3,2,1,0:T(8,128)(2,1)S(1)}, u32[]{:S(2)}, u32[]{:S(2)}) async-start(bf16[16,3,88,256]{3,2,1,0:T(8,128)(2,1)} %spatial_backward.1), calls=%async_computation.1 | async-start | bytes 4325376 | tf_op jit(solution)/shard_map/all_to_all | solution.py:355
  88.5 19.1 %collective-permute-start = (bf16[4,64,1408]{2,1,0:T(8,128)(2,1)}, bf16[4,64,1408]{2,1,0:T(8,128)(2,1)}, u32[]{:S(2)}, u32[]{:S(2)}) collective-permute-start(bf16[4,64,1408]{2,1,0:T(8,128)(2,1)} %refs_0_.3), channel_id=1, source_target_pairs={{0,16},{16,32},{32,48},{48,0},{1,17},{17,33},{33,49},{49,1},{2,18}... | collective-permute-start | bytes 2162696 | tf_op jit(solution)/shard_map/ppermute | solution.py:359
  89.6 34.3 %collective-permute-start.1 = (bf16[4,64,1408]{2,1,0:T(8,128)(2,1)}, bf16[4,64,1408]{2,1,0:T(8,128)(2,1)}, u32[]{:S(2)}, u32[]{:S(2)}) collective-permute-start(bf16[4,64,1408]{2,1,0:T(8,128)(2,1)} %refs_0_.3), channel_id=1, source_target_pairs={{0,32},{16,48},{32,0},{48,16},{1,33},{17,49},{33,1},{49,17},{2,34}... | collective-permute-start | bytes 2162696 | tf_op jit(solution)/shard_map/ppermute | solution.py:359
  92.1 32.9 %collective-permute-start.2 = (bf16[4,64,1408]{2,1,0:T(8,128)(2,1)}, bf16[4,64,1408]{2,1,0:T(8,128)(2,1)}, u32[]{:S(2)}, u32[]{:S(2)}) collective-permute-start(bf16[4,64,1408]{2,1,0:T(8,128)(2,1)} %refs_0_.3), channel_id=1, source_target_pairs={{0,48},{16,0},{32,16},{48,32},{1,49},{17,1},{33,17},{49,33},{2,50}... | collective-permute-start | bytes 2162696 | tf_op jit(solution)/shard_map/ppermute | solution.py:359
  93.2 31.8 %collective-permute-start.3 = (bf16[4,64,1408]{2,1,0:T(8,128)(2,1)}, bf16[4,64,1408]{2,1,0:T(8,128)(2,1)}, u32[]{:S(2)}, u32[]{:S(2)}) collective-permute-start(bf16[4,64,1408]{2,1,0:T(8,128)(2,1)} %refs_0_.3), channel_id=1, source_target_pairs={{0,1},{1,0},{2,3},{3,2},{4,5},{5,4},{6,7},{7,6},{8,9},{9,8},{10,11... | collective-permute-start | bytes 2162696 | tf_op jit(solution)/shard_map/ppermute | solution.py:368
  107.5 17.5 %collective-permute-start.4 = (bf16[4,64,1408]{2,1,0:T(8,128)(2,1)}, bf16[4,64,1408]{2,1,0:T(8,128)(2,1)}, u32[]{:S(2)}, u32[]{:S(2)}) collective-permute-start(bf16[4,64,1408]{2,1,0:T(8,128)(2,1)} %collective-permute-done.refs_1_), channel_id=1, source_target_pairs={{0,1},{1,0},{2,3},{3,2},{4,5},{5,4},{6,7},{7,6},{8,9},{9,8},{10,11... | collective-permute-start | bytes 2162696 | tf_op jit(solution)/shard_map/ppermute | solution.py:368
  123.9 3.2 %collective-permute-start.5 = (bf16[4,64,1408]{2,1,0:T(8,128)(2,1)}, bf16[4,64,1408]{2,1,0:T(8,128)(2,1)}, u32[]{:S(2)}, u32[]{:S(2)}) collective-permute-start(bf16[4,64,1408]{2,1,0:T(8,128)(2,1)} %collective-permute-done.1.refs_2_), channel_id=1, source_target_pairs={{0,1},{1,0},{2,3},{3,2},{4,5},{5,4},{6,7},{7,6},{8,9},{9,8},{10,11... | collective-permute-start | bytes 2162696 | tf_op jit(solution)/shard_map/ppermute | solution.py:368
  125.0 3.2 %collective-permute-start.6 = (bf16[4,64,1408]{2,1,0:T(8,128)(2,1)}, bf16[4,64,1408]{2,1,0:T(8,128)(2,1)}, u32[]{:S(2)}, u32[]{:S(2)}) collective-permute-start(bf16[4,64,1408]{2,1,0:T(8,128)(2,1)} %collective-permute-done.2.refs_3_), channel_id=1, source_target_pairs={{0,1},{1,0},{2,3},{3,2},{4,5},{5,4},{6,7},{7,6},{8,9},{9,8},{10,11... | collective-permute-start | bytes 2162696 | tf_op jit(solution)/shard_map/ppermute | solution.py:368
  132.5 6.3 %collective-permute-start.7 = (bf16[4,2,22,384]{3,2,1,0:T(8,128)(2,1)S(1)}, bf16[4,2,22,384]{3,2,1,0:T(8,128)(2,1)S(1)}, u32[]{:S(2)}, u32[]{:S(2)}) collective-permute-start(bf16[4,2,22,384]{3,2,1,0:T(8,128)(2,1)S(1)} %get-tuple-element.25), channel_id=1, source_target_pairs={{0,64},{64,8},{8,72},{72,0},{1,65},{65,9},{9,73},{73,1},{2,66},{66... | collective-permute-start | bytes 405512 | tf_op jit(solution)/shard_map/ppermute | solution.py:364
  133.0 10.2 %collective-permute-start.8 = (bf16[4,2,22,384]{3,2,1,0:T(8,128)(2,1)S(1)}, bf16[4,2,22,384]{3,2,1,0:T(8,128)(2,1)S(1)}, u32[]{:S(2)}, u32[]{:S(2)}) collective-permute-start(bf16[4,2,22,384]{3,2,1,0:T(8,128)(2,1)S(1)} %get-tuple-element.26), channel_id=1, source_target_pairs={{0,8},{64,72},{8,0},{72,64},{1,9},{65,73},{9,1},{73,65},{2,10},{66... | collective-permute-start | bytes 405512 | tf_op jit(solution)/shard_map/ppermute | solution.py:364
  136.4 6.7 %collective-permute-start.9 = (bf16[4,2,22,384]{3,2,1,0:T(8,128)(2,1)S(1)}, bf16[4,2,22,384]{3,2,1,0:T(8,128)(2,1)S(1)}, u32[]{:S(2)}, u32[]{:S(2)}) collective-permute-start(bf16[4,2,22,384]{3,2,1,0:T(8,128)(2,1)S(1)} %get-tuple-element.27), channel_id=1, source_target_pairs={{0,72},{64,0},{8,64},{72,8},{1,73},{65,1},{9,65},{73,9},{2,74},{66... | collective-permute-start | bytes 405512 | tf_op jit(solution)/shard_map/ppermute | solution.py:364
  143.9 6.4 %collective-permute-start.10 = (f32[4,22,192]{2,1,0:T(8,128)S(1)}, f32[4,22,192]{2,1,0:T(8,128)S(1)}, u32[]{:S(2)}, u32[]{:S(2)}) collective-permute-start(f32[4,22,192]{2,1,0:T(8,128)S(1)} %get-tuple-element.29), channel_id=1, source_target_pairs={{0,16},{16,32},{32,48},{48,0},{1,17},{17,33},{33,49},{49,1},{2,18}... | collective-permute-start | bytes 202760 | tf_op jit(solution)/shard_map/ppermute | solution.py:359
  144.0 6.3 %collective-permute-start.11 = (f32[4,22,192]{2,1,0:T(8,128)S(1)}, f32[4,22,192]{2,1,0:T(8,128)S(1)}, u32[]{:S(2)}, u32[]{:S(2)}) collective-permute-start(f32[4,22,192]{2,1,0:T(8,128)S(1)} %get-tuple-element.30), channel_id=1, source_target_pairs={{0,32},{16,48},{32,0},{48,16},{1,33},{17,49},{33,1},{49,17},{2,34}... | collective-permute-start | bytes 202760 | tf_op jit(solution)/shard_map/ppermute | solution.py:359
  146.1 4.6 %collective-permute-start.12 = (f32[4,22,192]{2,1,0:T(8,128)S(1)}, f32[4,22,192]{2,1,0:T(8,128)S(1)}, u32[]{:S(2)}, u32[]{:S(2)}) collective-permute-start(f32[4,22,192]{2,1,0:T(8,128)S(1)} %get-tuple-element.31), channel_id=1, source_target_pairs={{0,48},{16,0},{32,16},{48,32},{1,49},{17,1},{33,17},{49,33},{2,50}... | collective-permute-start | bytes 202760 | tf_op jit(solution)/shard_map/ppermute | solution.py:359
  151.3 3.6 %collective-permute-start.13 = (f32[4,4,11,192]{3,2,1,0:T(8,128)S(1)}, f32[4,4,11,192]{3,2,1,0:T(8,128)S(1)}, u32[]{:S(2)}, u32[]{:S(2)}) collective-permute-start(f32[4,4,11,192]{3,2,1,0:T(8,128)S(1)} %get-tuple-element.33), channel_id=1, source_target_pairs={{0,1},{1,0},{2,3},{3,2},{4,5},{5,4},{6,7},{7,6},{8,9},{9,8},{10,11... | collective-permute-start | bytes 405512 | tf_op jit(solution)/shard_map/ppermute | solution.py:368
  156.1 4.8 %collective-permute-start.14 = (bf16[11,1408]{1,0:T(8,128)(2,1)S(1)}, bf16[11,1408]{1,0:T(8,128)(2,1)S(1)}, u32[]{:S(2)}, u32[]{:S(2)}) collective-permute-start(bf16[11,1408]{1,0:T(8,128)(2,1)S(1)} %get-tuple-element.35), channel_id=1, source_target_pairs={{0,2},{2,4},{4,6},{6,0},{1,3},{3,5},{5,7},{7,1},{8,10},{10,12},{12... | collective-permute-start | bytes 92936 | tf_op jit(solution)/shard_map/ppermute | solution.py:359
  157.4 4.6 %collective-permute-start.15 = (bf16[11,1408]{1,0:T(8,128)(2,1)S(1)}, bf16[11,1408]{1,0:T(8,128)(2,1)S(1)}, u32[]{:S(2)}, u32[]{:S(2)}) collective-permute-start(bf16[11,1408]{1,0:T(8,128)(2,1)S(1)} %get-tuple-element.36), channel_id=1, source_target_pairs={{0,4},{2,6},{4,0},{6,2},{1,5},{3,7},{5,1},{7,3},{8,12},{10,14},{12... | collective-permute-start | bytes 92936 | tf_op jit(solution)/shard_map/ppermute | solution.py:359
  159.8 3.2 %collective-permute-start.16 = (bf16[11,1408]{1,0:T(8,128)(2,1)S(1)}, bf16[11,1408]{1,0:T(8,128)(2,1)S(1)}, u32[]{:S(2)}, u32[]{:S(2)}) collective-permute-start(bf16[11,1408]{1,0:T(8,128)(2,1)S(1)} %get-tuple-element.37), channel_id=1, source_target_pairs={{0,6},{2,0},{4,2},{6,4},{1,7},{3,1},{5,3},{7,5},{8,14},{10,8},{12,... | collective-permute-start | bytes 92936 | tf_op jit(solution)/shard_map/ppermute | solution.py:359
